TPU v7x, 256 devices: a whole 4x4x8 slice. The times are simulated.
256 devices in a mesh: dp: 16 (over x, y), seq: 16 (over z, core).
Axes of the slice: x: 4, y: 4, z: 8, core: 2. Of those that a mesh axis runs over, the one named last changes fastest.
Arguments:
- tokens: bfloat16 [16, 16, 32, 4, 512], P('dp', 'seq'), may hold values from -6 to 6
- conv_first: bfloat16 [27, 512, 128], replicated, may hold values from -0.0546875 to 0.0546875
- bias_first: float32 [128], replicated, may hold values from -3 to 3
- conv_second: bfloat16 [27, 128, 384], replicated, may hold values from -0.109375 to 0.109375
- bias_second: float32 [384], replicated, may hold values from -3 to 3
- pixels: bfloat16 [16, 16, 32, 4, 1536], P('dp', None, 'seq'), may hold values from 0 to 1
- mask_index: int32 [16, 115], P('dp'), may hold values from 0 to 127, as said below
Outputs:
- grad_first: float32 [27, 512, 128], P(None, 'seq', 'dp')
- grad_second: float32 [27, 128, 384], P(None, 'seq', 'dp')
Inputs may be any that keep to these rules, and one draw needn't show every extreme that they name: `mask_index`: each row holds 115 distinct positions of the 32 x 4 token grid.
All inputs are finite; a program needn't handle non-finite values.
Results may differ from a plain program's by a relative error of at most 0.003.
Values may be sent and summed in bfloat16 or wider, within the bound.
No kernel may reach another device: no remote copies, remote signals or barrier semaphores. Data moves between devices by JAX's collectives and lax.ppermute only.
A program may use at most 128 MiB of HBM per device.

v0:
```python
from functools import partial

import jax
import jax.numpy as jnp
from jax import lax
from jax.experimental import pallas as pl
from jax.experimental.pallas import tpu as pltpu
from jax.sharding import PartitionSpec as P

F32 = jnp.float32
BF16 = jnp.bfloat16
POS, COLS, PAD = 128, 4, 8
D, C1, CO = 512, 128, 384
TAPS9 = [(row, col) for row in range(3) for col in range(3)]
PHASES = [(i, j) for i in range(2) for j in range(2)]
PAIRS = [(-1, 1), (0, 0), (0, 1), (1, 0)]
PAIRS_OF_TAP = [[(0, 1), (1, 0)], [(0, 0), (0, 1)], [(-1, 1), (0, 0)]]


def token_step(phase, tap):
    return (phase + tap - 1) // 2


def column_mask(step, shape, axis):
    column = lax.broadcasted_iota(jnp.int32, shape, axis) % COLS + step
    return (column >= 0) & (column < COLS)


def spot_mask(row_step, col_step, shape, axis):
    spot = lax.broadcasted_iota(jnp.int32, shape, axis)
    column = spot % COLS + col_step
    row = spot // COLS + row_step
    return (column >= 0) & (column < COLS) & (row >= 0) & (row < POS // COLS)


def call(body, out_shape, scratch=(), flops=0, size=0):
    return pl.pallas_call(
        body,
        out_shape=out_shape,
        scratch_shapes=list(scratch),
        compiler_params=pltpu.CompilerParams(vmem_limit_bytes=48 << 20),
        cost_estimate=pl.CostEstimate(flops=flops, bytes_accessed=size, transcendentals=0),
    )


def struct(shape, dtype):
    return jax.ShapeDtypeStruct(shape, dtype)


def first_conv(tokens_ref, weight_ref, y0_ref, y1_ref, y2_ref, turned_ref, padded):
    padded[0:PAD] = jnp.zeros((PAD, D), F32)
    padded[PAD + POS :] = jnp.zeros((PAD, D), F32)
    tokens = tokens_ref[...]
    padded[PAD : PAD + POS] = tokens.astype(F32)
    total = jnp.zeros((POS, 3 * C1), F32)
    for row, col in TAPS9:
        step = PAD + COLS * (row - 1) + col - 1
        window = padded[step : step + POS]
        if col != 1:
            window = jnp.where(column_mask(col - 1, (POS, D), 0), window, 0.0)
        tap = 3 * row + col
        weight = jnp.concatenate([weight_ref[tap + 9 * k] for k in range(3)], axis=1)
        total = total + jnp.dot(window.astype(BF16), weight, preferred_element_type=F32)
    y0_ref[...] = total[:, 0:C1]
    y1_ref[...] = total[:, C1 : 2 * C1]
    y2_ref[...] = total[:, 2 * C1 :]
    turned_ref[...] = tokens.T


def tap_weight(weight_ref, row, col):
    return jnp.concatenate([weight_ref[9 * k + 3 * row + col] for k in range(3)], axis=0)


def loss_cotangent(before_ref, here_ref, after_ref, weight_ref, bias_ref, pixel_ref, index_ref,
                   cot_ref, turned_ref, padded, moved):
    zeros = jnp.zeros((PAD, 3 * C1), F32)
    padded[0:PAD] = zeros
    padded[PAD + POS :] = zeros
    for k, ref in enumerate((before_ref, here_ref, after_ref)):
        padded[PAD : PAD + POS, k * C1 : (k + 1) * C1] = ref[...].astype(F32)
    for row, col in TAPS9:
        step = PAD + COLS * (row - 1) + col - 1
        window = padded[step : step + POS]
        if col != 1:
            window = jnp.where(column_mask(col - 1, (POS, 3 * C1), 0), window, 0.0)
        moved[3 * row + col] = window.astype(BF16)
    predict = jnp.zeros((4 * POS, CO), F32)
    for row, col in TAPS9:
        lhs = jnp.concatenate(
            [moved[3 * (token_step(i, row) + 1) + token_step(j, col) + 1] for i, j in PHASES], axis=0
        )
        predict = predict + jnp.dot(
            lhs, tap_weight(weight_ref, row, col), preferred_element_type=F32
        )
    predict = predict + bias_ref[...]
    pix = pixel_ref[...].astype(F32)
    center = pix - jnp.mean(pix, axis=-1, keepdims=True)
    spread = jnp.mean(center * center, axis=-1, keepdims=True)
    normed = center * lax.rsqrt(spread + 1e-06)
    spot = lax.broadcasted_iota(jnp.int32, (POS, index_ref.shape[1]), 0)
    hits = jnp.sum((spot == index_ref[...]).astype(F32), axis=1, keepdims=True)
    scale = (2.0 / (4 * CO)) * hits
    turned = []
    for k in range(4):
        cot = scale * (predict[k * POS : (k + 1) * POS] - normed[:, k * CO : (k + 1) * CO])
        cot = cot.astype(BF16)
        cot_ref[k * POS : (k + 1) * POS] = cot
        turned.append(cot.astype(F32).T)
    width = CO // 16
    for block in range(16):
        turned_ref[block] = jnp.concatenate(
            [part[block * width : (block + 1) * width] for part in turned], axis=0
        ).astype(BF16)


def back_conv(cot_ref, weight_ref, u0_ref, u1_ref, u2_ref, padded):
    cot = cot_ref[...]
    sums = {}
    for row, col in TAPS9:
        part = lax.dot_general(
            cot, tap_weight(weight_ref, row, col), (((1,), (1,)), ((), ())),
            preferred_element_type=F32,
        )
        for k, (i, j) in enumerate(PHASES):
            key = (token_step(i, row), token_step(j, col))
            piece = part[k * POS : (k + 1) * POS]
            sums[key] = sums[key] + piece if key in sums else piece
    zeros = jnp.zeros((PAD, 3 * C1), F32)
    total = sums[(0, 0)]
    for k, ((row, col), value) in enumerate(sums.items()):
        if (row, col) == (0, 0):
            continue
        if col != 0:
            value = jnp.where(column_mask(col, (POS, 3 * C1), 0), value, 0.0)
        padded[k, 0:PAD] = zeros
        padded[k, PAD + POS :] = zeros
        padded[k, PAD : PAD + POS] = value
        step = PAD - COLS * row - col
        total = total + padded[k, step : step + POS]
    u0_ref[...] = total[:, 0:C1]
    u1_ref[...] = total[:, C1 : 2 * C1]
    u2_ref[...] = total[:, 2 * C1 :]


def second_grads(before_ref, here_ref, after_ref, turned_ref, out_ref, left):
    clips = turned_ref.shape[0]
    width = CO // 16
    masks = {}
    for row in (-1, 0, 1):
        for col in (-1, 0, 1):
            masks[(row, col)] = spot_mask(row, col, (width, POS), 1)
    for clip in range(clips):
        values = turned_ref[clip].astype(F32)
        parts = []
        for row, i in PAIRS:
            for col, j in PAIRS:
                k = 2 * i + j
                value = values[k * width : (k + 1) * width]
                step = COLS * row + col
                if step != 0:
                    value = pltpu.roll(value, (POS - step) % POS, 1)
                    value = jnp.where(masks[(row, col)], value, 0.0)
                parts.append(value)
        left[:, clip * POS : (clip + 1) * POS] = jnp.concatenate(parts, axis=0).astype(BF16)
    right = jnp.concatenate(
        [ref[...].reshape(clips * POS, C1) for ref in (before_ref, here_ref, after_ref)], axis=1
    )
    both = jnp.dot(left[...], right, preferred_element_type=F32)
    parts = []
    for k in range(3):
        for row in range(3):
            for col in range(3):
                value = None
                for row_pair in PAIRS_OF_TAP[row]:
                    for col_pair in PAIRS_OF_TAP[col]:
                        at = 4 * PAIRS.index(row_pair) + PAIRS.index(col_pair)
                        piece = both[at * width : (at + 1) * width, k * C1 : (k + 1) * C1]
                        value = piece if value is None else value + piece
                parts.append(value)
    parts.append(jnp.zeros((6 * 128 - 27 * width, C1), F32))
    turned = jnp.concatenate(parts, axis=0).T
    out_ref[...] = turned.reshape(out_ref.shape)


def moved_tokens(tokens_ref, out_ref):
    frames, width, _ = tokens_ref.shape
    zeros = jnp.zeros((9 * width, POS), BF16)
    out_ref[:, 0:POS] = zeros
    out_ref[:, (frames + 1) * POS :] = zeros
    for frame in range(frames):
        value = tokens_ref[frame].astype(F32)
        parts = []
        for row, col in TAPS9:
            step = COLS * (row - 1) + col - 1
            if step == 0:
                parts.append(value)
            else:
                part = pltpu.roll(value, (POS - step) % POS, 1)
                parts.append(
                    jnp.where(spot_mask(row - 1, col - 1, (width, POS), 1), part, 0.0)
                )
        out_ref[:, (frame + 1) * POS : (frame + 2) * POS] = jnp.concatenate(parts, axis=0).astype(
            BF16
        )


def first_grads(moved_ref, gz_ref, out_ref):
    frames = gz_ref.shape[0]
    right = gz_ref[...].reshape(frames * POS, C1)
    parts = []
    for k in range(3):
        parts.append(
            jnp.dot(
                moved_ref[:, k * POS : (k + frames) * POS], right, preferred_element_type=F32
            )
        )
    rows = 3 * parts[0].shape[0]
    parts.append(jnp.zeros((out_ref.shape[2] - rows, C1), F32))
    turned = jnp.concatenate(parts, axis=0).T
    out_ref[...] = turned.reshape(out_ref.shape)


def summed_second(parts_ref, out_ref):
    total = jnp.sum(parts_ref[...], axis=0)
    width = out_ref.shape[2]
    for k in range(27):
        out_ref[k] = total[:, k * width : (k + 1) * width]


def summed_first(parts_ref, out_ref):
    total = jnp.sum(parts_ref[...], axis=0)
    high, wide = total.shape
    total = jnp.concatenate([total, jnp.zeros((128 - high, wide), F32)], axis=0)
    turned = total.T
    width = out_ref.shape[1]
    for k in range(27):
        out_ref[k] = turned[k * width : (k + 1) * width, 0:high]


def exchange(value, axis):
    return lax.all_to_all(value, axis, split_axis=0, concat_axis=0, tiled=True)


def up(value, axis="seq"):
    count = lax.axis_size(axis)
    return lax.ppermute(value, axis, [(i, i + 1) for i in range(count - 1)])


def down(value, axis="seq"):
    count = lax.axis_size(axis)
    return lax.ppermute(value, axis, [(i + 1, i) for i in range(count - 1)])


def per_device(tokens, conv_first, bias_first, conv_second, bias_second, pixels, mask_index):
    gelu_tanh = partial(jax.nn.gelu, approximate=True)
    field = tokens.reshape(POS, D)
    pix = exchange(pixels[0], "seq").reshape(POS, 4 * CO)

    plane = struct((POS, C1), F32)
    y0, y1, y2, turned = call(
        first_conv,
        (plane, plane, plane, struct((D, POS), BF16)),
        [pltpu.VMEM((POS + 2 * PAD, D), F32)],
        flops=2 * POS * 27 * D * C1,
        size=4 << 20,
    )(field, conv_first)
    zsum = up(y0) + y1 + down(y2) + bias_first
    hidden = gelu_tanh(zsum).astype(BF16)
    before, after = up(hidden), down(hidden)
    hidden_all = exchange(jnp.broadcast_to(hidden[None], (16, POS, C1)), "dp")

    cot, cot_turned = call(
        loss_cotangent,
        (struct((4 * POS, CO), BF16), struct((16, CO // 4, POS), BF16)),
        [pltpu.VMEM((POS + 2 * PAD, 3 * C1), F32), pltpu.VMEM((9, POS, 3 * C1), BF16)],
        flops=2 * 4 * POS * 27 * C1 * CO,
        size=4 << 20,
    )(before, hidden, after, conv_second, bias_second[None], pix, mask_index)
    u0, u1, u2 = call(
        back_conv,
        (plane, plane, plane),
        [pltpu.VMEM((9, POS + 2 * PAD, 3 * C1), F32)],
        flops=2 * 4 * POS * 27 * C1 * CO,
        size=4 << 20,
    )(cot, conv_second)
    grad_hidden = down(u0) + u1 + up(u2)
    grad_z = jax.vjp(gelu_tanh, zsum)[1](grad_hidden)[0].astype(BF16)

    cot_all = exchange(cot_turned, "dp")
    grad_z_all = exchange(jnp.broadcast_to(grad_z[None], (16, POS, C1)), "seq")
    part_second = call(
        second_grads,
        struct((16, C1 // 16, 6 * 128), F32),
        [pltpu.VMEM((CO, 16 * POS), BF16)],
        flops=2 * 16 * POS * CO * CO,
        size=3 << 20,
    )(up(hidden_all), hidden_all, down(hidden_all), cot_all)
    all_second = exchange(part_second, "seq")

    token_part = exchange(turned.reshape(16, D // 16, POS), "seq")
    moved = call(
        moved_tokens, struct((9 * D // 16, 18 * POS), BF16), flops=1 << 20, size=2 << 20
    )(token_part)
    part_first = call(
        first_grads,
        struct((16, C1 // 16, 7 * 128), F32),
        flops=2 * 16 * POS * 27 * C1 * D // 16,
        size=3 << 20,
    )(moved, grad_z_all)
    all_first = exchange(part_first, "dp")

    grad_first = call(summed_first, struct((27, D // 16, C1 // 16), F32), size=1 << 20)(all_first)
    grad_second = call(summed_second, struct((27, C1 // 16, CO // 16), F32), size=1 << 20)(
        all_second
    )
    return grad_first, grad_second


def solution(mesh):
    return jax.shard_map(
        per_device,
        mesh=mesh,
        in_specs=(
            P("dp", "seq", None, None, None),
            P(),
            P(),
            P(),
            P(),
            P("dp", None, "seq", None, None),
            P("dp", None),
        ),
        out_specs=(P(None, "seq", "dp"), P(None, "seq", "dp")),
        check_vma=False,
    )
```

profile of v0, /device:TPU:1, one launch (start us, length us, event | category | flops | bytes accessed | tf_op | source)
XLA Modules:
  0.0 148.9 jit_solution(1782063174616209582)
XLA Ops:
  0.6 0.9 reshape.16.tokens_ref
  1.6 2.0 %copy-done = bf16[27,512,128]{2,1,0:T(8,128)(2,1)S(1)} copy-done((bf16[27,512,128]{2,1,0:T(8,128)(2,1)S(1)}, bf16[27,512,128]{2,1,0:T(8,128)(2,1)}, u32[]{:S(2)}) %copy-start) | copy-done | bytes 3538968
  4.4 18.9 %all_to_all.35.tokens_ref = bf16[16,32,128]{2,1,0:T(8,128)(2,1)S(1)} all-to-all(bf16[16,32,128]{2,1,0:T(8,128)(2,1)S(1)} %bitcast.2), channel_id=1, replica_groups=mesh['dp'=16,'seq'=16] {'seq'}, dimensions={0} | all-to-all | bytes 262144 | tf_op jit(solution)/shard_map/all_to_all | solution.py:241
  23.3 3.5 %all-to-all-start.1 = ((bf16[16,2,4,1536]{3,2,1,0:T(4,128)(2,1)}), bf16[16,2,4,1536]{3,2,1,0:T(4,128)(2,1)S(1)}, u32[]{:S(2)}, u32[]{:S(2)}) async-start(bf16[16,2,4,1536]{3,2,1,0:T(4,128)(2,1)} %bitcast.1), calls=%async_computation.1 | async-start | bytes 786432 | tf_op jit(solution)/shard_map/all_to_all | solution.py:241
  26.8 1.9 %collective-permute-start.1 = (f32[128,128]{1,0:T(8,128)S(1)}, f32[128,128]{1,0:T(8,128)S(1)}, u32[]{:S(2)}, u32[]{:S(2)}) collective-permute-start(f32[128,128]{1,0:T(8,128)S(1)} %get-tuple-element.14), channel_id=1, source_target_pairs={{1,0},{2,1},{3,2},{4,3},{5,4},{6,5},{7,6},{8,7},{9,8},{10,9},{11,1... | collective-permute-start | bytes 196616 | tf_op jit(solution)/shard_map/ppermute | solution.py:251
  28.7 3.6 %collective-permute-start = (f32[128,128]{1,0:T(8,128)S(1)}, f32[128,128]{1,0:T(8,128)S(1)}, u32[]{:S(2)}, u32[]{:S(2)}) collective-permute-start(f32[128,128]{1,0:T(8,128)S(1)} %get-tuple-element.12), channel_id=1, source_target_pairs={{0,1},{1,2},{2,3},{3,4},{4,5},{5,6},{6,7},{7,8},{8,9},{9,10},{10,1... | collective-permute-start | bytes 196616 | tf_op jit(solution)/shard_map/ppermute | solution.py:246
  32.4 6.0 %collective-permute-done.1 = f32[128,128]{1,0:T(8,128)S(1)} collective-permute-done((f32[128,128]{1,0:T(8,128)S(1)}, f32[128,128]{1,0:T(8,128)S(1)}, u32[]{:S(2)}, u32[]{:S(2)}) %collective-permute-start.1) | collective-permute-done | bytes 65568 | tf_op jit(solution)/shard_map/ppermute | solution.py:251
  38.4 2.5 %all-to-all-done.1 = bf16[16,2,4,1536]{3,2,1,0:T(4,128)(2,1)S(1)} async-done(((bf16[16,2,4,1536]{3,2,1,0:T(4,128)(2,1)}), bf16[16,2,4,1536]{3,2,1,0:T(4,128)(2,1)S(1)}, u32[]{:S(2)}, u32[]{:S(2)}) %all-to-all-start.1) | async-done | bytes 393248 | tf_op jit(solution)/shard_map/all_to_all | solution.py:241
  41.9 6.8 %all-to-all-start.4 = ((bf16[16,128,128]{2,1,0:T(8,128)(2,1)}), bf16[16,128,128]{2,1,0:T(8,128)(2,1)S(1)}, u32[]{:S(2)}, u32[]{:S(2)}) async-start(bf16[16,128,128]{2,1,0:T(8,128)(2,1)} %broadcast_in_dim.8), calls=%async_computation.4 | async-start | bytes 1048576 | tf_op jit(solution)/shard_map/all_to_all | solution.py:241
  48.6 1.9 %collective-permute-start.2 = (bf16[128,128]{1,0:T(8,128)(2,1)S(1)}, bf16[128,128]{1,0:T(8,128)(2,1)S(1)}, u32[]{:S(2)}, u32[]{:S(2)}) collective-permute-start(bf16[128,128]{1,0:T(8,128)(2,1)S(1)} %get-tuple-element.22.here_ref), channel_id=1, source_target_pairs={{0,1},{1,2},{2,3},{3,4},{4,5},{5,6},{6,7},{7,8},{8,9},{9,10},{10,1... | collective-permute-start | bytes 98312 | tf_op jit(solution)/shard_map/ppermute | solution.py:246
  50.5 2.4 %collective-permute-start.3 = (bf16[128,128]{1,0:T(8,128)(2,1)S(1)}, bf16[128,128]{1,0:T(8,128)(2,1)S(1)}, u32[]{:S(2)}, u32[]{:S(2)}) collective-permute-start(bf16[128,128]{1,0:T(8,128)(2,1)S(1)} %get-tuple-element.22.here_ref), channel_id=1, source_target_pairs={{1,0},{2,1},{3,2},{4,3},{5,4},{6,5},{7,6},{8,7},{9,8},{10,9},{11,1... | collective-permute-start | bytes 98312 | tf_op jit(solution)/shard_map/ppermute | solution.py:251
  53.1 3.0 %collective-permute-done.3.after_ref = bf16[128,128]{1,0:T(8,128)(2,1)S(1)} collective-permute-done((bf16[128,128]{1,0:T(8,128)(2,1)S(1)}, bf16[128,128]{1,0:T(8,128)(2,1)S(1)}, u32[]{:S(2)}, u32[]{:S(2)}) %collective-permute-start.3) | collective-permute-done | bytes 32800 | tf_op jit(solution)/shard_map/ppermute | solution.py:251
  56.1 1.7 %copy-done.1 = bf16[27,128,384]{2,1,0:T(8,128)(2,1)S(1)} copy-done((bf16[27,128,384]{2,1,0:T(8,128)(2,1)S(1)}, bf16[27,128,384]{2,1,0:T(8,128)(2,1)}, u32[]{:S(2)}) %copy-start.1) | copy-done | bytes 2654232
  57.8 3.3 %shard_map.88 = (bf16[512,384]{1,0:T(8,128)(2,1)S(1)}, bf16[16,96,128]{2,1,0:T(8,128)(2,1)}) custom-call(bf16[128,128]{1,0:T(8,128)(2,1)S(1)} %collective-permute-done.2.before_ref, bf16[128,128]{1,0:T(8,128)(2,1)S(1)} %get-tuple-element.22.here_ref, bf16[128,128]{1,0:T(8,128)(2,1)S(1)} %collective-permute-done.3.after_ref, ...), custom_call_target="tpu_custom_call" | custom-call | flops 1358954496 | bytes 4194304 | tf_op jit(solution)/shard_map/pallas_call | solution.py:272
  61.1 6.6 %all-to-all-start.5 = ((bf16[16,96,128]{2,1,0:T(8,128)(2,1)}), bf16[16,96,128]{2,1,0:T(8,128)(2,1)S(1)}, u32[]{:S(2)}, u32[]{:S(2)}) async-start(bf16[16,96,128]{2,1,0:T(8,128)(2,1)} %get-tuple-element.19), calls=%async_computation.5 | async-start | bytes 786432 | tf_op jit(solution)/shard_map/all_to_all | solution.py:241
  67.8 1.7 %copy-done.2 = bf16[27,128,384]{2,1,0:T(8,128)(2,1)S(1)} copy-done((bf16[27,128,384]{2,1,0:T(8,128)(2,1)S(1)}, bf16[27,128,384]{2,1,0:T(8,128)(2,1)}, u32[]{:S(2)}) %copy-start.2) | copy-done | bytes 2654232
  69.5 2.4 %shard_map.89 = (f32[128,128]{1,0:T(8,128)S(1)}, f32[128,128]{1,0:T(8,128)S(1)}, f32[128,128]{1,0:T(8,128)S(1)}) custom-call(bf16[512,384]{1,0:T(8,128)(2,1)S(1)} %get-tuple-element.15.cot_ref, bf16[27,128,384]{2,1,0:T(8,128)(2,1)S(1)} %copy-done.2), custom_call_target="tpu_custom_call" | custom-call | flops 1358954496 | bytes 4194304 | tf_op jit(solution)/shard_map/pallas_call | solution.py:279
  71.9 1.9 %collective-permute-start.5 = (f32[128,128]{1,0:T(8,128)S(1)}, f32[128,128]{1,0:T(8,128)S(1)}, u32[]{:S(2)}, u32[]{:S(2)}) collective-permute-start(f32[128,128]{1,0:T(8,128)S(1)} %get-tuple-element.18), channel_id=1, source_target_pairs={{0,1},{1,2},{2,3},{3,4},{4,5},{5,6},{6,7},{7,8},{8,9},{9,10},{10,1... | collective-permute-start | bytes 196616 | tf_op jit(solution)/shard_map/ppermute | solution.py:246
  73.8 2.4 %collective-permute-start.4 = (f32[128,128]{1,0:T(8,128)S(1)}, f32[128,128]{1,0:T(8,128)S(1)}, u32[]{:S(2)}, u32[]{:S(2)}) collective-permute-start(f32[128,128]{1,0:T(8,128)S(1)} %get-tuple-element.16), channel_id=1, source_target_pairs={{1,0},{2,1},{3,2},{4,3},{5,4},{6,5},{7,6},{8,7},{9,8},{10,9},{11,1... | collective-permute-start | bytes 196616 | tf_op jit(solution)/shard_map/ppermute | solution.py:251
  76.3 3.2 %collective-permute-done.4 = f32[128,128]{1,0:T(8,128)S(1)} collective-permute-done((f32[128,128]{1,0:T(8,128)S(1)}, f32[128,128]{1,0:T(8,128)S(1)}, u32[]{:S(2)}, u32[]{:S(2)}) %collective-permute-start.4) | collective-permute-done | bytes 65568 | tf_op jit(solution)/shard_map/ppermute | solution.py:251
  79.5 0.9 broadcast_in_dim.7
  80.4 6.8 %all-to-all-start.2 = ((bf16[16,128,128]{2,1,0:T(8,128)(2,1)}), bf16[16,128,128]{2,1,0:T(8,128)(2,1)S(1)}, u32[]{:S(2)}, u32[]{:S(2)}) async-start(bf16[16,128,128]{2,1,0:T(8,128)(2,1)} %broadcast_in_dim.7), calls=%async_computation.2 | async-start | bytes 1048576 | tf_op jit(solution)/shard_map/all_to_all | solution.py:241
  87.3 3.5 %collective-permute-start.6 = (bf16[16,128,128]{2,1,0:T(8,128)(2,1)S(1)}, bf16[16,128,128]{2,1,0:T(8,128)(2,1)S(1)}, u32[]{:S(2)}, u32[]{:S(2)}) collective-permute-start(bf16[16,128,128]{2,1,0:T(8,128)(2,1)S(1)} %all-to-all-done.4.here_ref), channel_id=1, source_target_pairs={{0,1},{1,2},{2,3},{3,4},{4,5},{5,6},{6,7},{7,8},{8,9},{9,10},{10,1... | collective-permute-start | bytes 1572872 | tf_op jit(solution)/shard_map/ppermute | solution.py:246
  90.8 1.9 %collective-permute-start.7 = (bf16[16,128,128]{2,1,0:T(8,128)(2,1)S(1)}, bf16[16,128,128]{2,1,0:T(8,128)(2,1)S(1)}, u32[]{:S(2)}, u32[]{:S(2)}) collective-permute-start(bf16[16,128,128]{2,1,0:T(8,128)(2,1)S(1)} %all-to-all-done.4.here_ref), channel_id=1, source_target_pairs={{1,0},{2,1},{3,2},{4,3},{5,4},{6,5},{7,6},{8,7},{9,8},{10,9},{11,1... | collective-permute-start | bytes 1572872 | tf_op jit(solution)/shard_map/ppermute | solution.py:251
  92.7 12.1 %collective-permute-done.6.before_ref = bf16[16,128,128]{2,1,0:T(8,128)(2,1)S(1)} collective-permute-done((bf16[16,128,128]{2,1,0:T(8,128)(2,1)S(1)}, bf16[16,128,128]{2,1,0:T(8,128)(2,1)S(1)}, u32[]{:S(2)}, u32[]{:S(2)}) %collective-permute-start.6) | collective-permute-done | bytes 524320 | tf_op jit(solution)/shard_map/ppermute | solution.py:246
  104.8 1.8 %collective-permute-done.7.after_ref = bf16[16,128,128]{2,1,0:T(8,128)(2,1)S(1)} collective-permute-done((bf16[16,128,128]{2,1,0:T(8,128)(2,1)S(1)}, bf16[16,128,128]{2,1,0:T(8,128)(2,1)S(1)}, u32[]{:S(2)}, u32[]{:S(2)}) %collective-permute-start.7) | collective-permute-done | bytes 524320 | tf_op jit(solution)/shard_map/ppermute | solution.py:251
  106.7 2.0 %shard_map.92 = f32[16,8,768]{2,1,0:T(8,128)} custom-call(bf16[16,128,128]{2,1,0:T(8,128)(2,1)S(1)} %collective-permute-done.6.before_ref, bf16[16,128,128]{2,1,0:T(8,128)(2,1)S(1)} %all-to-all-done.4.here_ref, bf16[16,128,128]{2,1,0:T(8,128)(2,1)S(1)} %collective-permute-done.7.after_ref, bf16[16,96,128]{2,1,0:T(8,128)(2,1)S(1)} %all-to-all-done.5.turned_ref), custom_call_target="tpu_custom_call" | custom-call | flops 603979776 | bytes 3145728 | tf_op jit(solution)/shard_map/pallas_call | solution.py:291
  108.6 6.4 %all-to-all-start.6 = ((f32[16,8,768]{2,1,0:T(8,128)}), f32[16,8,768]{2,1,0:T(8,128)S(1)}, u32[]{:S(2)}, u32[]{:S(2)}) async-start(f32[16,8,768]{2,1,0:T(8,128)} %shard_map.92), calls=%async_computation.6 | async-start | bytes 786432 | tf_op jit(solution)/shard_map/all_to_all | solution.py:241
  115.4 2.0 %shard_map.90 = f32[16,8,896]{2,1,0:T(8,128)} custom-call(bf16[288,2304]{1,0:T(8,128)(2,1)S(1)} %shard_map.87.moved_ref, bf16[16,128,128]{2,1,0:T(8,128)(2,1)S(1)} %all-to-all-done.2.gz_ref), custom_call_target="tpu_custom_call" | custom-call | flops 452984832 | bytes 3145728 | tf_op jit(solution)/shard_map/pallas_call | solution.py:304
  117.4 12.2 %all-to-all-done.6.parts_ref = f32[16,8,768]{2,1,0:T(8,128)S(1)} async-done(((f32[16,8,768]{2,1,0:T(8,128)}), f32[16,8,768]{2,1,0:T(8,128)S(1)}, u32[]{:S(2)}, u32[]{:S(2)}) %all-to-all-start.6) | async-done | bytes 393248 | tf_op jit(solution)/shard_map/all_to_all | solution.py:241
  129.6 6.9 %all-to-all-start.3 = ((f32[16,8,896]{2,1,0:T(8,128)}), f32[16,8,896]{2,1,0:T(8,128)S(1)}, u32[]{:S(2)}, u32[]{:S(2)}) async-start(f32[16,8,896]{2,1,0:T(8,128)} %shard_map.90), calls=%async_computation.3 | async-start | bytes 917504 | tf_op jit(solution)/shard_map/all_to_all | solution.py:241
  137.4 10.4 %all-to-all-done.3.parts_ref = f32[16,8,896]{2,1,0:T(8,128)S(1)} async-done(((f32[16,8,896]{2,1,0:T(8,128)}), f32[16,8,896]{2,1,0:T(8,128)S(1)}, u32[]{:S(2)}, u32[]{:S(2)}) %all-to-all-start.3) | async-done | bytes 458784 | tf_op jit(solution)/shard_map/all_to_all | solution.py:241
  (26 shorter events, 4.2 us)
Async XLA Ops:
  0.6 37.7 %copy-start.5 = (f32[128]{0:T(128)S(1)}, f32[128]{0:T(128)}, u32[]{:S(2)}) copy-start(f32[128]{0:T(128)} %param.9) | copy-start | bytes 1540
  1.6 2.0 %copy-start = (bf16[27,512,128]{2,1,0:T(8,128)(2,1)S(1)}, bf16[27,512,128]{2,1,0:T(8,128)(2,1)}, u32[]{:S(2)}) copy-start(bf16[27,512,128]{2,1,0:T(8,128)(2,1)} %weight_ref.3) | copy-start | bytes 10616836
  3.6 49.4 %copy-start.4 = (f32[384]{0:T(512)S(1)}, f32[384]{0:T(512)}, u32[]{:S(2)}) copy-start(f32[384]{0:T(512)} %param.11) | copy-start | bytes 4612
  4.4 51.7 %copy-start.3 = (s32[1,115]{1,0:T(1,128)S(1)}, s32[1,115]{1,0:T(1,128)}, u32[]{:S(2)}) copy-start(s32[1,115]{1,0:T(1,128)} %index_ref.1) | copy-start | bytes 1384
  23.3 17.6 %all-to-all-start.1 = ((bf16[16,2,4,1536]{3,2,1,0:T(4,128)(2,1)}), bf16[16,2,4,1536]{3,2,1,0:T(4,128)(2,1)S(1)}, u32[]{:S(2)}, u32[]{:S(2)}) async-start(bf16[16,2,4,1536]{3,2,1,0:T(4,128)(2,1)} %bitcast.1), calls=%async_computation.1 | async-start | bytes 786432 | tf_op jit(solution)/shard_map/all_to_all | solution.py:241
  26.8 11.6 %collective-permute-start.1 = (f32[128,128]{1,0:T(8,128)S(1)}, f32[128,128]{1,0:T(8,128)S(1)}, u32[]{:S(2)}, u32[]{:S(2)}) collective-permute-start(f32[128,128]{1,0:T(8,128)S(1)} %get-tuple-element.14), channel_id=1, source_target_pairs={{1,0},{2,1},{3,2},{4,3},{5,4},{6,5},{7,6},{8,7},{9,8},{10,9},{11,1... | collective-permute-start | bytes 196616 | tf_op jit(solution)/shard_map/ppermute | solution.py:251
  28.7 9.6 %collective-permute-start = (f32[128,128]{1,0:T(8,128)S(1)}, f32[128,128]{1,0:T(8,128)S(1)}, u32[]{:S(2)}, u32[]{:S(2)}) collective-permute-start(f32[128,128]{1,0:T(8,128)S(1)} %get-tuple-element.12), channel_id=1, source_target_pairs={{0,1},{1,2},{2,3},{3,4},{4,5},{5,6},{6,7},{7,8},{8,9},{9,10},{10,1... | collective-permute-start | bytes 196616 | tf_op jit(solution)/shard_map/ppermute | solution.py:246
  41.9 19.3 %all-to-all-start.4 = ((bf16[16,128,128]{2,1,0:T(8,128)(2,1)}), bf16[16,128,128]{2,1,0:T(8,128)(2,1)S(1)}, u32[]{:S(2)}, u32[]{:S(2)}) async-start(bf16[16,128,128]{2,1,0:T(8,128)(2,1)} %broadcast_in_dim.8), calls=%async_computation.4 | async-start | bytes 1048576 | tf_op jit(solution)/shard_map/all_to_all | solution.py:241
  48.6 4.5 %collective-permute-start.2 = (bf16[128,128]{1,0:T(8,128)(2,1)S(1)}, bf16[128,128]{1,0:T(8,128)(2,1)S(1)}, u32[]{:S(2)}, u32[]{:S(2)}) collective-permute-start(bf16[128,128]{1,0:T(8,128)(2,1)S(1)} %get-tuple-element.22.here_ref), channel_id=1, source_target_pairs={{0,1},{1,2},{2,3},{3,4},{4,5},{5,6},{6,7},{7,8},{8,9},{9,10},{10,1... | collective-permute-start | bytes 98312 | tf_op jit(solution)/shard_map/ppermute | solution.py:246
  50.5 5.5 %collective-permute-start.3 = (bf16[128,128]{1,0:T(8,128)(2,1)S(1)}, bf16[128,128]{1,0:T(8,128)(2,1)S(1)}, u32[]{:S(2)}, u32[]{:S(2)}) collective-permute-start(bf16[128,128]{1,0:T(8,128)(2,1)S(1)} %get-tuple-element.22.here_ref), channel_id=1, source_target_pairs={{1,0},{2,1},{3,2},{4,3},{5,4},{6,5},{7,6},{8,7},{9,8},{10,9},{11,1... | collective-permute-start | bytes 98312 | tf_op jit(solution)/shard_map/ppermute | solution.py:251
  56.1 1.8 %copy-start.1 = (bf16[27,128,384]{2,1,0:T(8,128)(2,1)S(1)}, bf16[27,128,384]{2,1,0:T(8,128)(2,1)}, u32[]{:S(2)}) copy-start(bf16[27,128,384]{2,1,0:T(8,128)(2,1)} %weight_ref.5) | copy-start | bytes 7962628
  61.1 18.4 %all-to-all-start.5 = ((bf16[16,96,128]{2,1,0:T(8,128)(2,1)}), bf16[16,96,128]{2,1,0:T(8,128)(2,1)S(1)}, u32[]{:S(2)}, u32[]{:S(2)}) async-start(bf16[16,96,128]{2,1,0:T(8,128)(2,1)} %get-tuple-element.19), calls=%async_computation.5 | async-start | bytes 786432 | tf_op jit(solution)/shard_map/all_to_all | solution.py:241
  67.8 1.8 %copy-start.2 = (bf16[27,128,384]{2,1,0:T(8,128)(2,1)S(1)}, bf16[27,128,384]{2,1,0:T(8,128)(2,1)}, u32[]{:S(2)}) copy-start(bf16[27,128,384]{2,1,0:T(8,128)(2,1)} %weight_ref.5) | copy-start | bytes 7962628
  71.9 4.3 %collective-permute-start.5 = (f32[128,128]{1,0:T(8,128)S(1)}, f32[128,128]{1,0:T(8,128)S(1)}, u32[]{:S(2)}, u32[]{:S(2)}) collective-permute-start(f32[128,128]{1,0:T(8,128)S(1)} %get-tuple-element.18), channel_id=1, source_target_pairs={{0,1},{1,2},{2,3},{3,4},{4,5},{5,6},{6,7},{7,8},{8,9},{9,10},{10,1... | collective-permute-start | bytes 196616 | tf_op jit(solution)/shard_map/ppermute | solution.py:246
  73.8 5.6 %collective-permute-start.4 = (f32[128,128]{1,0:T(8,128)S(1)}, f32[128,128]{1,0:T(8,128)S(1)}, u32[]{:S(2)}, u32[]{:S(2)}) collective-permute-start(f32[128,128]{1,0:T(8,128)S(1)} %get-tuple-element.16), channel_id=1, source_target_pairs={{1,0},{2,1},{3,2},{4,3},{5,4},{6,5},{7,6},{8,7},{9,8},{10,9},{11,1... | collective-permute-start | bytes 196616 | tf_op jit(solution)/shard_map/ppermute | solution.py:251
  80.4 28.2 %all-to-all-start.2 = ((bf16[16,128,128]{2,1,0:T(8,128)(2,1)}), bf16[16,128,128]{2,1,0:T(8,128)(2,1)S(1)}, u32[]{:S(2)}, u32[]{:S(2)}) async-start(bf16[16,128,128]{2,1,0:T(8,128)(2,1)} %broadcast_in_dim.7), calls=%async_computation.2 | async-start | bytes 1048576 | tf_op jit(solution)/shard_map/all_to_all | solution.py:241
  87.3 17.6 %collective-permute-start.6 = (bf16[16,128,128]{2,1,0:T(8,128)(2,1)S(1)}, bf16[16,128,128]{2,1,0:T(8,128)(2,1)S(1)}, u32[]{:S(2)}, u32[]{:S(2)}) collective-permute-start(bf16[16,128,128]{2,1,0:T(8,128)(2,1)S(1)} %all-to-all-done.4.here_ref), channel_id=1, source_target_pairs={{0,1},{1,2},{2,3},{3,4},{4,5},{5,6},{6,7},{7,8},{8,9},{9,10},{10,1... | collective-permute-start | bytes 1572872 | tf_op jit(solution)/shard_map/ppermute | solution.py:246
  90.8 15.9 %collective-permute-start.7 = (bf16[16,128,128]{2,1,0:T(8,128)(2,1)S(1)}, bf16[16,128,128]{2,1,0:T(8,128)(2,1)S(1)}, u32[]{:S(2)}, u32[]{:S(2)}) collective-permute-start(bf16[16,128,128]{2,1,0:T(8,128)(2,1)S(1)} %all-to-all-done.4.here_ref), channel_id=1, source_target_pairs={{1,0},{2,1},{3,2},{4,3},{5,4},{6,5},{7,6},{8,7},{9,8},{10,9},{11,1... | collective-permute-start | bytes 1572872 | tf_op jit(solution)/shard_map/ppermute | solution.py:251
  108.6 21.0 %all-to-all-start.6 = ((f32[16,8,768]{2,1,0:T(8,128)}), f32[16,8,768]{2,1,0:T(8,128)S(1)}, u32[]{:S(2)}, u32[]{:S(2)}) async-start(f32[16,8,768]{2,1,0:T(8,128)} %shard_map.92), calls=%async_computation.6 | async-start | bytes 786432 | tf_op jit(solution)/shard_map/all_to_all | solution.py:241
  129.6 18.2 %all-to-all-start.3 = ((f32[16,8,896]{2,1,0:T(8,128)}), f32[16,8,896]{2,1,0:T(8,128)S(1)}, u32[]{:S(2)}, u32[]{:S(2)}) async-start(f32[16,8,896]{2,1,0:T(8,128)} %shard_map.90), calls=%async_computation.3 | async-start | bytes 917504 | tf_op jit(solution)/shard_map/all_to_all | solution.py:241
where the time goes:
time: 150 us; the launch traced here: 149 us
  starting transfers between devices  56.7 us (38%)
  waiting for transfers between devices  51.3 us (34%)
  blocking collectives  18.9 us (13%)
  Pallas kernels  11 us (7%)
  local copies, waits for them, and re-layouts  9.97 us (7%)
    all_to_all x6, starting transfers between devices, exchange(): return lax.all_to_all(value, axis, split_axis=0, concat_axis=0, tiled=True)  37.1 us
    all_to_all x6, waiting for transfers between devices, exchange(): return lax.all_to_all(value, axis, split_axis=0, concat_axis=0, tiled=True)  25.2 us
    all_to_all x1, blocking collectives, exchange(): return lax.all_to_all(value, axis, split_axis=0, concat_axis=0, tiled=True)  18.9 us
    ppermute x4, waiting for transfers between devices, down(): return lax.ppermute(value, axis, [(i + 1, i) for i in range(count - 1)])  14 us
    ppermute x4, waiting for transfers between devices, up(): return lax.ppermute(value, axis, [(i, i + 1) for i in range(count - 1)])  12.1 us
    ppermute x4, starting transfers between devices, up(): return lax.ppermute(value, axis, [(i, i + 1) for i in range(count - 1)])  11 us
    ppermute x4, starting transfers between devices, down(): return lax.ppermute(value, axis, [(i + 1, i) for i in range(count - 1)])  8.65 us
    unnamed x14, local copies, waits for them, and re-layouts  7.1 us
  transfers between devices with their start and end apart: 14, of which 8 were waited for; matrix products, arithmetic and copies ran while one was open for 1% of the time, Pallas kernels for 7%

commit v1 on v0

v1 whole, which is shorter than its diff:
```python
from functools import partial

import jax
import jax.numpy as jnp
from jax import lax
from jax.experimental import pallas as pl
from jax.experimental.pallas import tpu as pltpu
from jax.sharding import PartitionSpec as P

F32 = jnp.float32
BF16 = jnp.bfloat16
POS, COLS, PAD = 128, 4, 8
D, C1, CO = 512, 128, 384
CHUNK = 4 * CO // 16
TAPS9 = [(row, col) for row in range(3) for col in range(3)]
PHASES = [(i, j) for i in range(2) for j in range(2)]
PAIRS = [(-1, 1), (0, 0), (0, 1), (1, 0)]
PAIRS_OF_TAP = [[(0, 1), (1, 0)], [(0, 0), (0, 1)], [(-1, 1), (0, 0)]]


def token_step(phase, tap):
    return (phase + tap - 1) // 2


def column_mask(step, shape, axis):
    column = lax.broadcasted_iota(jnp.int32, shape, axis) % COLS + step
    return (column >= 0) & (column < COLS)


def spot_mask(row_step, col_step, shape, axis):
    spot = lax.broadcasted_iota(jnp.int32, shape, axis)
    column = spot % COLS + col_step
    row = spot // COLS + row_step
    return (column >= 0) & (column < COLS) & (row >= 0) & (row < POS // COLS)


def call(body, out_shape, in_specs, scratch=(), flops=0, size=0, limit=16):
    return pl.pallas_call(
        body,
        out_shape=out_shape,
        in_specs=in_specs,
        scratch_shapes=list(scratch),
        compiler_params=pltpu.CompilerParams(vmem_limit_bytes=limit << 20),
        cost_estimate=pl.CostEstimate(flops=flops, bytes_accessed=size, transcendentals=0),
    )


def struct(shape, dtype):
    return jax.ShapeDtypeStruct(shape, dtype)


SMEM, VMEM, HBM = pltpu.SMEM, pltpu.VMEM, pltpu.HBM


def spots(*kinds):
    return [pl.BlockSpec(memory_space=kind) for kind in kinds]


def packed_inputs(pixel_ref, tokens_ref, out_ref):
    turned = tokens_ref[...].T
    width = D // 16
    for block in range(16):
        pix = pixel_ref[block].astype(F32)
        out_ref[block, 0:CHUNK] = jnp.concatenate(
            [pix[:, n * 128 : (n + 1) * 128] for n in range(4 * CO // 128)], axis=0
        ).astype(BF16)
        out_ref[block, CHUNK:] = turned[block * width : (block + 1) * width]


def first_conv(place_ref, tokens_ref, weight_ref, pair_ref, keep_ref, cross_ref, padded):
    padded[0:PAD] = jnp.zeros((PAD, D), F32)
    padded[PAD + POS :] = jnp.zeros((PAD, D), F32)
    padded[PAD : PAD + POS] = tokens_ref[...].astype(F32)
    total = jnp.zeros((POS, 3 * C1), F32)
    for row, col in TAPS9:
        step = PAD + COLS * (row - 1) + col - 1
        window = padded[step : step + POS]
        if col != 1:
            window = jnp.where(column_mask(col - 1, (POS, D), 0), window, 0.0)
        tap = 3 * row + col
        weight = jnp.concatenate([weight_ref[tap + 9 * k] for k in range(3)], axis=1)
        total = total + jnp.dot(window.astype(BF16), weight, preferred_element_type=F32)
    to_next, to_last = total[:, 0:C1], total[:, 2 * C1 :]
    even = place_ref[0] == 0
    pair_ref[...] = jnp.where(even, to_next, to_last)
    keep_ref[...] = total[:, C1 : 2 * C1]
    cross_ref[...] = jnp.where(even, to_last, to_next)


def tap_weight(weight_ref, row, col):
    return jnp.concatenate([weight_ref[9 * k + 3 * row + col] for k in range(3)], axis=0)


def loss_and_back(place_ref, pair_ref, here_ref, cross_ref, weight_ref, bias_ref, packed_ref,
                  index_ref, blocks_ref, to_pair_ref, keep_ref, to_cross_ref,
                  padded, moved, cots, shifted):
    even = place_ref[0] == 0
    zeros = jnp.zeros((PAD, 3 * C1), F32)
    padded[0:PAD] = zeros
    padded[PAD + POS :] = zeros
    pair, cross = pair_ref[...].astype(F32), cross_ref[...].astype(F32)
    frames = (jnp.where(even, cross, pair), here_ref[...].astype(F32), jnp.where(even, pair, cross))
    for k, value in enumerate(frames):
        padded[PAD : PAD + POS, k * C1 : (k + 1) * C1] = value
        narrow = value.astype(BF16)
        for block in range(16):
            blocks_ref[block, CHUNK + k * POS : CHUNK + (k + 1) * POS] = narrow
    for row, col in TAPS9:
        step = PAD + COLS * (row - 1) + col - 1
        window = padded[step : step + POS]
        if col != 1:
            window = jnp.where(column_mask(col - 1, (POS, 3 * C1), 0), window, 0.0)
        moved[3 * row + col] = window.astype(BF16)
    slabs = []
    for slab in range(16):
        part = packed_ref[slab, 0:CHUNK].astype(F32)
        slabs.append(
            jnp.concatenate([part[8 * n : 8 * n + 8] for n in range(4 * CO // 128)], axis=1)
        )
    pix = jnp.concatenate(slabs, axis=0)
    center = pix - jnp.mean(pix, axis=-1, keepdims=True)
    spread = jnp.mean(center * center, axis=-1, keepdims=True)
    normed = center * lax.rsqrt(spread + 1e-06)
    spot = lax.broadcasted_iota(jnp.int32, (POS, index_ref.shape[1]), 0)
    hits = jnp.sum((spot == index_ref[...]).astype(F32), axis=1, keepdims=True)
    scale = (2.0 / (4 * CO)) * hits
    predict = jnp.zeros((4 * POS, CO), F32)
    for row, col in TAPS9:
        lhs = jnp.concatenate(
            [moved[3 * (token_step(i, row) + 1) + token_step(j, col) + 1] for i, j in PHASES], axis=0
        )
        predict = predict + jnp.dot(
            lhs, tap_weight(weight_ref, row, col), preferred_element_type=F32
        )
    predict = predict + bias_ref[...]
    turned = []
    for k in range(4):
        cot = scale * (predict[k * POS : (k + 1) * POS] - normed[:, k * CO : (k + 1) * CO])
        cot = cot.astype(BF16)
        cots[k * POS : (k + 1) * POS] = cot
        turned.append(cot.astype(F32).T)
    width = CO // 16
    for block in range(16):
        blocks_ref[block, 0:CHUNK] = jnp.concatenate(
            [part[block * width : (block + 1) * width] for part in turned], axis=0
        ).astype(BF16)

    cot = cots[...]
    sums = {}
    for row, col in TAPS9:
        part = lax.dot_general(
            cot, tap_weight(weight_ref, row, col), (((1,), (1,)), ((), ())),
            preferred_element_type=F32,
        )
        for k, (i, j) in enumerate(PHASES):
            key = (token_step(i, row), token_step(j, col))
            piece = part[k * POS : (k + 1) * POS]
            sums[key] = sums[key] + piece if key in sums else piece
    total = sums[(0, 0)]
    for k, ((row, col), value) in enumerate(sums.items()):
        if (row, col) == (0, 0):
            continue
        if col != 0:
            value = jnp.where(column_mask(col, (POS, 3 * C1), 0), value, 0.0)
        shifted[k, 0:PAD] = zeros
        shifted[k, PAD + POS :] = zeros
        shifted[k, PAD : PAD + POS] = value
        step = PAD - COLS * row - col
        total = total + shifted[k, step : step + POS]
    to_last, to_next = total[:, 0:C1], total[:, 2 * C1 :]
    to_pair_ref[...] = jnp.where(even, to_next, to_last)
    keep_ref[...] = total[:, C1 : 2 * C1]
    to_cross_ref[...] = jnp.where(even, to_last, to_next)


def second_grads(blocks_ref, out_ref, left, right):
    wide, thin = CO // 16, C1 // 16
    masks = {}
    for row in (-1, 0, 1):
        for col in (-1, 0, 1):
            masks[(row, col)] = spot_mask(row, col, (1, POS), 1)
    for clip in range(16):
        lanes = slice(clip * POS, (clip + 1) * POS)
        value = blocks_ref[clip, 0:CHUNK].astype(F32)
        parts = []
        for row, i in PAIRS:
            for col, j in PAIRS:
                phase = 2 * i + j
                part = value[phase * wide : (phase + 1) * wide]
                step = COLS * row + col
                if step != 0:
                    part = pltpu.roll(part, (POS - step) % POS, 1)
                    part = jnp.where(masks[(row, col)], part, 0.0)
                parts.append(part)
        left[:, lanes] = jnp.concatenate(parts, axis=0).astype(BF16)
        for k in range(3):
            right[lanes, k * C1 : (k + 1) * C1] = blocks_ref[
                clip, CHUNK + k * POS : CHUNK + (k + 1) * POS
            ]
    both = jnp.dot(left[...], right[...], preferred_element_type=F32)
    parts = []
    for k in range(3):
        for row in range(3):
            for col in range(3):
                value = None
                for row_pair in PAIRS_OF_TAP[row]:
                    for col_pair in PAIRS_OF_TAP[col]:
                        at = (4 * PAIRS.index(row_pair) + PAIRS.index(col_pair)) * wide
                        piece = both[at : at + wide, k * C1 : (k + 1) * C1]
                        value = piece if value is None else value + piece
                parts.append(value)
    parts.append(jnp.zeros((6 * 128 - 27 * wide, C1), F32))
    turned = jnp.concatenate(parts, axis=0).T
    for block in range(16):
        two = turned[block * thin : (block + 1) * thin]
        out_ref[block] = jnp.concatenate(
            [two[:, 128 * n : 128 * (n + 1)] for n in range(6)], axis=0
        ).astype(out_ref.dtype)


def first_grads(packed_ref, gz_ref, out_ref, moved):
    width, thin = D // 16, C1 // 16
    zeros = jnp.zeros((9 * width, POS), BF16)
    moved[:, 0:POS] = zeros
    moved[:, 17 * POS :] = zeros
    for frame in range(16):
        value = packed_ref[frame, CHUNK:].astype(F32)
        parts = []
        for row, col in TAPS9:
            part = value
            step = COLS * (row - 1) + col - 1
            if step != 0:
                part = pltpu.roll(value, (POS - step) % POS, 1)
                part = jnp.where(spot_mask(row - 1, col - 1, (1, POS), 1), part, 0.0)
            parts.append(part)
        moved[:, (frame + 1) * POS : (frame + 2) * POS] = jnp.concatenate(parts, axis=0).astype(
            BF16
        )
    right = gz_ref[...].reshape(16 * POS, C1)
    parts = []
    for k in range(3):
        parts.append(
            jnp.dot(moved[:, k * POS : (k + 16) * POS], right, preferred_element_type=F32)
        )
    parts.append(jnp.zeros((8 * 128 - 27 * width, C1), F32))
    turned = jnp.concatenate(parts, axis=0).T
    for block in range(16):
        one = turned[block * thin : (block + 1) * thin]
        out_ref[block] = jnp.concatenate(
            [one[:, 128 * n : 128 * (n + 1)] for n in range(8)], axis=0
        ).astype(out_ref.dtype)


def summed(parts_ref, out_ref):
    total = parts_ref[0].astype(F32)
    for source in range(1, 16):
        total = total + parts_ref[source].astype(F32)
    _, rows, width = out_ref.shape
    total = jnp.concatenate(
        [total[rows * n : rows * (n + 1)] for n in range(total.shape[0] // rows)], axis=1
    )
    for k in range(27):
        out_ref[k] = total[:, k * width : (k + 1) * width]


def exchange(value, axis):
    return lax.all_to_all(value, axis, split_axis=0, concat_axis=0, tiled=True)


def with_pair(value):
    return lax.ppermute(value, "seq", [(i, i ^ 1) for i in range(16)])


def with_cross(value):
    swaps = [(i, i + 1) for i in range(1, 15, 2)]
    return lax.ppermute(value, "seq", swaps + [(j, i) for i, j in swaps])


def per_device(tokens, conv_first, bias_first, conv_second, bias_second, pixels, mask_index):
    gelu_tanh = partial(jax.nn.gelu, approximate=True)
    place = (lax.axis_index("seq") % 2).reshape(1).astype(jnp.int32)
    field = tokens.reshape(POS, D)
    packed = call(
        packed_inputs, struct((16, CHUNK + D // 16, POS), BF16), spots(VMEM, VMEM)
    )(pixels.reshape(16, 8, 4 * CO), field)
    packed = exchange(packed, "seq")

    plane = struct((POS, C1), F32)
    pair, keep, cross = call(
        first_conv,
        (plane, plane, plane),
        spots(SMEM, VMEM, VMEM),
        [pltpu.VMEM((POS + 2 * PAD, D), F32)],
    )(place, field, conv_first)
    zsum = with_pair(pair) + keep + with_cross(cross) + bias_first
    hidden = gelu_tanh(zsum).astype(BF16)

    blocks, pair, keep, cross = call(
        loss_and_back,
        (struct((16, CHUNK + 3 * POS, POS), BF16), plane, plane, plane),
        spots(SMEM, *[VMEM] * 7),
        [
            pltpu.VMEM((POS + 2 * PAD, 3 * C1), F32),
            pltpu.VMEM((9, POS, 3 * C1), BF16),
            pltpu.VMEM((4 * POS, CO), BF16),
            pltpu.VMEM((9, POS + 2 * PAD, 3 * C1), F32),
        ],
    )(
        place, with_pair(hidden), hidden, with_cross(hidden), conv_second, bias_second[None],
        packed, mask_index,
    )
    blocks = exchange(blocks, "dp")
    grad_hidden = with_pair(pair) + keep + with_cross(cross)
    grad_z = jax.vjp(gelu_tanh, zsum)[1](grad_hidden)[0].astype(BF16)
    grad_z = lax.all_gather(grad_z, "seq")

    first = call(
        first_grads,
        struct((16, 64, 128), BF16),
        spots(VMEM, VMEM),
        [pltpu.VMEM((9 * D // 16, 18 * POS), BF16)],
    )(packed, grad_z)
    second = call(
        second_grads,
        struct((16, 48, 128), BF16),
        spots(VMEM),
        [pltpu.VMEM((CO, 16 * POS), BF16), pltpu.VMEM((16 * POS, CO), BF16)],
    )(blocks)
    grad_first = call(summed, struct((27, C1 // 16, D // 16), F32), spots(VMEM))(
        exchange(first, "dp")
    )
    grad_second = call(summed, struct((27, C1 // 16, CO // 16), F32), spots(VMEM))(
        exchange(second, "seq")
    )
    return grad_first.transpose(0, 2, 1), grad_second


def solution(mesh):
    return jax.shard_map(
        per_device,
        mesh=mesh,
        in_specs=(
            P("dp", "seq", None, None, None),
            P(),
            P(),
            P(),
            P(),
            P("dp", None, "seq", None, None),
            P("dp", None),
        ),
        out_specs=(P(None, "seq", "dp"), P(None, "seq", "dp")),
        check_vma=False,
    )
```

time: 150 us -> 113 us (0.75)
  waiting for transfers between devices: 51.3 us -> 28.1 us
  starting transfers between devices: 56.7 us -> 43.9 us
  local copies, waits for them, and re-layouts: 9.97 us -> 7.85 us
    all_gather x0 -> x1, blocking collectives: none -> 19.2 us  [per_device(): grad_z = lax.all_gather(grad_z, 'seq')]
    all_to_all x1 -> x0, blocking collectives: 18.9 us -> none  [exchange(): return lax.all_to_all(value, axis, split_axis=0, concat_axis=0, tiled=True)]
    ppermute x8 -> x6, waiting for transfers between devices: 26.1 us -> 12.7 us  [the longest x3 12.7 us: with_cross(): return lax.ppermute(value, 'seq', swaps + [(j, i) for i, j in swaps])]
    all_to_all x6 -> x4, waiting for transfers between devices: 25.2 us -> 15.5 us  [exchange(): return lax.all_to_all(value, axis, split_axis=0, concat_axis=0, tiled=True)]
    ppermute x8 -> x6, starting transfers between devices: 19.7 us -> 10.6 us  [the longest x3 10.2 us: with_cross(): return lax.ppermute(value, 'seq', swaps + [(j, i) for i, j in swaps])]
    all_to_all x6 -> x4, starting transfers between devices: 37.1 us -> 33.3 us  [exchange(): return lax.all_to_all(value, axis, split_axis=0, concat_axis=0, tiled=True)]
    broadcast_in_dim x2 -> x0, local copies, waits for them, and re-layouts: 1.82 us -> none  [the longest x1 0.91 us: per_device(): grad_z_all = exchange(jnp.broadcast_to(grad_z[None], (16, POS, C1)), 'seq')]
    unnamed x14 -> x13, local copies, waits for them, and re-layouts: 7.1 us -> 5.82 us
  transfers between devices with their start and end apart: 14 -> 10, of which waited for: 8 -> 5; matrix products, arithmetic and copies ran while one was open for 1% -> 0% of each run, Pallas kernels for 7% -> 5%
where the time goes in v1:
time: 113 us; the launch traced here: 112 us
  starting transfers between devices  43.9 us (39%)
  waiting for transfers between devices  28.1 us (25%)
  blocking collectives  19.2 us (17%)
  Pallas kernels  12 us (11%)
  local copies, waits for them, and re-layouts  7.85 us (7%)
    all_to_all x4, starting transfers between devices, exchange(): return lax.all_to_all(value, axis, split_axis=0, concat_axis=0, tiled=True)  33.3 us
    all_gather x1, blocking collectives, per_device(): grad_z = lax.all_gather(grad_z, 'seq')  19.2 us
    all_to_all x4, waiting for transfers between devices, exchange(): return lax.all_to_all(value, axis, split_axis=0, concat_axis=0, tiled=True)  15.5 us
    ppermute x3, waiting for transfers between devices, with_cross(): return lax.ppermute(value, 'seq', swaps + [(j, i) for i, j in swaps])  12.7 us
    ppermute x3, starting transfers between devices, with_cross(): return lax.ppermute(value, 'seq', swaps + [(j, i) for i, j in swaps])  10.2 us
    unnamed x13, local copies, waits for them, and re-layouts  5.82 us
    pallas_call x1, Pallas kernels, per_device(): call(loss_and_back, (struct((16, CHUNK + 3 * POS, POS), BF16), plane, pla...  5.69 us
  transfers between devices with their start and end apart: 10, of which 5 were waited for; matrix products, arithmetic and copies ran while one was open for 0% of the time, Pallas kernels for 5%

profile of v1, /device:TPU:1, one launch (start us, length us, event | category | flops | bytes accessed | tf_op | source)
XLA Modules:
  0.0 112.0 jit_solution(6431875001632508261)
XLA Ops:
  0.6 0.9 reshape.15.tokens_ref
  1.6 1.1 reshape.14.pixel_ref
  2.7 0.0 copy-start.5
  2.7 0.9 shard_map.86
  3.6 10.1 %all-to-all-start = ((bf16[16,128,128]{2,1,0:T(8,128)(2,1)}), bf16[16,128,128]{2,1,0:T(8,128)(2,1)S(1)}, u32[]{:S(2)}, u32[]{:S(2)}) async-start(bf16[16,128,128]{2,1,0:T(8,128)(2,1)} %shard_map.86), calls=%async_computation | async-start | bytes 1048576 | tf_op jit(solution)/shard_map/all_to_all | solution.py:267
  13.7 2.0 %copy-done = bf16[27,512,128]{2,1,0:T(8,128)(2,1)S(1)} copy-done((bf16[27,512,128]{2,1,0:T(8,128)(2,1)S(1)}, bf16[27,512,128]{2,1,0:T(8,128)(2,1)}, u32[]{:S(2)}) %copy-start) | copy-done | bytes 3538968
  15.7 0.8 shard_map.87
  16.5 0.2 collective-permute-start
  16.7 3.6 %collective-permute-start.1 = (f32[128,128]{1,0:T(8,128)S(1)}, f32[128,128]{1,0:T(8,128)S(1)}, u32[]{:S(2)}, u32[]{:S(2)}) collective-permute-start(f32[128,128]{1,0:T(8,128)S(1)} %get-tuple-element.11), channel_id=1, source_target_pairs={{1,2},{3,4},{5,6},{7,8},{9,10},{11,12},{13,14},{2,1},{4,3},{6,5},{... | collective-permute-start | bytes 196616 | tf_op jit(solution)/shard_map/ppermute | solution.py:276
  20.2 0.0 collective-permute-done
  20.3 8.3 %collective-permute-done.1 = f32[128,128]{1,0:T(8,128)S(1)} collective-permute-done((f32[128,128]{1,0:T(8,128)S(1)}, f32[128,128]{1,0:T(8,128)S(1)}, u32[]{:S(2)}, u32[]{:S(2)}) %collective-permute-start.1) | collective-permute-done | bytes 65568 | tf_op jit(solution)/shard_map/ppermute | solution.py:276
  28.6 0.1 collective-permute-start.2
  28.7 3.2 %collective-permute-start.3 = (bf16[128,128]{1,0:T(8,128)(2,1)S(1)}, bf16[128,128]{1,0:T(8,128)(2,1)S(1)}, u32[]{:S(2)}, u32[]{:S(2)}) collective-permute-start(bf16[128,128]{1,0:T(8,128)(2,1)S(1)} %get-tuple-element.18.here_ref), channel_id=1, source_target_pairs={{1,2},{3,4},{5,6},{7,8},{9,10},{11,12},{13,14},{2,1},{4,3},{6,5},{... | collective-permute-start | bytes 98312 | tf_op jit(solution)/shard_map/ppermute | solution.py:276
  31.9 2.0 %collective-permute-done.3.cross_ref = bf16[128,128]{1,0:T(8,128)(2,1)S(1)} collective-permute-done((bf16[128,128]{1,0:T(8,128)(2,1)S(1)}, bf16[128,128]{1,0:T(8,128)(2,1)S(1)}, u32[]{:S(2)}, u32[]{:S(2)}) %collective-permute-start.3) | collective-permute-done | bytes 32800 | tf_op jit(solution)/shard_map/ppermute | solution.py:276
  33.9 1.7 %copy-done.1 = bf16[27,128,384]{2,1,0:T(8,128)(2,1)S(1)} copy-done((bf16[27,128,384]{2,1,0:T(8,128)(2,1)S(1)}, bf16[27,128,384]{2,1,0:T(8,128)(2,1)}, u32[]{:S(2)}) %copy-start.1) | copy-done | bytes 2654232
  35.6 5.7 %shard_map.88 = (bf16[16,480,128]{2,1,0:T(8,128)(2,1)S(1)}, f32[128,128]{1,0:T(8,128)S(1)}, f32[128,128]{1,0:T(8,128)S(1)}, f32[128,128]{1,0:T(8,128)S(1)}) custom-call(s32[1]{0:T(128)} %bitcast.place_ref, bf16[128,128]{1,0:T(8,128)(2,1)S(1)} %collective-permute-done.2.pair_ref, bf16[128,128]{1,0:T(8,128)(2,1)S(1)} %get-tuple-element.18.here_ref, ...), custom_call_target="tpu_custom_call" | custom-call | tf_op jit(solution)/shard_map/pallas_call | solution.py:298
  41.3 1.3 %copy-done.2 = bf16[16,480,128]{2,1,0:T(8,128)(2,1)} copy-done((bf16[16,480,128]{2,1,0:T(8,128)(2,1)}, bf16[16,480,128]{2,1,0:T(8,128)(2,1)S(1)}, u32[]{:S(2)}) %copy-start.2) | copy-done | bytes 1966104
  42.6 6.8 %all-to-all-start.2 = ((bf16[16,480,128]{2,1,0:T(8,128)(2,1)}), bf16[16,480,128]{2,1,0:T(8,128)(2,1)S(1)}, u32[]{:S(2)}, u32[]{:S(2)}) async-start(bf16[16,480,128]{2,1,0:T(8,128)(2,1)} %copy-done.2), calls=%async_computation.2 | async-start | bytes 3932160 | tf_op jit(solution)/shard_map/all_to_all | solution.py:267
  49.4 0.1 collective-permute-start.4
  49.5 3.5 %collective-permute-start.5 = (f32[128,128]{1,0:T(8,128)S(1)}, f32[128,128]{1,0:T(8,128)S(1)}, u32[]{:S(2)}, u32[]{:S(2)}) collective-permute-start(f32[128,128]{1,0:T(8,128)S(1)} %get-tuple-element.14), channel_id=1, source_target_pairs={{1,2},{3,4},{5,6},{7,8},{9,10},{11,12},{13,14},{2,1},{4,3},{6,5},{... | collective-permute-start | bytes 196616 | tf_op jit(solution)/shard_map/ppermute | solution.py:276
  53.0 2.4 %collective-permute-done.5 = f32[128,128]{1,0:T(8,128)S(1)} collective-permute-done((f32[128,128]{1,0:T(8,128)S(1)}, f32[128,128]{1,0:T(8,128)S(1)}, u32[]{:S(2)}, u32[]{:S(2)}) %collective-permute-start.5) | collective-permute-done | bytes 65568 | tf_op jit(solution)/shard_map/ppermute | solution.py:276
  55.4 0.1 fusion.6
  55.4 19.2 %all-gather = bf16[2048,128]{1,0:T(8,128)(2,1)S(1)} all-gather(bf16[128,128]{1,0:T(8,128)(2,1)S(1)} %fusion.6), channel_id=2, replica_groups=mesh['dp'=16,'seq'=16] {'seq'}, dimensions={0}, use_global_device_ids=true | all-gather | bytes 557056 | tf_op jit(solution)/shard_map/all_gather | solution.py:315
  74.6 1.9 %shard_map.89 = bf16[16,64,128]{2,1,0:T(8,128)(2,1)} custom-call(bf16[16,128,128]{2,1,0:T(8,128)(2,1)S(1)} %all-to-all-done.packed_ref, bf16[16,128,128]{2,1,0:T(8,128)(2,1)S(1)} %bitcast.3), custom_call_target="tpu_custom_call" | custom-call | tf_op jit(solution)/shard_map/pallas_call | solution.py:317
  76.5 6.6 %all-to-all-start.1 = ((bf16[16,64,128]{2,1,0:T(8,128)(2,1)}), bf16[16,64,128]{2,1,0:T(8,128)(2,1)S(1)}, u32[]{:S(2)}, u32[]{:S(2)}) async-start(bf16[16,64,128]{2,1,0:T(8,128)(2,1)} %shard_map.89), calls=%async_computation.1 | async-start | bytes 524288 | tf_op jit(solution)/shard_map/all_to_all | solution.py:267
  83.1 1.9 %shard_map.91 = bf16[16,48,128]{2,1,0:T(8,128)(2,1)} custom-call(bf16[16,480,128]{2,1,0:T(8,128)(2,1)S(1)} %all-to-all-done.2.blocks_ref), custom_call_target="tpu_custom_call" | custom-call | tf_op jit(solution)/shard_map/pallas_call | solution.py:323
  85.0 5.9 %all-to-all-done.1.parts_ref = bf16[16,64,128]{2,1,0:T(8,128)(2,1)S(1)} async-done(((bf16[16,64,128]{2,1,0:T(8,128)(2,1)}), bf16[16,64,128]{2,1,0:T(8,128)(2,1)S(1)}, u32[]{:S(2)}, u32[]{:S(2)}) %all-to-all-start.1) | async-done | bytes 262176 | tf_op jit(solution)/shard_map/all_to_all | solution.py:267
  90.9 9.9 %all-to-all-start.3 = ((bf16[16,48,128]{2,1,0:T(8,128)(2,1)}), bf16[16,48,128]{2,1,0:T(8,128)(2,1)S(1)}, u32[]{:S(2)}, u32[]{:S(2)}) async-start(bf16[16,48,128]{2,1,0:T(8,128)(2,1)} %shard_map.91), calls=%async_computation.3 | async-start | bytes 393216 | tf_op jit(solution)/shard_map/all_to_all | solution.py:267
  100.8 0.8 shard_map.90
  101.5 9.6 %all-to-all-done.3.parts_ref = bf16[16,48,128]{2,1,0:T(8,128)(2,1)S(1)} async-done(((bf16[16,48,128]{2,1,0:T(8,128)(2,1)}), bf16[16,48,128]{2,1,0:T(8,128)(2,1)S(1)}, u32[]{:S(2)}, u32[]{:S(2)}) %all-to-all-start.3) | async-done | bytes 196640 | tf_op jit(solution)/shard_map/all_to_all | solution.py:267
  111.1 0.1 shard_map.92
  111.2 0.8 copy.9
  (14 shorter events, 0.1 us)
Async XLA Ops:
  2.7 25.8 %copy-start.5 = (f32[128]{0:T(128)S(1)}, f32[128]{0:T(128)}, u32[]{:S(2)}) copy-start(f32[128]{0:T(128)} %param.9) | copy-start | bytes 1540
  3.6 28.3 %copy-start.4 = (f32[384]{0:T(512)S(1)}, f32[384]{0:T(512)}, u32[]{:S(2)}) copy-start(f32[384]{0:T(512)} %param.11) | copy-start | bytes 4612
  3.6 30.3 %copy-start.3 = (s32[1,115]{1,0:T(1,128)S(1)}, s32[1,115]{1,0:T(1,128)}, u32[]{:S(2)}) copy-start(s32[1,115]{1,0:T(1,128)} %index_ref.1) | copy-start | bytes 1384
  3.6 30.3 %all-to-all-start = ((bf16[16,128,128]{2,1,0:T(8,128)(2,1)}), bf16[16,128,128]{2,1,0:T(8,128)(2,1)S(1)}, u32[]{:S(2)}, u32[]{:S(2)}) async-start(bf16[16,128,128]{2,1,0:T(8,128)(2,1)} %shard_map.86), calls=%async_computation | async-start | bytes 1048576 | tf_op jit(solution)/shard_map/all_to_all | solution.py:267
  13.7 2.0 %copy-start = (bf16[27,512,128]{2,1,0:T(8,128)(2,1)S(1)}, bf16[27,512,128]{2,1,0:T(8,128)(2,1)}, u32[]{:S(2)}) copy-start(bf16[27,512,128]{2,1,0:T(8,128)(2,1)} %weight_ref.2) | copy-start | bytes 10616836
  16.5 3.8 %collective-permute-start = (f32[128,128]{1,0:T(8,128)S(1)}, f32[128,128]{1,0:T(8,128)S(1)}, u32[]{:S(2)}, u32[]{:S(2)}) collective-permute-start(f32[128,128]{1,0:T(8,128)S(1)} %get-tuple-element.9), channel_id=1, source_target_pairs={{0,1},{1,0},{2,3},{3,2},{4,5},{5,4},{6,7},{7,6},{8,9},{9,8},{10,11... | collective-permute-start | bytes 196616 | tf_op jit(solution)/shard_map/ppermute | solution.py:271
  16.7 11.8 %collective-permute-start.1 = (f32[128,128]{1,0:T(8,128)S(1)}, f32[128,128]{1,0:T(8,128)S(1)}, u32[]{:S(2)}, u32[]{:S(2)}) collective-permute-start(f32[128,128]{1,0:T(8,128)S(1)} %get-tuple-element.11), channel_id=1, source_target_pairs={{1,2},{3,4},{5,6},{7,8},{9,10},{11,12},{13,14},{2,1},{4,3},{6,5},{... | collective-permute-start | bytes 196616 | tf_op jit(solution)/shard_map/ppermute | solution.py:276
  28.6 3.3 %collective-permute-start.2 = (bf16[128,128]{1,0:T(8,128)(2,1)S(1)}, bf16[128,128]{1,0:T(8,128)(2,1)S(1)}, u32[]{:S(2)}, u32[]{:S(2)}) collective-permute-start(bf16[128,128]{1,0:T(8,128)(2,1)S(1)} %get-tuple-element.18.here_ref), channel_id=1, source_target_pairs={{0,1},{1,0},{2,3},{3,2},{4,5},{5,4},{6,7},{7,6},{8,9},{9,8},{10,11... | collective-permute-start | bytes 98312 | tf_op jit(solution)/shard_map/ppermute | solution.py:271
  28.7 5.2 %collective-permute-start.3 = (bf16[128,128]{1,0:T(8,128)(2,1)S(1)}, bf16[128,128]{1,0:T(8,128)(2,1)S(1)}, u32[]{:S(2)}, u32[]{:S(2)}) collective-permute-start(bf16[128,128]{1,0:T(8,128)(2,1)S(1)} %get-tuple-element.18.here_ref), channel_id=1, source_target_pairs={{1,2},{3,4},{5,6},{7,8},{9,10},{11,12},{13,14},{2,1},{4,3},{6,5},{... | collective-permute-start | bytes 98312 | tf_op jit(solution)/shard_map/ppermute | solution.py:276
  33.9 1.8 %copy-start.1 = (bf16[27,128,384]{2,1,0:T(8,128)(2,1)S(1)}, bf16[27,128,384]{2,1,0:T(8,128)(2,1)}, u32[]{:S(2)}) copy-start(bf16[27,128,384]{2,1,0:T(8,128)(2,1)} %weight_ref.3) | copy-start | bytes 7962628
  41.3 1.3 %copy-start.2 = (bf16[16,480,128]{2,1,0:T(8,128)(2,1)}, bf16[16,480,128]{2,1,0:T(8,128)(2,1)S(1)}, u32[]{:S(2)}) copy-start(bf16[16,480,128]{2,1,0:T(8,128)(2,1)S(1)} %get-tuple-element.15) | copy-start | bytes 5898244
  42.6 33.9 %all-to-all-start.2 = ((bf16[16,480,128]{2,1,0:T(8,128)(2,1)}), bf16[16,480,128]{2,1,0:T(8,128)(2,1)S(1)}, u32[]{:S(2)}, u32[]{:S(2)}) async-start(bf16[16,480,128]{2,1,0:T(8,128)(2,1)} %copy-done.2), calls=%async_computation.2 | async-start | bytes 3932160 | tf_op jit(solution)/shard_map/all_to_all | solution.py:267
  49.4 3.6 %collective-permute-start.4 = (f32[128,128]{1,0:T(8,128)S(1)}, f32[128,128]{1,0:T(8,128)S(1)}, u32[]{:S(2)}, u32[]{:S(2)}) collective-permute-start(f32[128,128]{1,0:T(8,128)S(1)} %get-tuple-element.12), channel_id=1, source_target_pairs={{0,1},{1,0},{2,3},{3,2},{4,5},{5,4},{6,7},{7,6},{8,9},{9,8},{10,11... | collective-permute-start | bytes 196616 | tf_op jit(solution)/shard_map/ppermute | solution.py:271
  49.5 5.9 %collective-permute-start.5 = (f32[128,128]{1,0:T(8,128)S(1)}, f32[128,128]{1,0:T(8,128)S(1)}, u32[]{:S(2)}, u32[]{:S(2)}) collective-permute-start(f32[128,128]{1,0:T(8,128)S(1)} %get-tuple-element.14), channel_id=1, source_target_pairs={{1,2},{3,4},{5,6},{7,8},{9,10},{11,12},{13,14},{2,1},{4,3},{6,5},{... | collective-permute-start | bytes 196616 | tf_op jit(solution)/shard_map/ppermute | solution.py:276
  76.5 14.4 %all-to-all-start.1 = ((bf16[16,64,128]{2,1,0:T(8,128)(2,1)}), bf16[16,64,128]{2,1,0:T(8,128)(2,1)S(1)}, u32[]{:S(2)}, u32[]{:S(2)}) async-start(bf16[16,64,128]{2,1,0:T(8,128)(2,1)} %shard_map.89), calls=%async_computation.1 | async-start | bytes 524288 | tf_op jit(solution)/shard_map/all_to_all | solution.py:267
  90.9 20.2 %all-to-all-start.3 = ((bf16[16,48,128]{2,1,0:T(8,128)(2,1)}), bf16[16,48,128]{2,1,0:T(8,128)(2,1)S(1)}, u32[]{:S(2)}, u32[]{:S(2)}) async-start(bf16[16,48,128]{2,1,0:T(8,128)(2,1)} %shard_map.91), calls=%async_computation.3 | async-start | bytes 393216 | tf_op jit(solution)/shard_map/all_to_all | solution.py:267

commit v2 on v1

--- a/solution.py
+++ b/solution.py
@@ -12,6 +12,7 @@
 POS, COLS, PAD = 128, 4, 8
 D, C1, CO = 512, 128, 384
 CHUNK = 4 * CO // 16
+FLOPS = 40_000_000_000
 TAPS9 = [(row, col) for row in range(3) for col in range(3)]
 PHASES = [(i, j) for i in range(2) for j in range(2)]
 PAIRS = [(-1, 1), (0, 0), (0, 1), (1, 0)]
@@ -34,11 +35,12 @@
     return (column >= 0) & (column < COLS) & (row >= 0) & (row < POS // COLS)
 
 
-def call(body, out_shape, in_specs, scratch=(), flops=0, size=0, limit=16):
+def call(body, out_shape, in_specs, scratch=(), flops=0, size=0, limit=16, **options):
     return pl.pallas_call(
         body,
         out_shape=out_shape,
         in_specs=in_specs,
+        **options,
         scratch_shapes=list(scratch),
         compiler_params=pltpu.CompilerParams(vmem_limit_bytes=limit << 20),
         cost_estimate=pl.CostEstimate(flops=flops, bytes_accessed=size, transcendentals=0),
@@ -144,7 +146,6 @@
         blocks_ref[block, 0:CHUNK] = jnp.concatenate(
             [part[block * width : (block + 1) * width] for part in turned], axis=0
         ).astype(BF16)
-
     cot = cots[...]
     sums = {}
     for row, col in TAPS9:
@@ -173,7 +174,20 @@
     to_cross_ref[...] = jnp.where(even, to_last, to_next)
 
 
-def second_grads(blocks_ref, out_ref, left, right):
+def halved(pairs, bit, keep_ref, send_ref):
+    for at, (zero, one) in enumerate(pairs):
+        keep_ref[at] = jnp.where(bit == 0, zero, one)
+        send_ref[at] = jnp.where(bit == 0, one, zero)
+
+
+def hidden_grads(pair_ref, keep_ref, cross_ref, zsum_ref, out_ref):
+    grad = pair_ref[...] + keep_ref[...] + cross_ref[...]
+    gelu_tanh = partial(jax.nn.gelu, approximate=True)
+    out_ref[...] = jax.vjp(gelu_tanh, zsum_ref[...])[1](grad)[0].astype(BF16)
+
+
+def second_grads(place_ref, blocks_ref, after_ref, keep_ref, send_ref, left, right):
+    del after_ref
     wide, thin = CO // 16, C1 // 16
     masks = {}
     for row in (-1, 0, 1):
@@ -211,11 +225,23 @@
                 parts.append(value)
     parts.append(jnp.zeros((6 * 128 - 27 * wide, C1), F32))
     turned = jnp.concatenate(parts, axis=0).T
-    for block in range(16):
-        two = turned[block * thin : (block + 1) * thin]
-        out_ref[block] = jnp.concatenate(
-            [two[:, 128 * n : 128 * (n + 1)] for n in range(6)], axis=0
-        ).astype(out_ref.dtype)
+    blocks = [turned[block * thin : (block + 1) * thin] for block in range(16)]
+    halved(zip(blocks[0::2], blocks[1::2]), place_ref[0], keep_ref, send_ref)
+
+
+def half_sum(level, place_ref, kept_ref, came_ref, keep_ref, send_ref):
+    pairs = [
+        tuple(kept_ref[at] + came_ref[at] for at in (two, two + 1))
+        for two in range(0, kept_ref.shape[0], 2)
+    ]
+    halved(pairs, place_ref[level], keep_ref, send_ref)
+
+
+def last_sum(kept_ref, came_ref, out_ref):
+    total = kept_ref[0] + came_ref[0]
+    width = out_ref.shape[2]
+    for k in range(27):
+        out_ref[k] = total[:, k * width : (k + 1) * width]
 
 
 def first_grads(packed_ref, gz_ref, out_ref, moved):
@@ -267,8 +293,12 @@
     return lax.all_to_all(value, axis, split_axis=0, concat_axis=0, tiled=True)
 
 
+def swapped(value, step):
+    return lax.ppermute(value, "seq", [(i, i ^ step) for i in range(16)])
+
+
 def with_pair(value):
-    return lax.ppermute(value, "seq", [(i, i ^ 1) for i in range(16)])
+    return swapped(value, 1)
 
 
 def with_cross(value):
@@ -278,7 +308,7 @@
 
 def per_device(tokens, conv_first, bias_first, conv_second, bias_second, pixels, mask_index):
     gelu_tanh = partial(jax.nn.gelu, approximate=True)
-    place = (lax.axis_index("seq") % 2).reshape(1).astype(jnp.int32)
+    place = (lax.axis_index("seq") // jnp.array([1, 2, 4, 8])) % 2
     field = tokens.reshape(POS, D)
     packed = call(
         packed_inputs, struct((16, CHUNK + D // 16, POS), BF16), spots(VMEM, VMEM)
@@ -310,8 +340,9 @@
         packed, mask_index,
     )
     blocks = exchange(blocks, "dp")
-    grad_hidden = with_pair(pair) + keep + with_cross(cross)
-    grad_z = jax.vjp(gelu_tanh, zsum)[1](grad_hidden)[0].astype(BF16)
+    grad_z = call(hidden_grads, struct((POS, C1), BF16), spots(*[VMEM] * 4), flops=FLOPS)(
+        with_pair(pair), keep, with_cross(cross), zsum
+    )
     grad_z = lax.all_gather(grad_z, "seq")
 
     first = call(
@@ -320,17 +351,24 @@
         spots(VMEM, VMEM),
         [pltpu.VMEM((9 * D // 16, 18 * POS), BF16)],
     )(packed, grad_z)
-    second = call(
+    half = struct((8, C1 // 16, 6 * 128), F32)
+    keep, send = call(
         second_grads,
-        struct((16, 48, 128), BF16),
-        spots(VMEM),
+        (half, half),
+        spots(SMEM, VMEM, pl.ANY),
         [pltpu.VMEM((CO, 16 * POS), BF16), pltpu.VMEM((16 * POS, CO), BF16)],
-    )(blocks)
+    )(place, blocks, grad_z)
+    for level in (1, 2, 3):
+        half = struct((8 >> level, C1 // 16, 6 * 128), F32)
+        came = swapped(send, 1 << (level - 1))
+        keep, send = call(
+            partial(half_sum, level), (half, half), spots(SMEM, VMEM, VMEM)
+        )(place, keep, came)
+    grad_second = call(last_sum, struct((27, C1 // 16, CO // 16), F32), spots(VMEM, VMEM))(
+        keep, swapped(send, 8)
+    )
     grad_first = call(summed, struct((27, C1 // 16, D // 16), F32), spots(VMEM))(
         exchange(first, "dp")
-    )
-    grad_second = call(summed, struct((27, C1 // 16, CO // 16), F32), spots(VMEM))(
-        exchange(second, "seq")
     )
     return grad_first.transpose(0, 2, 1), grad_second
 

time: 113 us -> 113 us (level)
  the two profiles are of different devices: /device:TPU:1 before, /device:TPU:32 now
where the time goes in v2:
time: 113 us; the launch traced here: 112 us
  starting transfers between devices  38.2 us (34%)
  waiting for transfers between devices  31.6 us (28%)
  blocking collectives  18.8 us (17%)
  Pallas kernels  14.7 us (13%)
  local copies, waits for them, and re-layouts  7.85 us (7%)
    all_to_all x3, starting transfers between devices, exchange(): return lax.all_to_all(value, axis, split_axis=0, concat_axis=0, tiled=True)  20.6 us
    all_gather x1, blocking collectives, per_device(): grad_z = lax.all_gather(grad_z, 'seq')  18.8 us
    ppermute x7, waiting for transfers between devices, swapped(): return lax.ppermute(value, 'seq', [(i, i ^ step) for i in range(16)])  13 us
    ppermute x7, starting transfers between devices, swapped(): return lax.ppermute(value, 'seq', [(i, i ^ step) for i in range(16)])  11 us
    all_to_all x3, waiting for transfers between devices, exchange(): return lax.all_to_all(value, axis, split_axis=0, concat_axis=0, tiled=True)  10 us
    ppermute x3, waiting for transfers between devices, with_cross(): return lax.ppermute(value, 'seq', swaps + [(j, i) for i, j in swaps])  8.51 us
    ppermute x3, starting transfers between devices, with_cross(): return lax.ppermute(value, 'seq', swaps + [(j, i) for i, j in swaps])  6.63 us
    pallas_call x1, Pallas kernels, per_device(): call(loss_and_back, (struct((16, CHUNK + 3 * POS, POS), BF16), plane, pla...  6.24 us
  transfers between devices with their start and end apart: 13, of which 6 were waited for; matrix products, arithmetic and copies ran while one was open for 0% of the time, Pallas kernels for 5%

profile of v2, /device:TPU:32, one launch (start us, length us, event | category | flops | bytes accessed | tf_op | source)
XLA Modules:
  0.0 112.2 jit_solution(9656718650815074193)
XLA Ops:
  0.6 1.1 reshape.11.pixel_ref
  1.7 0.9 reshape.12.tokens_ref
  2.7 0.9 shard_map.95
  3.6 8.7 %all-to-all-start = ((bf16[16,128,128]{2,1,0:T(8,128)(2,1)}), bf16[16,128,128]{2,1,0:T(8,128)(2,1)S(1)}, u32[]{:S(2)}, u32[]{:S(2)}) async-start(bf16[16,128,128]{2,1,0:T(8,128)(2,1)} %shard_map.95), calls=%async_computation | async-start | bytes 1048576 | tf_op jit(solution)/shard_map/all_to_all | solution.py:293
  12.5 2.0 %copy-done = bf16[27,512,128]{2,1,0:T(8,128)(2,1)S(1)} copy-done((bf16[27,512,128]{2,1,0:T(8,128)(2,1)S(1)}, bf16[27,512,128]{2,1,0:T(8,128)(2,1)}, u32[]{:S(2)}) %copy-start) | copy-done | bytes 3538968
  14.5 1.3 %shard_map.96 = (f32[128,128]{1,0:T(8,128)S(1)}, f32[128,128]{1,0:T(8,128)S(1)}, f32[128,128]{1,0:T(8,128)S(1)}) custom-call(s32[4]{0:T(128)S(1)} %and_select_fusion.place_ref, bf16[128,512]{1,0:T(8,128)(2,1)S(1)} %reshape.12.tokens_ref, bf16[27,512,128]{2,1,0:T(8,128)(2,1)S(1)} %copy-done), custom_call_target="tpu_custom_call" | custom-call | tf_op jit(solution)/shard_map/pallas_call | solution.py:319
  15.8 2.0 %collective-permute-start.1 = (f32[128,128]{1,0:T(8,128)S(1)}, f32[128,128]{1,0:T(8,128)S(1)}, u32[]{:S(2)}, u32[]{:S(2)}) collective-permute-start(f32[128,128]{1,0:T(8,128)S(1)} %get-tuple-element.19), channel_id=1, source_target_pairs={{1,2},{3,4},{5,6},{7,8},{9,10},{11,12},{13,14},{2,1},{4,3},{6,5},{... | collective-permute-start | bytes 196616 | tf_op jit(solution)/shard_map/ppermute | solution.py:306
  17.8 1.6 %collective-permute-start = (f32[128,128]{1,0:T(8,128)S(1)}, f32[128,128]{1,0:T(8,128)S(1)}, u32[]{:S(2)}, u32[]{:S(2)}) collective-permute-start(f32[128,128]{1,0:T(8,128)S(1)} %get-tuple-element.17), channel_id=1, source_target_pairs={{0,1},{1,0},{2,3},{3,2},{4,5},{5,4},{6,7},{7,6},{8,9},{9,8},{10,11... | collective-permute-start | bytes 196616 | tf_op jit(solution)/shard_map/ppermute | solution.py:297
  19.4 5.7 %collective-permute-done.1 = f32[128,128]{1,0:T(8,128)S(1)} collective-permute-done((f32[128,128]{1,0:T(8,128)S(1)}, f32[128,128]{1,0:T(8,128)S(1)}, u32[]{:S(2)}, u32[]{:S(2)}) %collective-permute-start.1) | collective-permute-done | bytes 65568 | tf_op jit(solution)/shard_map/ppermute | solution.py:306
  25.1 1.8 %collective-permute-start.2 = (bf16[128,128]{1,0:T(8,128)(2,1)S(1)}, bf16[128,128]{1,0:T(8,128)(2,1)S(1)}, u32[]{:S(2)}, u32[]{:S(2)}) collective-permute-start(bf16[128,128]{1,0:T(8,128)(2,1)S(1)} %get-tuple-element.34.here_ref), channel_id=1, source_target_pairs={{0,1},{1,0},{2,3},{3,2},{4,5},{5,4},{6,7},{7,6},{8,9},{9,8},{10,11... | collective-permute-start | bytes 98312 | tf_op jit(solution)/shard_map/ppermute | solution.py:297
  26.9 2.4 %collective-permute-start.3 = (bf16[128,128]{1,0:T(8,128)(2,1)S(1)}, bf16[128,128]{1,0:T(8,128)(2,1)S(1)}, u32[]{:S(2)}, u32[]{:S(2)}) collective-permute-start(bf16[128,128]{1,0:T(8,128)(2,1)S(1)} %get-tuple-element.34.here_ref), channel_id=1, source_target_pairs={{1,2},{3,4},{5,6},{7,8},{9,10},{11,12},{13,14},{2,1},{4,3},{6,5},{... | collective-permute-start | bytes 98312 | tf_op jit(solution)/shard_map/ppermute | solution.py:306
  29.3 2.8 %collective-permute-done.3.cross_ref = bf16[128,128]{1,0:T(8,128)(2,1)S(1)} collective-permute-done((bf16[128,128]{1,0:T(8,128)(2,1)S(1)}, bf16[128,128]{1,0:T(8,128)(2,1)S(1)}, u32[]{:S(2)}, u32[]{:S(2)}) %collective-permute-start.3) | collective-permute-done | bytes 32800 | tf_op jit(solution)/shard_map/ppermute | solution.py:306
  32.2 1.7 %copy-done.1 = bf16[27,128,384]{2,1,0:T(8,128)(2,1)S(1)} copy-done((bf16[27,128,384]{2,1,0:T(8,128)(2,1)S(1)}, bf16[27,128,384]{2,1,0:T(8,128)(2,1)}, u32[]{:S(2)}) %copy-start.1) | copy-done | bytes 2654232
  33.9 6.2 %shard_map.97 = (bf16[16,480,128]{2,1,0:T(8,128)(2,1)S(1)}, f32[128,128]{1,0:T(8,128)S(1)}, f32[128,128]{1,0:T(8,128)S(1)}, f32[128,128]{1,0:T(8,128)S(1)}) custom-call(s32[4]{0:T(128)S(1)} %and_select_fusion.place_ref, bf16[128,128]{1,0:T(8,128)(2,1)S(1)} %collective-permute-done.2.pair_ref, bf16[128,128]{1,0:T(8,128)(2,1)S(1)} %get-tuple-element.34.here_ref, ...), custom_call_target="tpu_custom_call" | custom-call | tf_op jit(solution)/shard_map/pallas_call | solution.py:328
  40.2 1.3 %copy-done.2 = bf16[16,480,128]{2,1,0:T(8,128)(2,1)} copy-done((bf16[16,480,128]{2,1,0:T(8,128)(2,1)}, bf16[16,480,128]{2,1,0:T(8,128)(2,1)S(1)}, u32[]{:S(2)}) %copy-start.2) | copy-done | bytes 1966104
  41.6 2.2 %collective-permute-start.5 = (f32[128,128]{1,0:T(8,128)S(1)}, f32[128,128]{1,0:T(8,128)S(1)}, u32[]{:S(2)}, u32[]{:S(2)}) collective-permute-start(f32[128,128]{1,0:T(8,128)S(1)} %get-tuple-element.22), channel_id=1, source_target_pairs={{1,2},{3,4},{5,6},{7,8},{9,10},{11,12},{13,14},{2,1},{4,3},{6,5},{... | collective-permute-start | bytes 196616 | tf_op jit(solution)/shard_map/ppermute | solution.py:306
  43.8 7.1 %all-to-all-start.2 = ((bf16[16,480,128]{2,1,0:T(8,128)(2,1)}), bf16[16,480,128]{2,1,0:T(8,128)(2,1)S(1)}, u32[]{:S(2)}, u32[]{:S(2)}) async-start(bf16[16,480,128]{2,1,0:T(8,128)(2,1)} %copy-done.2), calls=%async_computation.2 | async-start | bytes 3932160 | tf_op jit(solution)/shard_map/all_to_all | solution.py:293
  51.0 18.8 %all-gather = bf16[2048,128]{1,0:T(8,128)(2,1)S(1)} all-gather(bf16[128,128]{1,0:T(8,128)(2,1)S(1)} %shard_map.98), channel_id=2, replica_groups=mesh['dp'=16,'seq'=16] {'seq'}, dimensions={0}, use_global_device_ids=true | all-gather | bytes 557056 | tf_op jit(solution)/shard_map/all_gather | solution.py:346
  69.8 10.0 %all-to-all-done.2.blocks_ref = bf16[16,480,128]{2,1,0:T(8,128)(2,1)S(1)} async-done(((bf16[16,480,128]{2,1,0:T(8,128)(2,1)}), bf16[16,480,128]{2,1,0:T(8,128)(2,1)S(1)}, u32[]{:S(2)}, u32[]{:S(2)}) %all-to-all-start.2) | async-done | bytes 1966112 | tf_op jit(solution)/shard_map/all_to_all | solution.py:293
  79.8 1.8 %shard_map.101 = (f32[8,8,768]{2,1,0:T(8,128)S(1)}, f32[8,8,768]{2,1,0:T(8,128)S(1)}) custom-call(s32[4]{0:T(128)S(1)} %and_select_fusion.place_ref, bf16[16,480,128]{2,1,0:T(8,128)(2,1)S(1)} %all-to-all-done.2.blocks_ref, bf16[16,128,128]{2,1,0:T(8,128)(2,1)S(1)} %bitcast.2), custom_call_target="tpu_custom_call" | custom-call | tf_op jit(solution)/shard_map/pallas_call | solution.py:355
  81.6 1.2 %collective-permute-start.6 = (f32[8,8,768]{2,1,0:T(8,128)S(1)}, f32[8,8,768]{2,1,0:T(8,128)S(1)}, u32[]{:S(2)}, u32[]{:S(2)}) collective-permute-start(f32[8,8,768]{2,1,0:T(8,128)S(1)} %get-tuple-element.25), channel_id=1, source_target_pairs={{0,1},{1,0},{2,3},{3,2},{4,5},{5,4},{6,7},{7,6},{8,9},{9,8},{10,11... | collective-permute-start | bytes 589832 | tf_op jit(solution)/shard_map/ppermute | solution.py:297
  82.7 1.9 %shard_map.99 = bf16[16,64,128]{2,1,0:T(8,128)(2,1)} custom-call(bf16[16,128,128]{2,1,0:T(8,128)(2,1)S(1)} %all-to-all-done.packed_ref, bf16[16,128,128]{2,1,0:T(8,128)(2,1)S(1)} %bitcast.3), custom_call_target="tpu_custom_call" | custom-call | tf_op jit(solution)/shard_map/pallas_call | solution.py:348
  84.7 4.8 %all-to-all-start.1 = ((bf16[16,64,128]{2,1,0:T(8,128)(2,1)}), bf16[16,64,128]{2,1,0:T(8,128)(2,1)S(1)}, u32[]{:S(2)}, u32[]{:S(2)}) async-start(bf16[16,64,128]{2,1,0:T(8,128)(2,1)} %shard_map.99), calls=%async_computation.1 | async-start | bytes 524288 | tf_op jit(solution)/shard_map/all_to_all | solution.py:293
  89.5 0.6 shard_map.102
  90.1 4.6 %collective-permute-done.7.came_ref = f32[4,8,768]{2,1,0:T(8,128)S(1)} collective-permute-done((f32[4,8,768]{2,1,0:T(8,128)S(1)}, f32[4,8,768]{2,1,0:T(8,128)S(1)}, u32[]{:S(2)}, u32[]{:S(2)}) %collective-permute-start.7) | collective-permute-done | bytes 98336 | tf_op jit(solution)/shard_map/ppermute | solution.py:297
  94.7 0.6 shard_map.103
  95.3 5.4 %collective-permute-start.8 = (f32[2,8,768]{2,1,0:T(8,128)S(1)}, f32[2,8,768]{2,1,0:T(8,128)S(1)}, u32[]{:S(2)}, u32[]{:S(2)}) collective-permute-start(f32[2,8,768]{2,1,0:T(8,128)S(1)} %get-tuple-element.29), channel_id=1, source_target_pairs={{0,4},{1,5},{2,6},{3,7},{4,0},{5,1},{6,2},{7,3},{8,12},{9,13},{10,... | collective-permute-start | bytes 147464 | tf_op jit(solution)/shard_map/ppermute | solution.py:297
  100.7 2.1 %collective-permute-done.8.came_ref = f32[2,8,768]{2,1,0:T(8,128)S(1)} collective-permute-done((f32[2,8,768]{2,1,0:T(8,128)S(1)}, f32[2,8,768]{2,1,0:T(8,128)S(1)}, u32[]{:S(2)}, u32[]{:S(2)}) %collective-permute-start.8) | collective-permute-done | bytes 49184 | tf_op jit(solution)/shard_map/ppermute | solution.py:297
  103.3 0.9 collective-permute-start.9
  104.2 0.8 shard_map.100
  105.0 6.4 %collective-permute-done.9.came_ref = f32[1,8,768]{2,1,0:T(8,128)S(1)} collective-permute-done((f32[1,8,768]{2,1,0:T(8,128)S(1)}, f32[1,8,768]{2,1,0:T(8,128)S(1)}, u32[]{:S(2)}, u32[]{:S(2)}) %collective-permute-start.9) | collective-permute-done | bytes 24608 | tf_op jit(solution)/shard_map/ppermute | solution.py:297
  111.4 0.8 copy.10
  (26 shorter events, 1.1 us)
Async XLA Ops:
  0.6 11.7 %copy-start.6 = (s32[4]{0:T(128)S(1)}, s32[4]{0:T(128)}, u32[]{:S(2)}) copy-start(s32[4]{0:T(128)} %constant.35.clone) | copy-start | bytes 52
  2.7 22.4 %copy-start.5 = (f32[128]{0:T(128)S(1)}, f32[128]{0:T(128)}, u32[]{:S(2)}) copy-start(f32[128]{0:T(128)} %param.10) | copy-start | bytes 1540
  3.6 25.7 %copy-start.4 = (f32[384]{0:T(512)S(1)}, f32[384]{0:T(512)}, u32[]{:S(2)}) copy-start(f32[384]{0:T(512)} %param.12) | copy-start | bytes 4612
  3.6 28.6 %copy-start.3 = (s32[1,115]{1,0:T(1,128)S(1)}, s32[1,115]{1,0:T(1,128)}, u32[]{:S(2)}) copy-start(s32[1,115]{1,0:T(1,128)} %index_ref.1) | copy-start | bytes 1384
  3.6 28.6 %all-to-all-start = ((bf16[16,128,128]{2,1,0:T(8,128)(2,1)}), bf16[16,128,128]{2,1,0:T(8,128)(2,1)S(1)}, u32[]{:S(2)}, u32[]{:S(2)}) async-start(bf16[16,128,128]{2,1,0:T(8,128)(2,1)} %shard_map.95), calls=%async_computation | async-start | bytes 1048576 | tf_op jit(solution)/shard_map/all_to_all | solution.py:293
  12.5 2.0 %copy-start = (bf16[27,512,128]{2,1,0:T(8,128)(2,1)S(1)}, bf16[27,512,128]{2,1,0:T(8,128)(2,1)}, u32[]{:S(2)}) copy-start(bf16[27,512,128]{2,1,0:T(8,128)(2,1)} %weight_ref.2) | copy-start | bytes 10616836
  15.8 9.3 %collective-permute-start.1 = (f32[128,128]{1,0:T(8,128)S(1)}, f32[128,128]{1,0:T(8,128)S(1)}, u32[]{:S(2)}, u32[]{:S(2)}) collective-permute-start(f32[128,128]{1,0:T(8,128)S(1)} %get-tuple-element.19), channel_id=1, source_target_pairs={{1,2},{3,4},{5,6},{7,8},{9,10},{11,12},{13,14},{2,1},{4,3},{6,5},{... | collective-permute-start | bytes 196616 | tf_op jit(solution)/shard_map/ppermute | solution.py:306
  17.8 7.2 %collective-permute-start = (f32[128,128]{1,0:T(8,128)S(1)}, f32[128,128]{1,0:T(8,128)S(1)}, u32[]{:S(2)}, u32[]{:S(2)}) collective-permute-start(f32[128,128]{1,0:T(8,128)S(1)} %get-tuple-element.17), channel_id=1, source_target_pairs={{0,1},{1,0},{2,3},{3,2},{4,5},{5,4},{6,7},{7,6},{8,9},{9,8},{10,11... | collective-permute-start | bytes 196616 | tf_op jit(solution)/shard_map/ppermute | solution.py:297
  25.1 4.2 %collective-permute-start.2 = (bf16[128,128]{1,0:T(8,128)(2,1)S(1)}, bf16[128,128]{1,0:T(8,128)(2,1)S(1)}, u32[]{:S(2)}, u32[]{:S(2)}) collective-permute-start(bf16[128,128]{1,0:T(8,128)(2,1)S(1)} %get-tuple-element.34.here_ref), channel_id=1, source_target_pairs={{0,1},{1,0},{2,3},{3,2},{4,5},{5,4},{6,7},{7,6},{8,9},{9,8},{10,11... | collective-permute-start | bytes 98312 | tf_op jit(solution)/shard_map/ppermute | solution.py:297
  26.9 5.2 %collective-permute-start.3 = (bf16[128,128]{1,0:T(8,128)(2,1)S(1)}, bf16[128,128]{1,0:T(8,128)(2,1)S(1)}, u32[]{:S(2)}, u32[]{:S(2)}) collective-permute-start(bf16[128,128]{1,0:T(8,128)(2,1)S(1)} %get-tuple-element.34.here_ref), channel_id=1, source_target_pairs={{1,2},{3,4},{5,6},{7,8},{9,10},{11,12},{13,14},{2,1},{4,3},{6,5},{... | collective-permute-start | bytes 98312 | tf_op jit(solution)/shard_map/ppermute | solution.py:306
  32.2 1.8 %copy-start.1 = (bf16[27,128,384]{2,1,0:T(8,128)(2,1)S(1)}, bf16[27,128,384]{2,1,0:T(8,128)(2,1)}, u32[]{:S(2)}) copy-start(bf16[27,128,384]{2,1,0:T(8,128)(2,1)} %weight_ref.3) | copy-start | bytes 7962628
  40.2 1.3 %copy-start.2 = (bf16[16,480,128]{2,1,0:T(8,128)(2,1)}, bf16[16,480,128]{2,1,0:T(8,128)(2,1)S(1)}, u32[]{:S(2)}) copy-start(bf16[16,480,128]{2,1,0:T(8,128)(2,1)S(1)} %get-tuple-element.23) | copy-start | bytes 5898244
  41.5 9.4 %collective-permute-start.4 = (f32[128,128]{1,0:T(8,128)S(1)}, f32[128,128]{1,0:T(8,128)S(1)}, u32[]{:S(2)}, u32[]{:S(2)}) collective-permute-start(f32[128,128]{1,0:T(8,128)S(1)} %get-tuple-element.20), channel_id=1, source_target_pairs={{0,1},{1,0},{2,3},{3,2},{4,5},{5,4},{6,7},{7,6},{8,9},{9,8},{10,11... | collective-permute-start | bytes 196616 | tf_op jit(solution)/shard_map/ppermute | solution.py:297
  41.6 9.3 %collective-permute-start.5 = (f32[128,128]{1,0:T(8,128)S(1)}, f32[128,128]{1,0:T(8,128)S(1)}, u32[]{:S(2)}, u32[]{:S(2)}) collective-permute-start(f32[128,128]{1,0:T(8,128)S(1)} %get-tuple-element.22), channel_id=1, source_target_pairs={{1,2},{3,4},{5,6},{7,8},{9,10},{11,12},{13,14},{2,1},{4,3},{6,5},{... | collective-permute-start | bytes 196616 | tf_op jit(solution)/shard_map/ppermute | solution.py:306
  43.8 36.0 %all-to-all-start.2 = ((bf16[16,480,128]{2,1,0:T(8,128)(2,1)}), bf16[16,480,128]{2,1,0:T(8,128)(2,1)S(1)}, u32[]{:S(2)}, u32[]{:S(2)}) async-start(bf16[16,480,128]{2,1,0:T(8,128)(2,1)} %copy-done.2), calls=%async_computation.2 | async-start | bytes 3932160 | tf_op jit(solution)/shard_map/all_to_all | solution.py:293
  81.6 7.9 %collective-permute-start.6 = (f32[8,8,768]{2,1,0:T(8,128)S(1)}, f32[8,8,768]{2,1,0:T(8,128)S(1)}, u32[]{:S(2)}, u32[]{:S(2)}) collective-permute-start(f32[8,8,768]{2,1,0:T(8,128)S(1)} %get-tuple-element.25), channel_id=1, source_target_pairs={{0,1},{1,0},{2,3},{3,2},{4,5},{5,4},{6,7},{7,6},{8,9},{9,8},{10,11... | collective-permute-start | bytes 589832 | tf_op jit(solution)/shard_map/ppermute | solution.py:297
  84.7 19.6 %all-to-all-start.1 = ((bf16[16,64,128]{2,1,0:T(8,128)(2,1)}), bf16[16,64,128]{2,1,0:T(8,128)(2,1)S(1)}, u32[]{:S(2)}, u32[]{:S(2)}) async-start(bf16[16,64,128]{2,1,0:T(8,128)(2,1)} %shard_map.99), calls=%async_computation.1 | async-start | bytes 524288 | tf_op jit(solution)/shard_map/all_to_all | solution.py:293
  90.0 4.7 %collective-permute-start.7 = (f32[4,8,768]{2,1,0:T(8,128)S(1)}, f32[4,8,768]{2,1,0:T(8,128)S(1)}, u32[]{:S(2)}, u32[]{:S(2)}) collective-permute-start(f32[4,8,768]{2,1,0:T(8,128)S(1)} %get-tuple-element.27), channel_id=1, source_target_pairs={{0,2},{1,3},{2,0},{3,1},{4,6},{5,7},{6,4},{7,5},{8,10},{9,11},{10,... | collective-permute-start | bytes 294920 | tf_op jit(solution)/shard_map/ppermute | solution.py:297
  95.3 7.5 %collective-permute-start.8 = (f32[2,8,768]{2,1,0:T(8,128)S(1)}, f32[2,8,768]{2,1,0:T(8,128)S(1)}, u32[]{:S(2)}, u32[]{:S(2)}) collective-permute-start(f32[2,8,768]{2,1,0:T(8,128)S(1)} %get-tuple-element.29), channel_id=1, source_target_pairs={{0,4},{1,5},{2,6},{3,7},{4,0},{5,1},{6,2},{7,3},{8,12},{9,13},{10,... | collective-permute-start | bytes 147464 | tf_op jit(solution)/shard_map/ppermute | solution.py:297
  103.3 8.0 %collective-permute-start.9 = (f32[1,8,768]{2,1,0:T(8,128)S(1)}, f32[1,8,768]{2,1,0:T(8,128)S(1)}, u32[]{:S(2)}, u32[]{:S(2)}) collective-permute-start(f32[1,8,768]{2,1,0:T(8,128)S(1)} %get-tuple-element.31), channel_id=1, source_target_pairs={{0,8},{1,9},{2,10},{3,11},{4,12},{5,13},{6,14},{7,15},{8,0},{9,1},... | collective-permute-start | bytes 73736 | tf_op jit(solution)/shard_map/ppermute | solution.py:297

commit v3 on v1

--- a/solution.py
+++ b/solution.py
@@ -34,11 +34,12 @@
     return (column >= 0) & (column < COLS) & (row >= 0) & (row < POS // COLS)
 
 
-def call(body, out_shape, in_specs, scratch=(), flops=0, size=0, limit=16):
+def call(body, out_shape, in_specs, scratch=(), flops=0, size=0, limit=16, **options):
     return pl.pallas_call(
         body,
         out_shape=out_shape,
         in_specs=in_specs,
+        **options,
         scratch_shapes=list(scratch),
         compiler_params=pltpu.CompilerParams(vmem_limit_bytes=limit << 20),
         cost_estimate=pl.CostEstimate(flops=flops, bytes_accessed=size, transcendentals=0),
@@ -91,9 +92,8 @@
     return jnp.concatenate([weight_ref[9 * k + 3 * row + col] for k in range(3)], axis=0)
 
 
-def loss_and_back(place_ref, pair_ref, here_ref, cross_ref, weight_ref, bias_ref, packed_ref,
-                  index_ref, blocks_ref, to_pair_ref, keep_ref, to_cross_ref,
-                  padded, moved, cots, shifted):
+def loss_cotangent(place_ref, pair_ref, here_ref, cross_ref, weight_ref, bias_ref, packed_ref,
+                   index_ref, blocks_ref, cots, padded, moved):
     even = place_ref[0] == 0
     zeros = jnp.zeros((PAD, 3 * C1), F32)
     padded[0:PAD] = zeros
@@ -145,6 +145,9 @@
             [part[block * width : (block + 1) * width] for part in turned], axis=0
         ).astype(BF16)
 
+def back_conv(place_ref, cots, weight_ref, to_pair_ref, keep_ref, to_cross_ref, shifted):
+    even = place_ref[0] == 0
+    zeros = jnp.zeros((PAD, 3 * C1), F32)
     cot = cots[...]
     sums = {}
     for row, col in TAPS9:
@@ -171,6 +174,18 @@
     to_pair_ref[...] = jnp.where(even, to_next, to_last)
     keep_ref[...] = total[:, C1 : 2 * C1]
     to_cross_ref[...] = jnp.where(even, to_last, to_next)
+
+
+def halved(pairs, bit, keep_ref, send_ref):
+    for at, (zero, one) in enumerate(pairs):
+        keep_ref[at] = jnp.where(bit == 0, zero, one)
+        send_ref[at] = jnp.where(bit == 0, one, zero)
+
+
+def hidden_grads(pair_ref, keep_ref, cross_ref, zsum_ref, out_ref):
+    grad = pair_ref[...] + keep_ref[...] + cross_ref[...]
+    gelu_tanh = partial(jax.nn.gelu, approximate=True)
+    out_ref[...] = jax.vjp(gelu_tanh, zsum_ref[...])[1](grad)[0].astype(BF16)
 
 
 def second_grads(blocks_ref, out_ref, left, right):
@@ -218,7 +233,22 @@
         ).astype(out_ref.dtype)
 
 
-def first_grads(packed_ref, gz_ref, out_ref, moved):
+def half_sum(level, place_ref, kept_ref, came_ref, keep_ref, send_ref):
+    pairs = [
+        tuple(kept_ref[at] + came_ref[at] for at in (two, two + 1))
+        for two in range(0, kept_ref.shape[0], 2)
+    ]
+    halved(pairs, place_ref[level], keep_ref, send_ref)
+
+
+def last_sum(kept_ref, came_ref, out_ref):
+    total = kept_ref[0] + came_ref[0]
+    width = out_ref.shape[2]
+    for k in range(27):
+        out_ref[k] = total[:, k * width : (k + 1) * width]
+
+
+def first_grads(place_ref, packed_ref, gz_ref, keep_ref, send_ref, moved):
     width, thin = D // 16, C1 // 16
     zeros = jnp.zeros((9 * width, POS), BF16)
     moved[:, 0:POS] = zeros
@@ -242,13 +272,10 @@
         parts.append(
             jnp.dot(moved[:, k * POS : (k + 16) * POS], right, preferred_element_type=F32)
         )
-    parts.append(jnp.zeros((8 * 128 - 27 * width, C1), F32))
+    parts.append(jnp.zeros((7 * 128 - 27 * width, C1), F32))
     turned = jnp.concatenate(parts, axis=0).T
-    for block in range(16):
-        one = turned[block * thin : (block + 1) * thin]
-        out_ref[block] = jnp.concatenate(
-            [one[:, 128 * n : 128 * (n + 1)] for n in range(8)], axis=0
-        ).astype(out_ref.dtype)
+    blocks = [turned[block * thin : (block + 1) * thin] for block in range(16)]
+    halved(zip(blocks[0::2], blocks[1::2]), place_ref[1], keep_ref, send_ref)
 
 
 def summed(parts_ref, out_ref):
@@ -267,8 +294,12 @@
     return lax.all_to_all(value, axis, split_axis=0, concat_axis=0, tiled=True)
 
 
+def swapped(value, step, axis="seq"):
+    return lax.ppermute(value, axis, [(i, i ^ step) for i in range(16)])
+
+
 def with_pair(value):
-    return lax.ppermute(value, "seq", [(i, i ^ 1) for i in range(16)])
+    return swapped(value, 1)
 
 
 def with_cross(value):
@@ -278,7 +309,8 @@
 
 def per_device(tokens, conv_first, bias_first, conv_second, bias_second, pixels, mask_index):
     gelu_tanh = partial(jax.nn.gelu, approximate=True)
-    place = (lax.axis_index("seq") % 2).reshape(1).astype(jnp.int32)
+    clip, frame = lax.axis_index("dp"), lax.axis_index("seq")
+    place = jnp.stack([frame, clip, clip // 2, clip // 4, clip // 8]) % 2
     field = tokens.reshape(POS, D)
     packed = call(
         packed_inputs, struct((16, CHUNK + D // 16, POS), BF16), spots(VMEM, VMEM)
@@ -295,40 +327,49 @@
     zsum = with_pair(pair) + keep + with_cross(cross) + bias_first
     hidden = gelu_tanh(zsum).astype(BF16)
 
-    blocks, pair, keep, cross = call(
-        loss_and_back,
-        (struct((16, CHUNK + 3 * POS, POS), BF16), plane, plane, plane),
+    blocks, cot = call(
+        loss_cotangent,
+        (struct((16, CHUNK + 3 * POS, POS), BF16), struct((4 * POS, CO), BF16)),
         spots(SMEM, *[VMEM] * 7),
-        [
-            pltpu.VMEM((POS + 2 * PAD, 3 * C1), F32),
-            pltpu.VMEM((9, POS, 3 * C1), BF16),
-            pltpu.VMEM((4 * POS, CO), BF16),
-            pltpu.VMEM((9, POS + 2 * PAD, 3 * C1), F32),
-        ],
+        [pltpu.VMEM((POS + 2 * PAD, 3 * C1), F32), pltpu.VMEM((9, POS, 3 * C1), BF16)],
     )(
         place, with_pair(hidden), hidden, with_cross(hidden), conv_second, bias_second[None],
         packed, mask_index,
     )
+    pair, keep, cross = call(
+        back_conv,
+        (plane, plane, plane),
+        spots(SMEM, VMEM, VMEM),
+        [pltpu.VMEM((9, POS + 2 * PAD, 3 * C1), F32)],
+    )(place, cot, conv_second)
     blocks = exchange(blocks, "dp")
-    grad_hidden = with_pair(pair) + keep + with_cross(cross)
-    grad_z = jax.vjp(gelu_tanh, zsum)[1](grad_hidden)[0].astype(BF16)
+    grad_z = call(hidden_grads, struct((POS, C1), BF16), spots(*[VMEM] * 4))(
+        with_pair(pair), keep, with_cross(cross), zsum
+    )
     grad_z = lax.all_gather(grad_z, "seq")
 
-    first = call(
+    half = struct((8, C1 // 16, 7 * 128), F32)
+    keep, send = call(
         first_grads,
-        struct((16, 64, 128), BF16),
-        spots(VMEM, VMEM),
+        (half, half),
+        spots(SMEM, VMEM, VMEM),
         [pltpu.VMEM((9 * D // 16, 18 * POS), BF16)],
-    )(packed, grad_z)
+    )(place, packed, grad_z)
+    for level in (1, 2, 3):
+        half = struct((8 >> level, C1 // 16, 7 * 128), F32)
+        came = swapped(send, 1 << (level - 1), "dp")
+        keep, send = call(
+            partial(half_sum, level + 1), (half, half), spots(SMEM, VMEM, VMEM)
+        )(place, keep, came)
+    grad_first = call(last_sum, struct((27, C1 // 16, D // 16), F32), spots(VMEM, VMEM))(
+        keep, swapped(send, 8, "dp")
+    )
     second = call(
         second_grads,
         struct((16, 48, 128), BF16),
         spots(VMEM),
         [pltpu.VMEM((CO, 16 * POS), BF16), pltpu.VMEM((16 * POS, CO), BF16)],
     )(blocks)
-    grad_first = call(summed, struct((27, C1 // 16, D // 16), F32), spots(VMEM))(
-        exchange(first, "dp")
-    )
     grad_second = call(summed, struct((27, C1 // 16, CO // 16), F32), spots(VMEM))(
         exchange(second, "seq")
     )

time: 113 us -> 108 us (0.956)
  the two profiles are of different devices: /device:TPU:1 before, /device:TPU:32 now
where the time goes in v3:
time: 108 us; the launch traced here: 107 us
  starting transfers between devices  40.8 us (38%)
  waiting for transfers between devices  22.5 us (21%)
  blocking collectives  18.5 us (17%)
  Pallas kernels  15.3 us (14%)
  local copies, waits for them, and re-layouts  8.75 us (8%)
    all_to_all x3, starting transfers between devices, exchange(): return lax.all_to_all(value, axis, split_axis=0, concat_axis=0, tiled=True)  22.8 us
    all_gather x1, blocking collectives, per_device(): grad_z = lax.all_gather(grad_z, 'seq')  18.5 us
    ppermute x3, waiting for transfers between devices, with_cross(): return lax.ppermute(value, 'seq', swaps + [(j, i) for i, j in swaps])  13.4 us
    ppermute x7, starting transfers between devices, swapped(): return lax.ppermute(value, axis, [(i, i ^ step) for i in range(16)])  11.5 us
    ppermute x7, waiting for transfers between devices, swapped(): return lax.ppermute(value, axis, [(i, i ^ step) for i in range(16)])  9.14 us
    unnamed x19, local copies, waits for them, and re-layouts  6.63 us
    ppermute x3, starting transfers between devices, with_cross(): return lax.ppermute(value, 'seq', swaps + [(j, i) for i, j in swaps])  6.44 us
    pallas_call x1, Pallas kernels, per_device(): call(second_grads, struct((16, 48, 128), BF16), spots(VMEM), [pltpu.VMEM(...  3.42 us
  transfers between devices with their start and end apart: 13, of which 6 were waited for; matrix products, arithmetic and copies ran while one was open for 0% of the time, Pallas kernels for 11%

profile of v3, /device:TPU:32, one launch (start us, length us, event | category | flops | bytes accessed | tf_op | source)
XLA Modules:
  0.0 106.7 jit_solution(11562789970370515716)
XLA Ops:
  0.6 0.9 reshape.12.tokens_ref
  1.6 1.1 %reshape.11.pixel_ref = bf16[16,8,1536]{2,1,0:T(8,128)(2,1)S(1)} reshape(bf16[1,16,2,4,1536]{4,3,2,1,0:T(4,128)(2,1)} %param.12) | data formatting | bytes 786432 | tf_op jit(solution)/shard_map/reshape | solution.py:317
  2.8 0.8 copy-done.2
  3.6 8.8 %all-to-all-start = ((bf16[16,128,128]{2,1,0:T(8,128)(2,1)}), bf16[16,128,128]{2,1,0:T(8,128)(2,1)S(1)}, u32[]{:S(2)}, u32[]{:S(2)}) async-start(bf16[16,128,128]{2,1,0:T(8,128)(2,1)} %copy-done.2), calls=%async_computation | async-start | bytes 1048576 | tf_op jit(solution)/shard_map/all_to_all | solution.py:294
  12.6 2.0 %copy-done.1 = bf16[27,512,128]{2,1,0:T(8,128)(2,1)S(1)} copy-done((bf16[27,512,128]{2,1,0:T(8,128)(2,1)S(1)}, bf16[27,512,128]{2,1,0:T(8,128)(2,1)}, u32[]{:S(2)}) %copy-start.1) | copy-done | bytes 3538968
  14.6 1.3 %shard_map.87 = (f32[128,128]{1,0:T(8,128)S(1)}, f32[128,128]{1,0:T(8,128)S(1)}, f32[128,128]{1,0:T(8,128)S(1)}) custom-call(s32[5]{0:T(128)S(1)} %and_select_fusion.place_ref, bf16[128,512]{1,0:T(8,128)(2,1)S(1)} %reshape.12.tokens_ref, bf16[27,512,128]{2,1,0:T(8,128)(2,1)S(1)} %copy-done.1), custom_call_target="tpu_custom_call" | custom-call | tf_op jit(solution)/shard_map/pallas_call | solution.py:321
  16.1 2.0 %collective-permute-start.1 = (f32[128,128]{1,0:T(8,128)S(1)}, f32[128,128]{1,0:T(8,128)S(1)}, u32[]{:S(2)}, u32[]{:S(2)}) collective-permute-start(f32[128,128]{1,0:T(8,128)S(1)} %get-tuple-element.20), channel_id=1, source_target_pairs={{1,2},{3,4},{5,6},{7,8},{9,10},{11,12},{13,14},{2,1},{4,3},{6,5},{... | collective-permute-start | bytes 196616 | tf_op jit(solution)/shard_map/ppermute | solution.py:307
  18.1 7.1 %collective-permute-done.1 = f32[128,128]{1,0:T(8,128)S(1)} collective-permute-done((f32[128,128]{1,0:T(8,128)S(1)}, f32[128,128]{1,0:T(8,128)S(1)}, u32[]{:S(2)}, u32[]{:S(2)}) %collective-permute-start.1) | collective-permute-done | bytes 65568 | tf_op jit(solution)/shard_map/ppermute | solution.py:307
  25.2 1.8 %collective-permute-start.2 = (bf16[128,128]{1,0:T(8,128)(2,1)S(1)}, bf16[128,128]{1,0:T(8,128)(2,1)S(1)}, u32[]{:S(2)}, u32[]{:S(2)}) collective-permute-start(bf16[128,128]{1,0:T(8,128)(2,1)S(1)} %get-tuple-element.36.here_ref), channel_id=1, source_target_pairs={{0,1},{1,0},{2,3},{3,2},{4,5},{5,4},{6,7},{7,6},{8,9},{9,8},{10,11... | collective-permute-start | bytes 98312 | tf_op jit(solution)/shard_map/ppermute | solution.py:298
  27.1 2.4 %collective-permute-start.3 = (bf16[128,128]{1,0:T(8,128)(2,1)S(1)}, bf16[128,128]{1,0:T(8,128)(2,1)S(1)}, u32[]{:S(2)}, u32[]{:S(2)}) collective-permute-start(bf16[128,128]{1,0:T(8,128)(2,1)S(1)} %get-tuple-element.36.here_ref), channel_id=1, source_target_pairs={{1,2},{3,4},{5,6},{7,8},{9,10},{11,12},{13,14},{2,1},{4,3},{6,5},{... | collective-permute-start | bytes 98312 | tf_op jit(solution)/shard_map/ppermute | solution.py:307
  29.5 2.8 %collective-permute-done.3.cross_ref = bf16[128,128]{1,0:T(8,128)(2,1)S(1)} collective-permute-done((bf16[128,128]{1,0:T(8,128)(2,1)S(1)}, bf16[128,128]{1,0:T(8,128)(2,1)S(1)}, u32[]{:S(2)}, u32[]{:S(2)}) %collective-permute-start.3) | collective-permute-done | bytes 32800 | tf_op jit(solution)/shard_map/ppermute | solution.py:307
  32.3 3.2 %shard_map.88 = (bf16[16,480,128]{2,1,0:T(8,128)(2,1)S(1)}, bf16[512,384]{1,0:T(8,128)(2,1)S(1)}) custom-call(s32[5]{0:T(128)S(1)} %and_select_fusion.place_ref, bf16[128,128]{1,0:T(8,128)(2,1)S(1)} %collective-permute-done.2.pair_ref, bf16[128,128]{1,0:T(8,128)(2,1)S(1)} %get-tuple-element.36.here_ref, ...), custom_call_target="tpu_custom_call" | custom-call | tf_op jit(solution)/shard_map/pallas_call | solution.py:330
  35.5 1.3 %copy-done.3 = bf16[16,480,128]{2,1,0:T(8,128)(2,1)} copy-done((bf16[16,480,128]{2,1,0:T(8,128)(2,1)}, bf16[16,480,128]{2,1,0:T(8,128)(2,1)S(1)}, u32[]{:S(2)}) %copy-start.3) | copy-done | bytes 1966104
  36.8 0.8 copy-done.4
  37.6 7.1 %all-to-all-start.1 = ((bf16[16,480,128]{2,1,0:T(8,128)(2,1)}), bf16[16,480,128]{2,1,0:T(8,128)(2,1)}, u32[]{:S(2)}, u32[]{:S(2)}) async-start(bf16[16,480,128]{2,1,0:T(8,128)(2,1)} %copy-done.3), calls=%async_computation.1 | async-start | bytes 3932160 | tf_op jit(solution)/shard_map/all_to_all | solution.py:294
  44.7 1.0 copy-done.5
  45.7 2.9 %shard_map.89 = (f32[128,128]{1,0:T(8,128)S(1)}, f32[128,128]{1,0:T(8,128)S(1)}, f32[128,128]{1,0:T(8,128)S(1)}) custom-call(s32[5]{0:T(128)S(1)} %and_select_fusion.place_ref, bf16[512,384]{1,0:T(8,128)(2,1)S(1)} %copy-done.5, bf16[27,128,384]{2,1,0:T(8,128)(2,1)S(1)} %copy-done), custom_call_target="tpu_custom_call" | custom-call | tf_op jit(solution)/shard_map/pallas_call | solution.py:339
  48.7 2.1 %collective-permute-start.5 = (f32[128,128]{1,0:T(8,128)S(1)}, f32[128,128]{1,0:T(8,128)S(1)}, u32[]{:S(2)}, u32[]{:S(2)}) collective-permute-start(f32[128,128]{1,0:T(8,128)S(1)} %get-tuple-element.24), channel_id=1, source_target_pairs={{1,2},{3,4},{5,6},{7,8},{9,10},{11,12},{13,14},{2,1},{4,3},{6,5},{... | collective-permute-start | bytes 196616 | tf_op jit(solution)/shard_map/ppermute | solution.py:307
  50.8 3.5 %collective-permute-done.5.cross_ref = f32[128,128]{1,0:T(8,128)S(1)} collective-permute-done((f32[128,128]{1,0:T(8,128)S(1)}, f32[128,128]{1,0:T(8,128)S(1)}, u32[]{:S(2)}, u32[]{:S(2)}) %collective-permute-start.5) | collective-permute-done | bytes 65568 | tf_op jit(solution)/shard_map/ppermute | solution.py:307
  54.3 18.5 %all-gather = bf16[2048,128]{1,0:T(8,128)(2,1)S(1)} all-gather(bf16[128,128]{1,0:T(8,128)(2,1)S(1)} %shard_map.90), channel_id=2, replica_groups=mesh['dp'=16,'seq'=16] {'seq'}, dimensions={0}, use_global_device_ids=true | all-gather | bytes 557056 | tf_op jit(solution)/shard_map/all_gather | solution.py:349
  72.8 1.8 %shard_map.91 = (f32[8,8,896]{2,1,0:T(8,128)S(1)}, f32[8,8,896]{2,1,0:T(8,128)S(1)}) custom-call(s32[5]{0:T(128)S(1)} %and_select_fusion.place_ref, bf16[16,128,128]{2,1,0:T(8,128)(2,1)S(1)} %all-to-all-done.packed_ref, bf16[16,128,128]{2,1,0:T(8,128)(2,1)S(1)} %bitcast.7), custom_call_target="tpu_custom_call" | custom-call | tf_op jit(solution)/shard_map/pallas_call | solution.py:352
  74.6 2.0 %collective-permute-start.6 = (f32[8,8,896]{2,1,0:T(8,128)S(1)}, f32[8,8,896]{2,1,0:T(8,128)S(1)}, u32[]{:S(2)}, u32[]{:S(2)}) collective-permute-start(f32[8,8,896]{2,1,0:T(8,128)S(1)} %get-tuple-element.26), channel_id=1, source_target_pairs={{0,16},{16,0},{32,48},{48,32},{64,80},{80,64},{96,112},{112,96},{1... | collective-permute-start | bytes 688136 | tf_op jit(solution)/shard_map/ppermute | solution.py:298
  76.5 3.4 %shard_map.96 = bf16[16,48,128]{2,1,0:T(8,128)(2,1)} custom-call(bf16[16,480,128]{2,1,0:T(8,128)(2,1)} %all-to-all-done.1.blocks_ref), custom_call_target="tpu_custom_call" | custom-call | tf_op jit(solution)/shard_map/pallas_call | solution.py:367
  80.0 6.9 %all-to-all-start.2 = ((bf16[16,48,128]{2,1,0:T(8,128)(2,1)}), bf16[16,48,128]{2,1,0:T(8,128)(2,1)S(1)}, u32[]{:S(2)}, u32[]{:S(2)}) async-start(bf16[16,48,128]{2,1,0:T(8,128)(2,1)} %shard_map.96), calls=%async_computation.2 | async-start | bytes 393216 | tf_op jit(solution)/shard_map/all_to_all | solution.py:294
  87.5 2.8 %collective-permute-start.7 = (f32[4,8,896]{2,1,0:T(8,128)S(1)}, f32[4,8,896]{2,1,0:T(8,128)S(1)}, u32[]{:S(2)}, u32[]{:S(2)}) collective-permute-start(f32[4,8,896]{2,1,0:T(8,128)S(1)} %get-tuple-element.28), channel_id=1, source_target_pairs={{0,32},{16,48},{32,0},{48,16},{64,96},{80,112},{96,64},{112,80},{1... | collective-permute-start | bytes 344072 | tf_op jit(solution)/shard_map/ppermute | solution.py:298
  90.2 4.0 %collective-permute-done.7.came_ref = f32[4,8,896]{2,1,0:T(8,128)S(1)} collective-permute-done((f32[4,8,896]{2,1,0:T(8,128)S(1)}, f32[4,8,896]{2,1,0:T(8,128)S(1)}, u32[]{:S(2)}, u32[]{:S(2)}) %collective-permute-start.7) | collective-permute-done | bytes 114720 | tf_op jit(solution)/shard_map/ppermute | solution.py:298
  94.8 1.5 %collective-permute-start.8 = (f32[2,8,896]{2,1,0:T(8,128)S(1)}, f32[2,8,896]{2,1,0:T(8,128)S(1)}, u32[]{:S(2)}, u32[]{:S(2)}) collective-permute-start(f32[2,8,896]{2,1,0:T(8,128)S(1)} %get-tuple-element.30), channel_id=1, source_target_pairs={{0,64},{16,80},{32,96},{48,112},{64,0},{80,16},{96,32},{112,48},{1... | collective-permute-start | bytes 172040 | tf_op jit(solution)/shard_map/ppermute | solution.py:298
  96.3 2.8 %collective-permute-done.8.came_ref = f32[2,8,896]{2,1,0:T(8,128)S(1)} collective-permute-done((f32[2,8,896]{2,1,0:T(8,128)S(1)}, f32[2,8,896]{2,1,0:T(8,128)S(1)}, u32[]{:S(2)}, u32[]{:S(2)}) %collective-permute-start.8) | collective-permute-done | bytes 57376 | tf_op jit(solution)/shard_map/ppermute | solution.py:298
  99.6 3.1 %collective-permute-start.9 = (f32[1,8,896]{2,1,0:T(8,128)S(1)}, f32[1,8,896]{2,1,0:T(8,128)S(1)}, u32[]{:S(2)}, u32[]{:S(2)}) collective-permute-start(f32[1,8,896]{2,1,0:T(8,128)S(1)} %get-tuple-element.32), channel_id=1, source_target_pairs={{0,128},{16,144},{32,160},{48,176},{64,192},{80,208},{96,224},{112... | collective-permute-start | bytes 86024 | tf_op jit(solution)/shard_map/ppermute | solution.py:298
  102.8 2.3 %collective-permute-done.9.came_ref = f32[1,8,896]{2,1,0:T(8,128)S(1)} collective-permute-done((f32[1,8,896]{2,1,0:T(8,128)S(1)}, f32[1,8,896]{2,1,0:T(8,128)S(1)}, u32[]{:S(2)}, u32[]{:S(2)}) %collective-permute-start.9) | collective-permute-done | bytes 28704 | tf_op jit(solution)/shard_map/ppermute | solution.py:298
  105.1 0.7 shard_map.95
  106.0 0.8 copy.9
  (32 shorter events, 2.5 us)
Async XLA Ops:
  2.7 22.5 %copy-start.8 = (f32[128]{0:T(128)S(1)}, f32[128]{0:T(128)}, u32[]{:S(2)}) copy-start(f32[128]{0:T(128)} %param.9) | copy-start | bytes 1540
  2.7 26.8 %copy-start.7 = (f32[384]{0:T(512)S(1)}, f32[384]{0:T(512)}, u32[]{:S(2)}) copy-start(f32[384]{0:T(512)} %param.11) | copy-start | bytes 4612
  2.7 29.6 %copy-start.6 = (s32[1,115]{1,0:T(1,128)S(1)}, s32[1,115]{1,0:T(1,128)}, u32[]{:S(2)}) copy-start(s32[1,115]{1,0:T(1,128)} %index_ref.1) | copy-start | bytes 1384
  2.8 0.8 copy-start.2
  3.6 28.7 %copy-start = (bf16[27,128,384]{2,1,0:T(8,128)(2,1)S(1)}, bf16[27,128,384]{2,1,0:T(8,128)(2,1)}, u32[]{:S(2)}) copy-start(bf16[27,128,384]{2,1,0:T(8,128)(2,1)} %weight_ref.5) | copy-start | bytes 7962628
  3.6 28.7 %all-to-all-start = ((bf16[16,128,128]{2,1,0:T(8,128)(2,1)}), bf16[16,128,128]{2,1,0:T(8,128)(2,1)S(1)}, u32[]{:S(2)}, u32[]{:S(2)}) async-start(bf16[16,128,128]{2,1,0:T(8,128)(2,1)} %copy-done.2), calls=%async_computation | async-start | bytes 1048576 | tf_op jit(solution)/shard_map/all_to_all | solution.py:294
  12.6 2.0 %copy-start.1 = (bf16[27,512,128]{2,1,0:T(8,128)(2,1)S(1)}, bf16[27,512,128]{2,1,0:T(8,128)(2,1)}, u32[]{:S(2)}) copy-start(bf16[27,512,128]{2,1,0:T(8,128)(2,1)} %weight_ref.3) | copy-start | bytes 10616836
  15.9 2.2 %collective-permute-start = (f32[128,128]{1,0:T(8,128)S(1)}, f32[128,128]{1,0:T(8,128)S(1)}, u32[]{:S(2)}, u32[]{:S(2)}) collective-permute-start(f32[128,128]{1,0:T(8,128)S(1)} %get-tuple-element.18), channel_id=1, source_target_pairs={{0,1},{1,0},{2,3},{3,2},{4,5},{5,4},{6,7},{7,6},{8,9},{9,8},{10,11... | collective-permute-start | bytes 196616 | tf_op jit(solution)/shard_map/ppermute | solution.py:298
  16.1 9.1 %collective-permute-start.1 = (f32[128,128]{1,0:T(8,128)S(1)}, f32[128,128]{1,0:T(8,128)S(1)}, u32[]{:S(2)}, u32[]{:S(2)}) collective-permute-start(f32[128,128]{1,0:T(8,128)S(1)} %get-tuple-element.20), channel_id=1, source_target_pairs={{1,2},{3,4},{5,6},{7,8},{9,10},{11,12},{13,14},{2,1},{4,3},{6,5},{... | collective-permute-start | bytes 196616 | tf_op jit(solution)/shard_map/ppermute | solution.py:307
  25.2 4.2 %collective-permute-start.2 = (bf16[128,128]{1,0:T(8,128)(2,1)S(1)}, bf16[128,128]{1,0:T(8,128)(2,1)S(1)}, u32[]{:S(2)}, u32[]{:S(2)}) collective-permute-start(bf16[128,128]{1,0:T(8,128)(2,1)S(1)} %get-tuple-element.36.here_ref), channel_id=1, source_target_pairs={{0,1},{1,0},{2,3},{3,2},{4,5},{5,4},{6,7},{7,6},{8,9},{9,8},{10,11... | collective-permute-start | bytes 98312 | tf_op jit(solution)/shard_map/ppermute | solution.py:298
  27.1 5.2 %collective-permute-start.3 = (bf16[128,128]{1,0:T(8,128)(2,1)S(1)}, bf16[128,128]{1,0:T(8,128)(2,1)S(1)}, u32[]{:S(2)}, u32[]{:S(2)}) collective-permute-start(bf16[128,128]{1,0:T(8,128)(2,1)S(1)} %get-tuple-element.36.here_ref), channel_id=1, source_target_pairs={{1,2},{3,4},{5,6},{7,8},{9,10},{11,12},{13,14},{2,1},{4,3},{6,5},{... | collective-permute-start | bytes 98312 | tf_op jit(solution)/shard_map/ppermute | solution.py:307
  35.5 1.3 %copy-start.3 = (bf16[16,480,128]{2,1,0:T(8,128)(2,1)}, bf16[16,480,128]{2,1,0:T(8,128)(2,1)S(1)}, u32[]{:S(2)}) copy-start(bf16[16,480,128]{2,1,0:T(8,128)(2,1)S(1)} %get-tuple-element.33) | copy-start | bytes 5898244
  36.8 0.8 copy-start.4
  37.6 39.0 %all-to-all-start.1 = ((bf16[16,480,128]{2,1,0:T(8,128)(2,1)}), bf16[16,480,128]{2,1,0:T(8,128)(2,1)}, u32[]{:S(2)}, u32[]{:S(2)}) async-start(bf16[16,480,128]{2,1,0:T(8,128)(2,1)} %copy-done.3), calls=%async_computation.1 | async-start | bytes 3932160 | tf_op jit(solution)/shard_map/all_to_all | solution.py:294
  44.7 1.0 copy-start.5
  48.6 2.2 %collective-permute-start.4 = (f32[128,128]{1,0:T(8,128)S(1)}, f32[128,128]{1,0:T(8,128)S(1)}, u32[]{:S(2)}, u32[]{:S(2)}) collective-permute-start(f32[128,128]{1,0:T(8,128)S(1)} %get-tuple-element.22), channel_id=1, source_target_pairs={{0,1},{1,0},{2,3},{3,2},{4,5},{5,4},{6,7},{7,6},{8,9},{9,8},{10,11... | collective-permute-start | bytes 196616 | tf_op jit(solution)/shard_map/ppermute | solution.py:298
  48.7 5.6 %collective-permute-start.5 = (f32[128,128]{1,0:T(8,128)S(1)}, f32[128,128]{1,0:T(8,128)S(1)}, u32[]{:S(2)}, u32[]{:S(2)}) collective-permute-start(f32[128,128]{1,0:T(8,128)S(1)} %get-tuple-element.24), channel_id=1, source_target_pairs={{1,2},{3,4},{5,6},{7,8},{9,10},{11,12},{13,14},{2,1},{4,3},{6,5},{... | collective-permute-start | bytes 196616 | tf_op jit(solution)/shard_map/ppermute | solution.py:307
  74.6 12.3 %collective-permute-start.6 = (f32[8,8,896]{2,1,0:T(8,128)S(1)}, f32[8,8,896]{2,1,0:T(8,128)S(1)}, u32[]{:S(2)}, u32[]{:S(2)}) collective-permute-start(f32[8,8,896]{2,1,0:T(8,128)S(1)} %get-tuple-element.26), channel_id=1, source_target_pairs={{0,16},{16,0},{32,48},{48,32},{64,80},{80,64},{96,112},{112,96},{1... | collective-permute-start | bytes 688136 | tf_op jit(solution)/shard_map/ppermute | solution.py:298
  80.0 25.9 %all-to-all-start.2 = ((bf16[16,48,128]{2,1,0:T(8,128)(2,1)}), bf16[16,48,128]{2,1,0:T(8,128)(2,1)S(1)}, u32[]{:S(2)}, u32[]{:S(2)}) async-start(bf16[16,48,128]{2,1,0:T(8,128)(2,1)} %shard_map.96), calls=%async_computation.2 | async-start | bytes 393216 | tf_op jit(solution)/shard_map/all_to_all | solution.py:294
  87.5 6.8 %collective-permute-start.7 = (f32[4,8,896]{2,1,0:T(8,128)S(1)}, f32[4,8,896]{2,1,0:T(8,128)S(1)}, u32[]{:S(2)}, u32[]{:S(2)}) collective-permute-start(f32[4,8,896]{2,1,0:T(8,128)S(1)} %get-tuple-element.28), channel_id=1, source_target_pairs={{0,32},{16,48},{32,0},{48,16},{64,96},{80,112},{96,64},{112,80},{1... | collective-permute-start | bytes 344072 | tf_op jit(solution)/shard_map/ppermute | solution.py:298
  94.8 4.3 %collective-permute-start.8 = (f32[2,8,896]{2,1,0:T(8,128)S(1)}, f32[2,8,896]{2,1,0:T(8,128)S(1)}, u32[]{:S(2)}, u32[]{:S(2)}) collective-permute-start(f32[2,8,896]{2,1,0:T(8,128)S(1)} %get-tuple-element.30), channel_id=1, source_target_pairs={{0,64},{16,80},{32,96},{48,112},{64,0},{80,16},{96,32},{112,48},{1... | collective-permute-start | bytes 172040 | tf_op jit(solution)/shard_map/ppermute | solution.py:298
  99.6 5.5 %collective-permute-start.9 = (f32[1,8,896]{2,1,0:T(8,128)S(1)}, f32[1,8,896]{2,1,0:T(8,128)S(1)}, u32[]{:S(2)}, u32[]{:S(2)}) collective-permute-start(f32[1,8,896]{2,1,0:T(8,128)S(1)} %get-tuple-element.32), channel_id=1, source_target_pairs={{0,128},{16,144},{32,160},{48,176},{64,192},{80,208},{96,224},{112... | collective-permute-start | bytes 86024 | tf_op jit(solution)/shard_map/ppermute | solution.py:298

commit v4 on v3

--- a/solution.py
+++ b/solution.py
@@ -12,6 +12,8 @@
 POS, COLS, PAD = 128, 4, 8
 D, C1, CO = 512, 128, 384
 CHUNK = 4 * CO // 16
+FLOPS = 40_000_000_000
+STEPS = (2, 1, 8, 4)
 TAPS9 = [(row, col) for row in range(3) for col in range(3)]
 PHASES = [(i, j) for i in range(2) for j in range(2)]
 PAIRS = [(-1, 1), (0, 0), (0, 1), (1, 0)]
@@ -57,7 +59,8 @@
     return [pl.BlockSpec(memory_space=kind) for kind in kinds]
 
 
-def packed_inputs(pixel_ref, tokens_ref, out_ref):
+def packed_inputs(pixel_ref, tokens_ref, before_ref, out_ref):
+    del before_ref
     turned = tokens_ref[...].T
     width = D // 16
     for block in range(16):
@@ -182,13 +185,20 @@
         send_ref[at] = jnp.where(bit == 0, one, zero)
 
 
+def hidden_values(pair_ref, keep_ref, cross_ref, bias_ref, zsum_ref, hidden_ref):
+    zsum = pair_ref[...] + keep_ref[...] + cross_ref[...] + bias_ref[...]
+    zsum_ref[...] = zsum
+    hidden_ref[...] = jax.nn.gelu(zsum, approximate=True).astype(BF16)
+
+
 def hidden_grads(pair_ref, keep_ref, cross_ref, zsum_ref, out_ref):
     grad = pair_ref[...] + keep_ref[...] + cross_ref[...]
     gelu_tanh = partial(jax.nn.gelu, approximate=True)
     out_ref[...] = jax.vjp(gelu_tanh, zsum_ref[...])[1](grad)[0].astype(BF16)
 
 
-def second_grads(blocks_ref, out_ref, left, right):
+def second_grads(blocks_ref, before_ref, out_ref, left, right):
+    del before_ref
     wide, thin = CO // 16, C1 // 16
     masks = {}
     for row in (-1, 0, 1):
@@ -274,7 +284,8 @@
         )
     parts.append(jnp.zeros((7 * 128 - 27 * width, C1), F32))
     turned = jnp.concatenate(parts, axis=0).T
-    blocks = [turned[block * thin : (block + 1) * thin] for block in range(16)]
+    order = [sum(step for n, step in enumerate(STEPS) if slot >> n & 1) for slot in range(16)]
+    blocks = [turned[block * thin : (block + 1) * thin] for block in order]
     halved(zip(blocks[0::2], blocks[1::2]), place_ref[1], keep_ref, send_ref)
 
 
@@ -308,15 +319,9 @@
 
 
 def per_device(tokens, conv_first, bias_first, conv_second, bias_second, pixels, mask_index):
-    gelu_tanh = partial(jax.nn.gelu, approximate=True)
     clip, frame = lax.axis_index("dp"), lax.axis_index("seq")
-    place = jnp.stack([frame, clip, clip // 2, clip // 4, clip // 8]) % 2
+    place = jnp.stack([frame] + [clip // step for step in STEPS]) % 2
     field = tokens.reshape(POS, D)
-    packed = call(
-        packed_inputs, struct((16, CHUNK + D // 16, POS), BF16), spots(VMEM, VMEM)
-    )(pixels.reshape(16, 8, 4 * CO), field)
-    packed = exchange(packed, "seq")
-
     plane = struct((POS, C1), F32)
     pair, keep, cross = call(
         first_conv,
@@ -324,8 +329,16 @@
         spots(SMEM, VMEM, VMEM),
         [pltpu.VMEM((POS + 2 * PAD, D), F32)],
     )(place, field, conv_first)
-    zsum = with_pair(pair) + keep + with_cross(cross) + bias_first
-    hidden = gelu_tanh(zsum).astype(BF16)
+    packed = call(
+        packed_inputs, struct((16, CHUNK + D // 16, POS), BF16), spots(VMEM, VMEM, pl.ANY)
+    )(pixels.reshape(16, 8, 4 * CO), field, keep)
+    packed = exchange(packed, "seq")
+    zsum, hidden = call(
+        hidden_values,
+        (plane, struct((POS, C1), BF16)),
+        spots(*[VMEM] * 4),
+        flops=FLOPS,
+    )(with_pair(pair), keep, with_cross(cross), bias_first[None])
 
     blocks, cot = call(
         loss_cotangent,
@@ -343,7 +356,7 @@
         [pltpu.VMEM((9, POS + 2 * PAD, 3 * C1), F32)],
     )(place, cot, conv_second)
     blocks = exchange(blocks, "dp")
-    grad_z = call(hidden_grads, struct((POS, C1), BF16), spots(*[VMEM] * 4))(
+    grad_z = call(hidden_grads, struct((POS, C1), BF16), spots(*[VMEM] * 4), flops=FLOPS)(
         with_pair(pair), keep, with_cross(cross), zsum
     )
     grad_z = lax.all_gather(grad_z, "seq")
@@ -355,21 +368,22 @@
         spots(SMEM, VMEM, VMEM),
         [pltpu.VMEM((9 * D // 16, 18 * POS), BF16)],
     )(place, packed, grad_z)
+    grad_first_half = keep
     for level in (1, 2, 3):
         half = struct((8 >> level, C1 // 16, 7 * 128), F32)
-        came = swapped(send, 1 << (level - 1), "dp")
+        came = swapped(send, STEPS[level - 1], "dp")
         keep, send = call(
             partial(half_sum, level + 1), (half, half), spots(SMEM, VMEM, VMEM)
         )(place, keep, came)
     grad_first = call(last_sum, struct((27, C1 // 16, D // 16), F32), spots(VMEM, VMEM))(
-        keep, swapped(send, 8, "dp")
+        keep, swapped(send, STEPS[3], "dp")
     )
     second = call(
         second_grads,
         struct((16, 48, 128), BF16),
-        spots(VMEM),
+        spots(VMEM, pl.ANY),
         [pltpu.VMEM((CO, 16 * POS), BF16), pltpu.VMEM((16 * POS, CO), BF16)],
-    )(blocks)
+    )(blocks, grad_first_half)
     grad_second = call(summed, struct((27, C1 // 16, CO // 16), F32), spots(VMEM))(
         exchange(second, "seq")
     )

time: 108 us -> 107 us (level)
  waiting for transfers between devices: 22.5 us -> 30.3 us
  local copies, waits for them, and re-layouts: 8.75 us -> 5.18 us
  blocking collectives: 18.5 us -> 15.4 us
  starting transfers between devices: 40.8 us -> 38.2 us
    all_to_all x3, waiting for transfers between devices: 0.01 us -> 8.78 us  [exchange(): return lax.all_to_all(value, axis, split_axis=0, concat_axis=0, tiled=True)]
    ppermute x3, starting transfers between devices: 6.44 us -> 10.8 us  [with_cross(): return lax.ppermute(value, 'seq', swaps + [(j, i) for i, j in swaps])]
    ppermute x7, starting transfers between devices: 11.5 us -> 7.44 us  [swapped(): return lax.ppermute(value, axis, [(i, i ^ step) for i in range(16)])]
    ppermute x3, waiting for transfers between devices: 13.4 us -> 9.93 us  [with_cross(): return lax.ppermute(value, 'seq', swaps + [(j, i) for i, j in swaps])]
    all_gather x1, blocking collectives: 18.5 us -> 15.4 us  [per_device(): grad_z = lax.all_gather(grad_z, 'seq')]
    all_to_all x3, starting transfers between devices: 22.8 us -> 19.9 us  [exchange(): return lax.all_to_all(value, axis, split_axis=0, concat_axis=0, tiled=True)]
    unnamed x19 -> x15, local copies, waits for them, and re-layouts: 6.63 us -> 4.06 us
    ppermute x7, waiting for transfers between devices: 9.14 us -> 11.6 us  [swapped(): return lax.ppermute(value, axis, [(i, i ^ step) for i in range(16)])]
  transfers between devices with their start and end apart: 13 -> 13, of which waited for: 6 -> 6; matrix products, arithmetic and copies ran while one was open for 0% -> 0% of each run, Pallas kernels for 11% -> 7%
where the time goes in v4:
time: 107 us; the launch traced here: 105 us
  starting transfers between devices  38.2 us (36%)
  waiting for transfers between devices  30.3 us (28%)
  blocking collectives  15.4 us (14%)
  Pallas kernels  14.6 us (14%)
  local copies, waits for them, and re-layouts  5.18 us (5%)
    all_to_all x3, starting transfers between devices, exchange(): return lax.all_to_all(value, axis, split_axis=0, concat_axis=0, tiled=True)  19.9 us
    all_gather x1, blocking collectives, per_device(): grad_z = lax.all_gather(grad_z, 'seq')  15.4 us
    ppermute x7, waiting for transfers between devices, swapped(): return lax.ppermute(value, axis, [(i, i ^ step) for i in range(16)])  11.6 us
    ppermute x3, starting transfers between devices, with_cross(): return lax.ppermute(value, 'seq', swaps + [(j, i) for i, j in swaps])  10.8 us
    ppermute x3, waiting for transfers between devices, with_cross(): return lax.ppermute(value, 'seq', swaps + [(j, i) for i, j in swaps])  9.93 us
    all_to_all x3, waiting for transfers between devices, exchange(): return lax.all_to_all(value, axis, split_axis=0, concat_axis=0, tiled=True)  8.78 us
    ppermute x7, starting transfers between devices, swapped(): return lax.ppermute(value, axis, [(i, i ^ step) for i in range(16)])  7.44 us
    unnamed x15, local copies, waits for them, and re-layouts  4.06 us
  transfers between devices with their start and end apart: 13, of which 6 were waited for; matrix products, arithmetic and copies ran while one was open for 0% of the time, Pallas kernels for 7%

profile of v4, /device:TPU:32, one launch (start us, length us, event | category | flops | bytes accessed | tf_op | source)
XLA Modules:
  0.0 104.7 jit_solution(288166015144760362)
XLA Ops:
  0.8 0.9 reshape.11.tokens_ref
  1.7 2.0 %copy-done.1 = bf16[27,512,128]{2,1,0:T(8,128)(2,1)S(1)} copy-done((bf16[27,512,128]{2,1,0:T(8,128)(2,1)S(1)}, bf16[27,512,128]{2,1,0:T(8,128)(2,1)}, u32[]{:S(2)}) %copy-start.1) | copy-done | bytes 3538968
  3.7 1.3 %shard_map.86 = (f32[128,128]{1,0:T(8,128)S(1)}, f32[128,128]{1,0:T(8,128)S(1)}, f32[128,128]{1,0:T(8,128)S(1)}) custom-call(s32[5]{0:T(128)S(1)} %and_select_fusion.place_ref, bf16[128,512]{1,0:T(8,128)(2,1)S(1)} %reshape.11.tokens_ref, bf16[27,512,128]{2,1,0:T(8,128)(2,1)S(1)} %copy-done.1), custom_call_target="tpu_custom_call" | custom-call | tf_op jit(solution)/shard_map/pallas_call | solution.py:326
  5.1 3.8 %collective-permute-start.1 = (f32[128,128]{1,0:T(8,128)S(1)}, f32[128,128]{1,0:T(8,128)S(1)}, u32[]{:S(2)}, u32[]{:S(2)}) collective-permute-start(f32[128,128]{1,0:T(8,128)S(1)} %get-tuple-element.22), channel_id=1, source_target_pairs={{1,2},{3,4},{5,6},{7,8},{9,10},{11,12},{13,14},{2,1},{4,3},{6,5},{... | collective-permute-start | bytes 196616 | tf_op jit(solution)/shard_map/ppermute | solution.py:318
  9.1 0.9 shard_map.87
  10.0 7.4 %all-to-all-start = ((bf16[16,128,128]{2,1,0:T(8,128)(2,1)}), bf16[16,128,128]{2,1,0:T(8,128)(2,1)S(1)}, u32[]{:S(2)}, u32[]{:S(2)}) async-start(bf16[16,128,128]{2,1,0:T(8,128)(2,1)} %shard_map.87), calls=%async_computation | async-start | bytes 1048576 | tf_op jit(solution)/shard_map/all_to_all | solution.py:305
  17.5 0.2 collective-permute-start.2
  17.7 2.1 %collective-permute-start.3 = (bf16[128,128]{1,0:T(8,128)(2,1)S(1)}, bf16[128,128]{1,0:T(8,128)(2,1)S(1)}, u32[]{:S(2)}, u32[]{:S(2)}) collective-permute-start(bf16[128,128]{1,0:T(8,128)(2,1)S(1)} %get-tuple-element.23.here_ref), channel_id=1, source_target_pairs={{1,2},{3,4},{5,6},{7,8},{9,10},{11,12},{13,14},{2,1},{4,3},{6,5},{... | collective-permute-start | bytes 98312 | tf_op jit(solution)/shard_map/ppermute | solution.py:318
  19.9 9.9 %collective-permute-done.3.cross_ref = bf16[128,128]{1,0:T(8,128)(2,1)S(1)} collective-permute-done((bf16[128,128]{1,0:T(8,128)(2,1)S(1)}, bf16[128,128]{1,0:T(8,128)(2,1)S(1)}, u32[]{:S(2)}, u32[]{:S(2)}) %collective-permute-start.3) | collective-permute-done | bytes 32800 | tf_op jit(solution)/shard_map/ppermute | solution.py:318
  29.8 1.9 %all-to-all-done.packed_ref = bf16[16,128,128]{2,1,0:T(8,128)(2,1)S(1)} async-done(((bf16[16,128,128]{2,1,0:T(8,128)(2,1)}), bf16[16,128,128]{2,1,0:T(8,128)(2,1)S(1)}, u32[]{:S(2)}, u32[]{:S(2)}) %all-to-all-start) | async-done | bytes 524320 | tf_op jit(solution)/shard_map/all_to_all | solution.py:305
  31.7 3.2 %shard_map.89 = (bf16[16,480,128]{2,1,0:T(8,128)(2,1)S(1)}, bf16[512,384]{1,0:T(8,128)(2,1)S(1)}) custom-call(s32[5]{0:T(128)S(1)} %and_select_fusion.place_ref, bf16[128,128]{1,0:T(8,128)(2,1)S(1)} %collective-permute-done.2.pair_ref, bf16[128,128]{1,0:T(8,128)(2,1)S(1)} %get-tuple-element.23.here_ref, ...), custom_call_target="tpu_custom_call" | custom-call | tf_op jit(solution)/shard_map/pallas_call | solution.py:343
  35.0 1.3 %copy-done.2 = bf16[16,480,128]{2,1,0:T(8,128)(2,1)} copy-done((bf16[16,480,128]{2,1,0:T(8,128)(2,1)}, bf16[16,480,128]{2,1,0:T(8,128)(2,1)S(1)}, u32[]{:S(2)}) %copy-start.2) | copy-done | bytes 1966104
  36.2 2.9 %shard_map.90 = (f32[128,128]{1,0:T(8,128)S(1)}, f32[128,128]{1,0:T(8,128)S(1)}, f32[128,128]{1,0:T(8,128)S(1)}) custom-call(s32[5]{0:T(128)S(1)} %and_select_fusion.place_ref, bf16[512,384]{1,0:T(8,128)(2,1)S(1)} %get-tuple-element.24.cots, bf16[27,128,384]{2,1,0:T(8,128)(2,1)S(1)} %copy-done), custom_call_target="tpu_custom_call" | custom-call | tf_op jit(solution)/shard_map/pallas_call | solution.py:352
  39.3 4.9 %collective-permute-start.5 = (f32[128,128]{1,0:T(8,128)S(1)}, f32[128,128]{1,0:T(8,128)S(1)}, u32[]{:S(2)}, u32[]{:S(2)}) collective-permute-start(f32[128,128]{1,0:T(8,128)S(1)} %get-tuple-element.27), channel_id=1, source_target_pairs={{1,2},{3,4},{5,6},{7,8},{9,10},{11,12},{13,14},{2,1},{4,3},{6,5},{... | collective-permute-start | bytes 196616 | tf_op jit(solution)/shard_map/ppermute | solution.py:318
  44.3 7.0 %all-to-all-start.1 = ((bf16[16,480,128]{2,1,0:T(8,128)(2,1)}), bf16[16,480,128]{2,1,0:T(8,128)(2,1)S(1)}, u32[]{:S(2)}, u32[]{:S(2)}) async-start(bf16[16,480,128]{2,1,0:T(8,128)(2,1)} %copy-done.2), calls=%async_computation.1 | async-start | bytes 3932160 | tf_op jit(solution)/shard_map/all_to_all | solution.py:305
  51.4 15.4 %all-gather = bf16[2048,128]{1,0:T(8,128)(2,1)S(1)} all-gather(bf16[128,128]{1,0:T(8,128)(2,1)S(1)} %shard_map.91), channel_id=2, replica_groups=mesh['dp'=16,'seq'=16] {'seq'}, dimensions={0}, use_global_device_ids=true | all-gather | bytes 557056 | tf_op jit(solution)/shard_map/all_gather | solution.py:362
  66.8 1.8 %shard_map.92 = (f32[8,8,896]{2,1,0:T(8,128)S(1)}, f32[8,8,896]{2,1,0:T(8,128)S(1)}) custom-call(s32[5]{0:T(128)S(1)} %and_select_fusion.place_ref, bf16[16,128,128]{2,1,0:T(8,128)(2,1)S(1)} %all-to-all-done.packed_ref, bf16[16,128,128]{2,1,0:T(8,128)(2,1)S(1)} %bitcast.8), custom_call_target="tpu_custom_call" | custom-call | tf_op jit(solution)/shard_map/pallas_call | solution.py:365
  68.6 3.5 %collective-permute-start.6 = (f32[8,8,896]{2,1,0:T(8,128)S(1)}, f32[8,8,896]{2,1,0:T(8,128)S(1)}, u32[]{:S(2)}, u32[]{:S(2)}) collective-permute-start(f32[8,8,896]{2,1,0:T(8,128)S(1)} %get-tuple-element.30), channel_id=1, source_target_pairs={{0,32},{16,48},{32,0},{48,16},{64,96},{80,112},{96,64},{112,80},{1... | collective-permute-start | bytes 688136 | tf_op jit(solution)/shard_map/ppermute | solution.py:309
  72.1 6.8 %all-to-all-done.1.blocks_ref = bf16[16,480,128]{2,1,0:T(8,128)(2,1)S(1)} async-done(((bf16[16,480,128]{2,1,0:T(8,128)(2,1)}), bf16[16,480,128]{2,1,0:T(8,128)(2,1)S(1)}, u32[]{:S(2)}, u32[]{:S(2)}) %all-to-all-start.1) | async-done | bytes 1966112 | tf_op jit(solution)/shard_map/all_to_all | solution.py:305
  78.9 1.9 %shard_map.97 = bf16[16,48,128]{2,1,0:T(8,128)(2,1)} custom-call(bf16[16,480,128]{2,1,0:T(8,128)(2,1)S(1)} %all-to-all-done.1.blocks_ref, f32[8,8,896]{2,1,0:T(8,128)S(1)} %get-tuple-element.29.kept_ref.before_ref), custom_call_target="tpu_custom_call" | custom-call | tf_op jit(solution)/shard_map/pallas_call | solution.py:381
  80.8 5.5 %all-to-all-start.2 = ((bf16[16,48,128]{2,1,0:T(8,128)(2,1)}), bf16[16,48,128]{2,1,0:T(8,128)(2,1)S(1)}, u32[]{:S(2)}, u32[]{:S(2)}) async-start(bf16[16,48,128]{2,1,0:T(8,128)(2,1)} %shard_map.97), calls=%async_computation.2 | async-start | bytes 393216 | tf_op jit(solution)/shard_map/all_to_all | solution.py:305
  86.3 0.6 shard_map.93
  86.9 0.7 collective-permute-start.7
  87.6 4.6 %collective-permute-done.7.came_ref = f32[4,8,896]{2,1,0:T(8,128)S(1)} collective-permute-done((f32[4,8,896]{2,1,0:T(8,128)S(1)}, f32[4,8,896]{2,1,0:T(8,128)S(1)}, u32[]{:S(2)}, u32[]{:S(2)}) %collective-permute-start.7) | collective-permute-done | bytes 114720 | tf_op jit(solution)/shard_map/ppermute | solution.py:309
  92.2 0.6 shard_map.94
  92.8 2.0 %collective-permute-start.8 = (f32[2,8,896]{2,1,0:T(8,128)S(1)}, f32[2,8,896]{2,1,0:T(8,128)S(1)}, u32[]{:S(2)}, u32[]{:S(2)}) collective-permute-start(f32[2,8,896]{2,1,0:T(8,128)S(1)} %get-tuple-element.34), channel_id=1, source_target_pairs={{0,128},{16,144},{32,160},{48,176},{64,192},{80,208},{96,224},{112... | collective-permute-start | bytes 172040 | tf_op jit(solution)/shard_map/ppermute | solution.py:309
  94.8 3.8 %collective-permute-done.8.came_ref = f32[2,8,896]{2,1,0:T(8,128)S(1)} collective-permute-done((f32[2,8,896]{2,1,0:T(8,128)S(1)}, f32[2,8,896]{2,1,0:T(8,128)S(1)}, u32[]{:S(2)}, u32[]{:S(2)}) %collective-permute-start.8) | collective-permute-done | bytes 57376 | tf_op jit(solution)/shard_map/ppermute | solution.py:309
  98.5 0.6 shard_map.95
  99.1 0.7 collective-permute-start.9
  99.8 3.2 %collective-permute-done.9.came_ref = f32[1,8,896]{2,1,0:T(8,128)S(1)} collective-permute-done((f32[1,8,896]{2,1,0:T(8,128)S(1)}, f32[1,8,896]{2,1,0:T(8,128)S(1)}, u32[]{:S(2)}, u32[]{:S(2)}) %collective-permute-start.9) | collective-permute-done | bytes 28704 | tf_op jit(solution)/shard_map/ppermute | solution.py:309
  103.0 0.7 shard_map.96
  103.9 0.8 copy.9
  (28 shorter events, 0.8 us)
Async XLA Ops:
  1.7 2.0 %copy-start.1 = (bf16[27,512,128]{2,1,0:T(8,128)(2,1)S(1)}, bf16[27,512,128]{2,1,0:T(8,128)(2,1)}, u32[]{:S(2)}) copy-start(bf16[27,512,128]{2,1,0:T(8,128)(2,1)} %weight_ref.3) | copy-start | bytes 10616836
  3.7 5.3 %copy-start.5 = (bf16[1,16,2,4,1536]{4,3,2,1,0:T(4,128)(2,1)S(1)}, bf16[1,16,2,4,1536]{4,3,2,1,0:T(4,128)(2,1)}, u32[]{:S(2)}) copy-start(bf16[1,16,2,4,1536]{4,3,2,1,0:T(4,128)(2,1)} %param.12) | copy-start | bytes 1179652
  3.7 13.7 %copy-start.4 = (f32[128]{0:T(128)S(1)}, f32[128]{0:T(128)}, u32[]{:S(2)}) copy-start(f32[128]{0:T(128)} %param.9) | copy-start | bytes 1540
  5.0 12.4 %collective-permute-start = (f32[128,128]{1,0:T(8,128)S(1)}, f32[128,128]{1,0:T(8,128)S(1)}, u32[]{:S(2)}, u32[]{:S(2)}) collective-permute-start(f32[128,128]{1,0:T(8,128)S(1)} %get-tuple-element.21), channel_id=1, source_target_pairs={{0,1},{1,0},{2,3},{3,2},{4,5},{5,4},{6,7},{7,6},{8,9},{9,8},{10,11... | collective-permute-start | bytes 196616 | tf_op jit(solution)/shard_map/ppermute | solution.py:309
  5.1 12.3 %collective-permute-start.1 = (f32[128,128]{1,0:T(8,128)S(1)}, f32[128,128]{1,0:T(8,128)S(1)}, u32[]{:S(2)}, u32[]{:S(2)}) collective-permute-start(f32[128,128]{1,0:T(8,128)S(1)} %get-tuple-element.22), channel_id=1, source_target_pairs={{1,2},{3,4},{5,6},{7,8},{9,10},{11,12},{13,14},{2,1},{4,3},{6,5},{... | collective-permute-start | bytes 196616 | tf_op jit(solution)/shard_map/ppermute | solution.py:318
  10.0 21.8 %all-to-all-start = ((bf16[16,128,128]{2,1,0:T(8,128)(2,1)}), bf16[16,128,128]{2,1,0:T(8,128)(2,1)S(1)}, u32[]{:S(2)}, u32[]{:S(2)}) async-start(bf16[16,128,128]{2,1,0:T(8,128)(2,1)} %shard_map.87), calls=%async_computation | async-start | bytes 1048576 | tf_op jit(solution)/shard_map/all_to_all | solution.py:305
  17.4 2.4 %copy-start.6 = (f32[384]{0:T(512)S(1)}, f32[384]{0:T(512)}, u32[]{:S(2)}) copy-start(f32[384]{0:T(512)} %param.11) | copy-start | bytes 4612
  17.4 14.3 %copy-start = (bf16[27,128,384]{2,1,0:T(8,128)(2,1)S(1)}, bf16[27,128,384]{2,1,0:T(8,128)(2,1)}, u32[]{:S(2)}) copy-start(bf16[27,128,384]{2,1,0:T(8,128)(2,1)} %weight_ref.5) | copy-start | bytes 7962628
  17.4 14.3 %copy-start.3 = (s32[1,115]{1,0:T(1,128)S(1)}, s32[1,115]{1,0:T(1,128)}, u32[]{:S(2)}) copy-start(s32[1,115]{1,0:T(1,128)} %index_ref.1) | copy-start | bytes 1384
  17.5 2.4 %collective-permute-start.2 = (bf16[128,128]{1,0:T(8,128)(2,1)S(1)}, bf16[128,128]{1,0:T(8,128)(2,1)S(1)}, u32[]{:S(2)}, u32[]{:S(2)}) collective-permute-start(bf16[128,128]{1,0:T(8,128)(2,1)S(1)} %get-tuple-element.23.here_ref), channel_id=1, source_target_pairs={{0,1},{1,0},{2,3},{3,2},{4,5},{5,4},{6,7},{7,6},{8,9},{9,8},{10,11... | collective-permute-start | bytes 98312 | tf_op jit(solution)/shard_map/ppermute | solution.py:309
  17.7 12.1 %collective-permute-start.3 = (bf16[128,128]{1,0:T(8,128)(2,1)S(1)}, bf16[128,128]{1,0:T(8,128)(2,1)S(1)}, u32[]{:S(2)}, u32[]{:S(2)}) collective-permute-start(bf16[128,128]{1,0:T(8,128)(2,1)S(1)} %get-tuple-element.23.here_ref), channel_id=1, source_target_pairs={{1,2},{3,4},{5,6},{7,8},{9,10},{11,12},{13,14},{2,1},{4,3},{6,5},{... | collective-permute-start | bytes 98312 | tf_op jit(solution)/shard_map/ppermute | solution.py:318
  34.9 1.3 %copy-start.2 = (bf16[16,480,128]{2,1,0:T(8,128)(2,1)}, bf16[16,480,128]{2,1,0:T(8,128)(2,1)S(1)}, u32[]{:S(2)}) copy-start(bf16[16,480,128]{2,1,0:T(8,128)(2,1)S(1)} %get-tuple-element.37) | copy-start | bytes 5898244
  39.1 12.2 %collective-permute-start.4 = (f32[128,128]{1,0:T(8,128)S(1)}, f32[128,128]{1,0:T(8,128)S(1)}, u32[]{:S(2)}, u32[]{:S(2)}) collective-permute-start(f32[128,128]{1,0:T(8,128)S(1)} %get-tuple-element.25), channel_id=1, source_target_pairs={{0,1},{1,0},{2,3},{3,2},{4,5},{5,4},{6,7},{7,6},{8,9},{9,8},{10,11... | collective-permute-start | bytes 196616 | tf_op jit(solution)/shard_map/ppermute | solution.py:309
  39.3 12.0 %collective-permute-start.5 = (f32[128,128]{1,0:T(8,128)S(1)}, f32[128,128]{1,0:T(8,128)S(1)}, u32[]{:S(2)}, u32[]{:S(2)}) collective-permute-start(f32[128,128]{1,0:T(8,128)S(1)} %get-tuple-element.27), channel_id=1, source_target_pairs={{1,2},{3,4},{5,6},{7,8},{9,10},{11,12},{13,14},{2,1},{4,3},{6,5},{... | collective-permute-start | bytes 196616 | tf_op jit(solution)/shard_map/ppermute | solution.py:318
  44.3 34.7 %all-to-all-start.1 = ((bf16[16,480,128]{2,1,0:T(8,128)(2,1)}), bf16[16,480,128]{2,1,0:T(8,128)(2,1)S(1)}, u32[]{:S(2)}, u32[]{:S(2)}) async-start(bf16[16,480,128]{2,1,0:T(8,128)(2,1)} %copy-done.2), calls=%async_computation.1 | async-start | bytes 3932160 | tf_op jit(solution)/shard_map/all_to_all | solution.py:305
  68.6 17.8 %collective-permute-start.6 = (f32[8,8,896]{2,1,0:T(8,128)S(1)}, f32[8,8,896]{2,1,0:T(8,128)S(1)}, u32[]{:S(2)}, u32[]{:S(2)}) collective-permute-start(f32[8,8,896]{2,1,0:T(8,128)S(1)} %get-tuple-element.30), channel_id=1, source_target_pairs={{0,32},{16,48},{32,0},{48,16},{64,96},{80,112},{96,64},{112,80},{1... | collective-permute-start | bytes 688136 | tf_op jit(solution)/shard_map/ppermute | solution.py:309
  80.8 23.0 %all-to-all-start.2 = ((bf16[16,48,128]{2,1,0:T(8,128)(2,1)}), bf16[16,48,128]{2,1,0:T(8,128)(2,1)S(1)}, u32[]{:S(2)}, u32[]{:S(2)}) async-start(bf16[16,48,128]{2,1,0:T(8,128)(2,1)} %shard_map.97), calls=%async_computation.2 | async-start | bytes 393216 | tf_op jit(solution)/shard_map/all_to_all | solution.py:305
  86.9 5.3 %collective-permute-start.7 = (f32[4,8,896]{2,1,0:T(8,128)S(1)}, f32[4,8,896]{2,1,0:T(8,128)S(1)}, u32[]{:S(2)}, u32[]{:S(2)}) collective-permute-start(f32[4,8,896]{2,1,0:T(8,128)S(1)} %get-tuple-element.32), channel_id=1, source_target_pairs={{0,16},{16,0},{32,48},{48,32},{64,80},{80,64},{96,112},{112,96},{1... | collective-permute-start | bytes 344072 | tf_op jit(solution)/shard_map/ppermute | solution.py:309
  92.8 5.8 %collective-permute-start.8 = (f32[2,8,896]{2,1,0:T(8,128)S(1)}, f32[2,8,896]{2,1,0:T(8,128)S(1)}, u32[]{:S(2)}, u32[]{:S(2)}) collective-permute-start(f32[2,8,896]{2,1,0:T(8,128)S(1)} %get-tuple-element.34), channel_id=1, source_target_pairs={{0,128},{16,144},{32,160},{48,176},{64,192},{80,208},{96,224},{112... | collective-permute-start | bytes 172040 | tf_op jit(solution)/shard_map/ppermute | solution.py:309
  99.1 4.0 %collective-permute-start.9 = (f32[1,8,896]{2,1,0:T(8,128)S(1)}, f32[1,8,896]{2,1,0:T(8,128)S(1)}, u32[]{:S(2)}, u32[]{:S(2)}) collective-permute-start(f32[1,8,896]{2,1,0:T(8,128)S(1)} %get-tuple-element.36), channel_id=1, source_target_pairs={{0,64},{16,80},{32,96},{48,112},{64,0},{80,16},{96,32},{112,48},{1... | collective-permute-start | bytes 86024 | tf_op jit(solution)/shard_map/ppermute | solution.py:309

commit v5 on v4

--- a/solution.py
+++ b/solution.py
@@ -52,15 +52,14 @@
     return jax.ShapeDtypeStruct(shape, dtype)
 
 
-SMEM, VMEM, HBM = pltpu.SMEM, pltpu.VMEM, pltpu.HBM
+VMEM = pltpu.VMEM
 
 
 def spots(*kinds):
     return [pl.BlockSpec(memory_space=kind) for kind in kinds]
 
 
-def packed_inputs(pixel_ref, tokens_ref, before_ref, out_ref):
-    del before_ref
+def packed_inputs(pixel_ref, tokens_ref, out_ref):
     turned = tokens_ref[...].T
     width = D // 16
     for block in range(16):
@@ -71,7 +70,8 @@
         out_ref[block, CHUNK:] = turned[block * width : (block + 1) * width]
 
 
-def first_conv(place_ref, tokens_ref, weight_ref, pair_ref, keep_ref, cross_ref, padded):
+def first_conv(tokens_ref, weight_ref, before_ref, pair_ref, keep_ref, cross_ref, padded):
+    del before_ref
     padded[0:PAD] = jnp.zeros((PAD, D), F32)
     padded[PAD + POS :] = jnp.zeros((PAD, D), F32)
     padded[PAD : PAD + POS] = tokens_ref[...].astype(F32)
@@ -85,7 +85,7 @@
         weight = jnp.concatenate([weight_ref[tap + 9 * k] for k in range(3)], axis=1)
         total = total + jnp.dot(window.astype(BF16), weight, preferred_element_type=F32)
     to_next, to_last = total[:, 0:C1], total[:, 2 * C1 :]
-    even = place_ref[0] == 0
+    even = lax.axis_index("seq") % 2 == 0
     pair_ref[...] = jnp.where(even, to_next, to_last)
     keep_ref[...] = total[:, C1 : 2 * C1]
     cross_ref[...] = jnp.where(even, to_last, to_next)
@@ -95,9 +95,9 @@
     return jnp.concatenate([weight_ref[9 * k + 3 * row + col] for k in range(3)], axis=0)
 
 
-def loss_cotangent(place_ref, pair_ref, here_ref, cross_ref, weight_ref, bias_ref, packed_ref,
+def loss_cotangent(pair_ref, here_ref, cross_ref, weight_ref, bias_ref, packed_ref,
                    index_ref, blocks_ref, cots, padded, moved):
-    even = place_ref[0] == 0
+    even = lax.axis_index("seq") % 2 == 0
     zeros = jnp.zeros((PAD, 3 * C1), F32)
     padded[0:PAD] = zeros
     padded[PAD + POS :] = zeros
@@ -148,8 +148,8 @@
             [part[block * width : (block + 1) * width] for part in turned], axis=0
         ).astype(BF16)
 
-def back_conv(place_ref, cots, weight_ref, to_pair_ref, keep_ref, to_cross_ref, shifted):
-    even = place_ref[0] == 0
+def back_conv(cots, weight_ref, to_pair_ref, keep_ref, to_cross_ref, shifted):
+    even = lax.axis_index("seq") % 2 == 0
     zeros = jnp.zeros((PAD, 3 * C1), F32)
     cot = cots[...]
     sums = {}
@@ -179,7 +179,8 @@
     to_cross_ref[...] = jnp.where(even, to_last, to_next)
 
 
-def halved(pairs, bit, keep_ref, send_ref):
+def halved(pairs, level, keep_ref, send_ref):
+    bit = lax.axis_index("dp") // STEPS[level] % 2
     for at, (zero, one) in enumerate(pairs):
         keep_ref[at] = jnp.where(bit == 0, zero, one)
         send_ref[at] = jnp.where(bit == 0, one, zero)
@@ -243,12 +244,12 @@
         ).astype(out_ref.dtype)
 
 
-def half_sum(level, place_ref, kept_ref, came_ref, keep_ref, send_ref):
+def half_sum(level, kept_ref, came_ref, keep_ref, send_ref):
     pairs = [
         tuple(kept_ref[at] + came_ref[at] for at in (two, two + 1))
         for two in range(0, kept_ref.shape[0], 2)
     ]
-    halved(pairs, place_ref[level], keep_ref, send_ref)
+    halved(pairs, level, keep_ref, send_ref)
 
 
 def last_sum(kept_ref, came_ref, out_ref):
@@ -258,7 +259,7 @@
         out_ref[k] = total[:, k * width : (k + 1) * width]
 
 
-def first_grads(place_ref, packed_ref, gz_ref, keep_ref, send_ref, moved):
+def first_grads(packed_ref, gz_ref, keep_ref, send_ref, moved):
     width, thin = D // 16, C1 // 16
     zeros = jnp.zeros((9 * width, POS), BF16)
     moved[:, 0:POS] = zeros
@@ -286,7 +287,7 @@
     turned = jnp.concatenate(parts, axis=0).T
     order = [sum(step for n, step in enumerate(STEPS) if slot >> n & 1) for slot in range(16)]
     blocks = [turned[block * thin : (block + 1) * thin] for block in order]
-    halved(zip(blocks[0::2], blocks[1::2]), place_ref[1], keep_ref, send_ref)
+    halved(zip(blocks[0::2], blocks[1::2]), 0, keep_ref, send_ref)
 
 
 def summed(parts_ref, out_ref):
@@ -319,19 +320,17 @@
 
 
 def per_device(tokens, conv_first, bias_first, conv_second, bias_second, pixels, mask_index):
-    clip, frame = lax.axis_index("dp"), lax.axis_index("seq")
-    place = jnp.stack([frame] + [clip // step for step in STEPS]) % 2
     field = tokens.reshape(POS, D)
+    packed = call(
+        packed_inputs, struct((16, CHUNK + D // 16, POS), BF16), spots(VMEM, VMEM)
+    )(pixels.reshape(16, 8, 4 * CO), field)
     plane = struct((POS, C1), F32)
     pair, keep, cross = call(
         first_conv,
         (plane, plane, plane),
-        spots(SMEM, VMEM, VMEM),
+        spots(VMEM, VMEM, pl.ANY),
         [pltpu.VMEM((POS + 2 * PAD, D), F32)],
-    )(place, field, conv_first)
-    packed = call(
-        packed_inputs, struct((16, CHUNK + D // 16, POS), BF16), spots(VMEM, VMEM, pl.ANY)
-    )(pixels.reshape(16, 8, 4 * CO), field, keep)
+    )(field, conv_first, packed)
     packed = exchange(packed, "seq")
     zsum, hidden = call(
         hidden_values,
@@ -343,20 +342,20 @@
     blocks, cot = call(
         loss_cotangent,
         (struct((16, CHUNK + 3 * POS, POS), BF16), struct((4 * POS, CO), BF16)),
-        spots(SMEM, *[VMEM] * 7),
+        spots(*[VMEM] * 7),
         [pltpu.VMEM((POS + 2 * PAD, 3 * C1), F32), pltpu.VMEM((9, POS, 3 * C1), BF16)],
     )(
-        place, with_pair(hidden), hidden, with_cross(hidden), conv_second, bias_second[None],
+        with_pair(hidden), hidden, with_cross(hidden), conv_second, bias_second[None],
         packed, mask_index,
     )
     pair, keep, cross = call(
         back_conv,
         (plane, plane, plane),
-        spots(SMEM, VMEM, VMEM),
+        spots(VMEM, VMEM),
         [pltpu.VMEM((9, POS + 2 * PAD, 3 * C1), F32)],
-    )(place, cot, conv_second)
+    )(cot, conv_second)
     blocks = exchange(blocks, "dp")
-    grad_z = call(hidden_grads, struct((POS, C1), BF16), spots(*[VMEM] * 4), flops=FLOPS)(
+    grad_z = call(hidden_grads, struct((POS, C1), BF16), spots(*[VMEM] * 4))(
         with_pair(pair), keep, with_cross(cross), zsum
     )
     grad_z = lax.all_gather(grad_z, "seq")
@@ -365,16 +364,16 @@
     keep, send = call(
         first_grads,
         (half, half),
-        spots(SMEM, VMEM, VMEM),
+        spots(VMEM, VMEM),
         [pltpu.VMEM((9 * D // 16, 18 * POS), BF16)],
-    )(place, packed, grad_z)
+    )(packed, grad_z)
     grad_first_half = keep
     for level in (1, 2, 3):
         half = struct((8 >> level, C1 // 16, 7 * 128), F32)
         came = swapped(send, STEPS[level - 1], "dp")
         keep, send = call(
-            partial(half_sum, level + 1), (half, half), spots(SMEM, VMEM, VMEM)
-        )(place, keep, came)
+            partial(half_sum, level), (half, half), spots(VMEM, VMEM)
+        )(keep, came)
     grad_first = call(last_sum, struct((27, C1 // 16, D // 16), F32), spots(VMEM, VMEM))(
         keep, swapped(send, STEPS[3], "dp")
     )

time: 107 us -> 103 us (0.963); the launches traced: 105 us -> 102 us
  waiting for transfers between devices: 30.3 us -> 23.4 us
  starting transfers between devices: 38.2 us -> 41.5 us
  local copies, waits for them, and re-layouts: 5.18 us -> 7.84 us
  Pallas kernels: 14.6 us -> 12.4 us
    all_to_all x3, waiting for transfers between devices: 8.78 us -> 1.96 us  [exchange(): return lax.all_to_all(value, axis, split_axis=0, concat_axis=0, tiled=True)]
    pallas_call x7, Pallas kernels: 7.75 us -> 4.53 us  [the longest x1 2.37 us: per_device(): call(back_conv, (plane, plane, plane), spots(VMEM, VMEM), [pltpu.VMEM((9,...]
    ppermute x7, waiting for transfers between devices: 11.6 us -> 9.59 us  [swapped(): return lax.ppermute(value, axis, [(i, i ^ step) for i in range(16)])]
    ppermute x3, waiting for transfers between devices: 9.93 us -> 11.9 us  [with_cross(): return lax.ppermute(value, 'seq', swaps + [(j, i) for i, j in swaps])]
    ppermute x7, starting transfers between devices: 7.44 us -> 9.33 us  [swapped(): return lax.ppermute(value, axis, [(i, i ^ step) for i in range(16)])]
    unnamed x15 -> x17, local copies, waits for them, and re-layouts: 4.06 us -> 5.8 us
    all_to_all x3, starting transfers between devices: 19.9 us -> 21.5 us  [exchange(): return lax.all_to_all(value, axis, split_axis=0, concat_axis=0, tiled=True)]
    pallas_call x1, Pallas kernels: 1.89 us -> 3.42 us  [per_device(): call(second_grads, struct((16, 48, 128), BF16), spots(VMEM, pl.ANY), [plt...]
  transfers between devices with their start and end apart: 13 -> 13, of which waited for: 6 -> 6; matrix products, arithmetic and copies ran while one was open for 0% -> 0% of each run, Pallas kernels for 7% -> 8%
where the time goes in v5:
time: 103 us; the launch traced here: 102 us
  starting transfers between devices  41.5 us (40%)
  waiting for transfers between devices  23.4 us (23%)
  blocking collectives  16.1 us (16%)
  Pallas kernels  12.4 us (12%)
  local copies, waits for them, and re-layouts  7.84 us (8%)
    all_to_all x3, starting transfers between devices, exchange(): return lax.all_to_all(value, axis, split_axis=0, concat_axis=0, tiled=True)  21.5 us
    all_gather x1, blocking collectives, per_device(): grad_z = lax.all_gather(grad_z, 'seq')  16.1 us
    ppermute x3, waiting for transfers between devices, with_cross(): return lax.ppermute(value, 'seq', swaps + [(j, i) for i, j in swaps])  11.9 us
    ppermute x3, starting transfers between devices, with_cross(): return lax.ppermute(value, 'seq', swaps + [(j, i) for i, j in swaps])  10.7 us
    ppermute x7, waiting for transfers between devices, swapped(): return lax.ppermute(value, axis, [(i, i ^ step) for i in range(16)])  9.59 us
    ppermute x7, starting transfers between devices, swapped(): return lax.ppermute(value, axis, [(i, i ^ step) for i in range(16)])  9.33 us
    unnamed x17, local copies, waits for them, and re-layouts  5.8 us
    pallas_call x1, Pallas kernels, per_device(): call(second_grads, struct((16, 48, 128), BF16), spots(VMEM, pl.ANY), [plt...  3.42 us
  transfers between devices with their start and end apart: 13, of which 6 were waited for; matrix products, arithmetic and copies ran while one was open for 0% of the time, Pallas kernels for 8%

profile of v5, /device:TPU:32, one launch (start us, length us, event | category | flops | bytes accessed | tf_op | source)
XLA Modules:
  0.0 102.1 jit_solution(6669746241670236862)
XLA Ops:
  0.6 1.1 %reshape.10.pixel_ref = bf16[16,8,1536]{2,1,0:T(8,128)(2,1)S(1)} reshape(bf16[1,16,2,4,1536]{4,3,2,1,0:T(4,128)(2,1)} %param.12) | data formatting | bytes 786432 | tf_op jit(solution)/shard_map/reshape | solution.py:326
  1.7 0.9 reshape.11.tokens_ref
  2.7 0.9 shard_map.86.before_ref
  3.6 2.0 %copy-done.1 = bf16[27,512,128]{2,1,0:T(8,128)(2,1)S(1)} copy-done((bf16[27,512,128]{2,1,0:T(8,128)(2,1)S(1)}, bf16[27,512,128]{2,1,0:T(8,128)(2,1)}, u32[]{:S(2)}) %copy-start.1) | copy-done | bytes 3538968
  5.6 0.8 shard_map.87
  6.4 3.8 %collective-permute-start.1 = (f32[128,128]{1,0:T(8,128)S(1)}, f32[128,128]{1,0:T(8,128)S(1)}, u32[]{:S(2)}, u32[]{:S(2)}) collective-permute-start(f32[128,128]{1,0:T(8,128)S(1)} %get-tuple-element.22), channel_id=1, source_target_pairs={{1,2},{3,4},{5,6},{7,8},{9,10},{11,12},{13,14},{2,1},{4,3},{6,5},{... | collective-permute-start | bytes 196616 | tf_op jit(solution)/shard_map/ppermute | solution.py:319
  10.3 7.4 %all-to-all-start = ((bf16[16,128,128]{2,1,0:T(8,128)(2,1)}), bf16[16,128,128]{2,1,0:T(8,128)(2,1)S(1)}, u32[]{:S(2)}, u32[]{:S(2)}) async-start(bf16[16,128,128]{2,1,0:T(8,128)(2,1)} %shard_map.86.before_ref), calls=%async_computation | async-start | bytes 1048576 | tf_op jit(solution)/shard_map/all_to_all | solution.py:306
  17.8 0.2 collective-permute-start.2
  18.0 2.1 %collective-permute-start.3 = (bf16[128,128]{1,0:T(8,128)(2,1)S(1)}, bf16[128,128]{1,0:T(8,128)(2,1)S(1)}, u32[]{:S(2)}, u32[]{:S(2)}) collective-permute-start(bf16[128,128]{1,0:T(8,128)(2,1)S(1)} %get-tuple-element.23.here_ref), channel_id=1, source_target_pairs={{1,2},{3,4},{5,6},{7,8},{9,10},{11,12},{13,14},{2,1},{4,3},{6,5},{... | collective-permute-start | bytes 98312 | tf_op jit(solution)/shard_map/ppermute | solution.py:319
  20.2 9.9 %collective-permute-done.3.cross_ref = bf16[128,128]{1,0:T(8,128)(2,1)S(1)} collective-permute-done((bf16[128,128]{1,0:T(8,128)(2,1)S(1)}, bf16[128,128]{1,0:T(8,128)(2,1)S(1)}, u32[]{:S(2)}, u32[]{:S(2)}) %collective-permute-start.3) | collective-permute-done | bytes 32800 | tf_op jit(solution)/shard_map/ppermute | solution.py:319
  30.1 1.9 %all-to-all-done.packed_ref = bf16[16,128,128]{2,1,0:T(8,128)(2,1)S(1)} async-done(((bf16[16,128,128]{2,1,0:T(8,128)(2,1)}), bf16[16,128,128]{2,1,0:T(8,128)(2,1)S(1)}, u32[]{:S(2)}, u32[]{:S(2)}) %all-to-all-start) | async-done | bytes 524320 | tf_op jit(solution)/shard_map/all_to_all | solution.py:306
  32.1 2.7 %shard_map.89 = (bf16[16,480,128]{2,1,0:T(8,128)(2,1)S(1)}, bf16[512,384]{1,0:T(8,128)(2,1)S(1)}) custom-call(bf16[128,128]{1,0:T(8,128)(2,1)S(1)} %collective-permute-done.2.pair_ref, bf16[128,128]{1,0:T(8,128)(2,1)S(1)} %get-tuple-element.23.here_ref, bf16[128,128]{1,0:T(8,128)(2,1)S(1)} %collective-permute-done.3.cross_ref, ...), custom_call_target="tpu_custom_call" | custom-call | tf_op jit(solution)/shard_map/pallas_call | solution.py:342
  34.8 1.3 %copy-done.2 = bf16[16,480,128]{2,1,0:T(8,128)(2,1)} copy-done((bf16[16,480,128]{2,1,0:T(8,128)(2,1)}, bf16[16,480,128]{2,1,0:T(8,128)(2,1)S(1)}, u32[]{:S(2)}) %copy-start.2) | copy-done | bytes 1966104
  36.1 0.8 copy-done.3
  36.8 7.1 %all-to-all-start.1 = ((bf16[16,480,128]{2,1,0:T(8,128)(2,1)}), bf16[16,480,128]{2,1,0:T(8,128)(2,1)}, u32[]{:S(2)}, u32[]{:S(2)}) async-start(bf16[16,480,128]{2,1,0:T(8,128)(2,1)} %copy-done.2), calls=%async_computation.1 | async-start | bytes 3932160 | tf_op jit(solution)/shard_map/all_to_all | solution.py:306
  43.9 1.0 copy-done.4
  44.9 2.4 %shard_map.90 = (f32[128,128]{1,0:T(8,128)S(1)}, f32[128,128]{1,0:T(8,128)S(1)}, f32[128,128]{1,0:T(8,128)S(1)}) custom-call(bf16[512,384]{1,0:T(8,128)(2,1)S(1)} %copy-done.4, bf16[27,128,384]{2,1,0:T(8,128)(2,1)S(1)} %copy-done), custom_call_target="tpu_custom_call" | custom-call | tf_op jit(solution)/shard_map/pallas_call | solution.py:351
  47.4 4.7 %collective-permute-start.5 = (f32[128,128]{1,0:T(8,128)S(1)}, f32[128,128]{1,0:T(8,128)S(1)}, u32[]{:S(2)}, u32[]{:S(2)}) collective-permute-start(f32[128,128]{1,0:T(8,128)S(1)} %get-tuple-element.27), channel_id=1, source_target_pairs={{1,2},{3,4},{5,6},{7,8},{9,10},{11,12},{13,14},{2,1},{4,3},{6,5},{... | collective-permute-start | bytes 196616 | tf_op jit(solution)/shard_map/ppermute | solution.py:319
  52.1 1.9 %collective-permute-done.5.cross_ref = f32[128,128]{1,0:T(8,128)S(1)} collective-permute-done((f32[128,128]{1,0:T(8,128)S(1)}, f32[128,128]{1,0:T(8,128)S(1)}, u32[]{:S(2)}, u32[]{:S(2)}) %collective-permute-start.5) | collective-permute-done | bytes 65568 | tf_op jit(solution)/shard_map/ppermute | solution.py:319
  54.1 16.1 %all-gather = bf16[2048,128]{1,0:T(8,128)(2,1)S(1)} all-gather(bf16[128,128]{1,0:T(8,128)(2,1)S(1)} %shard_map.91), channel_id=2, replica_groups=mesh['dp'=16,'seq'=16] {'seq'}, dimensions={0}, use_global_device_ids=true | all-gather | bytes 557056 | tf_op jit(solution)/shard_map/all_gather | solution.py:361
  70.2 1.3 %shard_map.92 = (f32[8,8,896]{2,1,0:T(8,128)S(1)}, f32[8,8,896]{2,1,0:T(8,128)S(1)}) custom-call(bf16[16,128,128]{2,1,0:T(8,128)(2,1)S(1)} %all-to-all-done.packed_ref, bf16[16,128,128]{2,1,0:T(8,128)(2,1)S(1)} %bitcast.3), custom_call_target="tpu_custom_call" | custom-call | tf_op jit(solution)/shard_map/pallas_call | solution.py:364
  71.5 3.5 %collective-permute-start.6 = (f32[8,8,896]{2,1,0:T(8,128)S(1)}, f32[8,8,896]{2,1,0:T(8,128)S(1)}, u32[]{:S(2)}, u32[]{:S(2)}) collective-permute-start(f32[8,8,896]{2,1,0:T(8,128)S(1)} %get-tuple-element.30), channel_id=1, source_target_pairs={{0,32},{16,48},{32,0},{48,16},{64,96},{80,112},{96,64},{112,80},{1... | collective-permute-start | bytes 688136 | tf_op jit(solution)/shard_map/ppermute | solution.py:310
  75.0 3.4 %shard_map.97 = bf16[16,48,128]{2,1,0:T(8,128)(2,1)} custom-call(bf16[16,480,128]{2,1,0:T(8,128)(2,1)} %all-to-all-done.1.blocks_ref, f32[8,8,896]{2,1,0:T(8,128)S(1)} %get-tuple-element.29.kept_ref.before_ref), custom_call_target="tpu_custom_call" | custom-call | tf_op jit(solution)/shard_map/pallas_call | solution.py:380
  78.4 7.0 %all-to-all-start.2 = ((bf16[16,48,128]{2,1,0:T(8,128)(2,1)}), bf16[16,48,128]{2,1,0:T(8,128)(2,1)S(1)}, u32[]{:S(2)}, u32[]{:S(2)}) async-start(bf16[16,48,128]{2,1,0:T(8,128)(2,1)} %shard_map.97), calls=%async_computation.2 | async-start | bytes 393216 | tf_op jit(solution)/shard_map/all_to_all | solution.py:306
  85.4 0.6 collective-permute-start.7
  86.1 4.6 %collective-permute-done.7.came_ref = f32[4,8,896]{2,1,0:T(8,128)S(1)} collective-permute-done((f32[4,8,896]{2,1,0:T(8,128)S(1)}, f32[4,8,896]{2,1,0:T(8,128)S(1)}, u32[]{:S(2)}, u32[]{:S(2)}) %collective-permute-start.7) | collective-permute-done | bytes 114720 | tf_op jit(solution)/shard_map/ppermute | solution.py:310
  90.8 3.1 %collective-permute-start.8 = (f32[2,8,896]{2,1,0:T(8,128)S(1)}, f32[2,8,896]{2,1,0:T(8,128)S(1)}, u32[]{:S(2)}, u32[]{:S(2)}) collective-permute-start(f32[2,8,896]{2,1,0:T(8,128)S(1)} %get-tuple-element.34), channel_id=1, source_target_pairs={{0,128},{16,144},{32,160},{48,176},{64,192},{80,208},{96,224},{112... | collective-permute-start | bytes 172040 | tf_op jit(solution)/shard_map/ppermute | solution.py:310
  93.9 2.6 %collective-permute-done.8.came_ref = f32[2,8,896]{2,1,0:T(8,128)S(1)} collective-permute-done((f32[2,8,896]{2,1,0:T(8,128)S(1)}, f32[2,8,896]{2,1,0:T(8,128)S(1)}, u32[]{:S(2)}, u32[]{:S(2)}) %collective-permute-start.8) | collective-permute-done | bytes 57376 | tf_op jit(solution)/shard_map/ppermute | solution.py:310
  96.5 1.6 %collective-permute-start.9 = (f32[1,8,896]{2,1,0:T(8,128)S(1)}, f32[1,8,896]{2,1,0:T(8,128)S(1)}, u32[]{:S(2)}, u32[]{:S(2)}) collective-permute-start(f32[1,8,896]{2,1,0:T(8,128)S(1)} %get-tuple-element.36), channel_id=1, source_target_pairs={{0,64},{16,80},{32,96},{48,112},{64,0},{80,16},{96,32},{112,48},{1... | collective-permute-start | bytes 86024 | tf_op jit(solution)/shard_map/ppermute | solution.py:310
  98.2 2.3 %collective-permute-done.9.came_ref = f32[1,8,896]{2,1,0:T(8,128)S(1)} collective-permute-done((f32[1,8,896]{2,1,0:T(8,128)S(1)}, f32[1,8,896]{2,1,0:T(8,128)S(1)}, u32[]{:S(2)}, u32[]{:S(2)}) %collective-permute-start.9) | collective-permute-done | bytes 28704 | tf_op jit(solution)/shard_map/ppermute | solution.py:310
  100.5 0.7 shard_map.96
  101.4 0.8 copy.9
  (28 shorter events, 0.5 us)
Async XLA Ops:
  3.6 2.0 %copy-start.1 = (bf16[27,512,128]{2,1,0:T(8,128)(2,1)S(1)}, bf16[27,512,128]{2,1,0:T(8,128)(2,1)}, u32[]{:S(2)}) copy-start(bf16[27,512,128]{2,1,0:T(8,128)(2,1)} %weight_ref.3) | copy-start | bytes 10616836
  5.6 12.2 %copy-start.6 = (f32[128]{0:T(128)S(1)}, f32[128]{0:T(128)}, u32[]{:S(2)}) copy-start(f32[128]{0:T(128)} %param.9) | copy-start | bytes 1540
  6.3 11.4 %collective-permute-start = (f32[128,128]{1,0:T(8,128)S(1)}, f32[128,128]{1,0:T(8,128)S(1)}, u32[]{:S(2)}, u32[]{:S(2)}) collective-permute-start(f32[128,128]{1,0:T(8,128)S(1)} %get-tuple-element.20), channel_id=1, source_target_pairs={{0,1},{1,0},{2,3},{3,2},{4,5},{5,4},{6,7},{7,6},{8,9},{9,8},{10,11... | collective-permute-start | bytes 196616 | tf_op jit(solution)/shard_map/ppermute | solution.py:310
  6.4 11.3 %collective-permute-start.1 = (f32[128,128]{1,0:T(8,128)S(1)}, f32[128,128]{1,0:T(8,128)S(1)}, u32[]{:S(2)}, u32[]{:S(2)}) collective-permute-start(f32[128,128]{1,0:T(8,128)S(1)} %get-tuple-element.22), channel_id=1, source_target_pairs={{1,2},{3,4},{5,6},{7,8},{9,10},{11,12},{13,14},{2,1},{4,3},{6,5},{... | collective-permute-start | bytes 196616 | tf_op jit(solution)/shard_map/ppermute | solution.py:319
  10.3 21.8 %all-to-all-start = ((bf16[16,128,128]{2,1,0:T(8,128)(2,1)}), bf16[16,128,128]{2,1,0:T(8,128)(2,1)S(1)}, u32[]{:S(2)}, u32[]{:S(2)}) async-start(bf16[16,128,128]{2,1,0:T(8,128)(2,1)} %shard_map.86.before_ref), calls=%async_computation | async-start | bytes 1048576 | tf_op jit(solution)/shard_map/all_to_all | solution.py:306
  17.7 2.4 %copy-start.7 = (f32[384]{0:T(512)S(1)}, f32[384]{0:T(512)}, u32[]{:S(2)}) copy-start(f32[384]{0:T(512)} %param.11) | copy-start | bytes 4612
  17.7 14.3 %copy-start = (bf16[27,128,384]{2,1,0:T(8,128)(2,1)S(1)}, bf16[27,128,384]{2,1,0:T(8,128)(2,1)}, u32[]{:S(2)}) copy-start(bf16[27,128,384]{2,1,0:T(8,128)(2,1)} %weight_ref.5) | copy-start | bytes 7962628
  17.7 14.3 %copy-start.5 = (s32[1,115]{1,0:T(1,128)S(1)}, s32[1,115]{1,0:T(1,128)}, u32[]{:S(2)}) copy-start(s32[1,115]{1,0:T(1,128)} %index_ref.1) | copy-start | bytes 1384
  17.8 2.4 %collective-permute-start.2 = (bf16[128,128]{1,0:T(8,128)(2,1)S(1)}, bf16[128,128]{1,0:T(8,128)(2,1)S(1)}, u32[]{:S(2)}, u32[]{:S(2)}) collective-permute-start(bf16[128,128]{1,0:T(8,128)(2,1)S(1)} %get-tuple-element.23.here_ref), channel_id=1, source_target_pairs={{0,1},{1,0},{2,3},{3,2},{4,5},{5,4},{6,7},{7,6},{8,9},{9,8},{10,11... | collective-permute-start | bytes 98312 | tf_op jit(solution)/shard_map/ppermute | solution.py:310
  18.0 12.1 %collective-permute-start.3 = (bf16[128,128]{1,0:T(8,128)(2,1)S(1)}, bf16[128,128]{1,0:T(8,128)(2,1)S(1)}, u32[]{:S(2)}, u32[]{:S(2)}) collective-permute-start(bf16[128,128]{1,0:T(8,128)(2,1)S(1)} %get-tuple-element.23.here_ref), channel_id=1, source_target_pairs={{1,2},{3,4},{5,6},{7,8},{9,10},{11,12},{13,14},{2,1},{4,3},{6,5},{... | collective-permute-start | bytes 98312 | tf_op jit(solution)/shard_map/ppermute | solution.py:319
  34.8 1.3 %copy-start.2 = (bf16[16,480,128]{2,1,0:T(8,128)(2,1)}, bf16[16,480,128]{2,1,0:T(8,128)(2,1)S(1)}, u32[]{:S(2)}) copy-start(bf16[16,480,128]{2,1,0:T(8,128)(2,1)S(1)} %get-tuple-element.37) | copy-start | bytes 5898244
  36.0 0.8 copy-start.3
  36.8 38.2 %all-to-all-start.1 = ((bf16[16,480,128]{2,1,0:T(8,128)(2,1)}), bf16[16,480,128]{2,1,0:T(8,128)(2,1)}, u32[]{:S(2)}, u32[]{:S(2)}) async-start(bf16[16,480,128]{2,1,0:T(8,128)(2,1)} %copy-done.2), calls=%async_computation.1 | async-start | bytes 3932160 | tf_op jit(solution)/shard_map/all_to_all | solution.py:306
  43.9 1.0 copy-start.4
  47.3 4.8 %collective-permute-start.4 = (f32[128,128]{1,0:T(8,128)S(1)}, f32[128,128]{1,0:T(8,128)S(1)}, u32[]{:S(2)}, u32[]{:S(2)}) collective-permute-start(f32[128,128]{1,0:T(8,128)S(1)} %get-tuple-element.25), channel_id=1, source_target_pairs={{0,1},{1,0},{2,3},{3,2},{4,5},{5,4},{6,7},{7,6},{8,9},{9,8},{10,11... | collective-permute-start | bytes 196616 | tf_op jit(solution)/shard_map/ppermute | solution.py:310
  47.4 6.7 %collective-permute-start.5 = (f32[128,128]{1,0:T(8,128)S(1)}, f32[128,128]{1,0:T(8,128)S(1)}, u32[]{:S(2)}, u32[]{:S(2)}) collective-permute-start(f32[128,128]{1,0:T(8,128)S(1)} %get-tuple-element.27), channel_id=1, source_target_pairs={{1,2},{3,4},{5,6},{7,8},{9,10},{11,12},{13,14},{2,1},{4,3},{6,5},{... | collective-permute-start | bytes 196616 | tf_op jit(solution)/shard_map/ppermute | solution.py:319
  71.5 13.9 %collective-permute-start.6 = (f32[8,8,896]{2,1,0:T(8,128)S(1)}, f32[8,8,896]{2,1,0:T(8,128)S(1)}, u32[]{:S(2)}, u32[]{:S(2)}) collective-permute-start(f32[8,8,896]{2,1,0:T(8,128)S(1)} %get-tuple-element.30), channel_id=1, source_target_pairs={{0,32},{16,48},{32,0},{48,16},{64,96},{80,112},{96,64},{112,80},{1... | collective-permute-start | bytes 688136 | tf_op jit(solution)/shard_map/ppermute | solution.py:310
  78.4 22.9 %all-to-all-start.2 = ((bf16[16,48,128]{2,1,0:T(8,128)(2,1)}), bf16[16,48,128]{2,1,0:T(8,128)(2,1)S(1)}, u32[]{:S(2)}, u32[]{:S(2)}) async-start(bf16[16,48,128]{2,1,0:T(8,128)(2,1)} %shard_map.97), calls=%async_computation.2 | async-start | bytes 393216 | tf_op jit(solution)/shard_map/all_to_all | solution.py:306
  85.4 5.3 %collective-permute-start.7 = (f32[4,8,896]{2,1,0:T(8,128)S(1)}, f32[4,8,896]{2,1,0:T(8,128)S(1)}, u32[]{:S(2)}, u32[]{:S(2)}) collective-permute-start(f32[4,8,896]{2,1,0:T(8,128)S(1)} %get-tuple-element.32), channel_id=1, source_target_pairs={{0,16},{16,0},{32,48},{48,32},{64,80},{80,64},{96,112},{112,96},{1... | collective-permute-start | bytes 344072 | tf_op jit(solution)/shard_map/ppermute | solution.py:310
  90.8 5.8 %collective-permute-start.8 = (f32[2,8,896]{2,1,0:T(8,128)S(1)}, f32[2,8,896]{2,1,0:T(8,128)S(1)}, u32[]{:S(2)}, u32[]{:S(2)}) collective-permute-start(f32[2,8,896]{2,1,0:T(8,128)S(1)} %get-tuple-element.34), channel_id=1, source_target_pairs={{0,128},{16,144},{32,160},{48,176},{64,192},{80,208},{96,224},{112... | collective-permute-start | bytes 172040 | tf_op jit(solution)/shard_map/ppermute | solution.py:310
  96.5 4.0 %collective-permute-start.9 = (f32[1,8,896]{2,1,0:T(8,128)S(1)}, f32[1,8,896]{2,1,0:T(8,128)S(1)}, u32[]{:S(2)}, u32[]{:S(2)}) collective-permute-start(f32[1,8,896]{2,1,0:T(8,128)S(1)} %get-tuple-element.36), channel_id=1, source_target_pairs={{0,64},{16,80},{32,96},{48,112},{64,0},{80,16},{96,32},{112,48},{1... | collective-permute-start | bytes 86024 | tf_op jit(solution)/shard_map/ppermute | solution.py:310

commit v6 on v5

--- a/solution.py
+++ b/solution.py
@@ -252,7 +252,8 @@
     halved(pairs, level, keep_ref, send_ref)
 
 
-def last_sum(kept_ref, came_ref, out_ref):
+def last_sum(kept_ref, came_ref, before_ref, out_ref):
+    del before_ref
     total = kept_ref[0] + came_ref[0]
     width = out_ref.shape[2]
     for k in range(27):
@@ -322,7 +323,7 @@
 def per_device(tokens, conv_first, bias_first, conv_second, bias_second, pixels, mask_index):
     field = tokens.reshape(POS, D)
     packed = call(
-        packed_inputs, struct((16, CHUNK + D // 16, POS), BF16), spots(VMEM, VMEM)
+        packed_inputs, struct((16, CHUNK + D // 16, POS), BF16), spots(VMEM, VMEM), flops=FLOPS // 10
     )(pixels.reshape(16, 8, 4 * CO), field)
     plane = struct((POS, C1), F32)
     pair, keep, cross = call(
@@ -353,6 +354,7 @@
         (plane, plane, plane),
         spots(VMEM, VMEM),
         [pltpu.VMEM((9, POS + 2 * PAD, 3 * C1), F32)],
+        size=4 << 20,
     )(cot, conv_second)
     blocks = exchange(blocks, "dp")
     grad_z = call(hidden_grads, struct((POS, C1), BF16), spots(*[VMEM] * 4))(
@@ -374,19 +376,21 @@
         keep, send = call(
             partial(half_sum, level), (half, half), spots(VMEM, VMEM)
         )(keep, came)
-    grad_first = call(last_sum, struct((27, C1 // 16, D // 16), F32), spots(VMEM, VMEM))(
-        keep, swapped(send, STEPS[3], "dp")
-    )
     second = call(
         second_grads,
         struct((16, 48, 128), BF16),
         spots(VMEM, pl.ANY),
         [pltpu.VMEM((CO, 16 * POS), BF16), pltpu.VMEM((16 * POS, CO), BF16)],
+        size=4 << 20,
     )(blocks, grad_first_half)
     grad_second = call(summed, struct((27, C1 // 16, CO // 16), F32), spots(VMEM))(
         exchange(second, "seq")
     )
-    return grad_first.transpose(0, 2, 1), grad_second
+    grad_second = grad_second.transpose(1, 2, 0)
+    grad_first = call(last_sum, struct((27, C1 // 16, D // 16), F32), spots(VMEM, VMEM, pl.ANY))(
+        keep, swapped(send, STEPS[3], "dp"), grad_second
+    )
+    return grad_first.transpose(0, 2, 1), grad_second.transpose(2, 0, 1)
 
 
 def solution(mesh):

time: 103 us -> 101 us (0.981)
  local copies, waits for them, and re-layouts: 7.84 us -> 6.51 us
    unnamed x17 -> x18, local copies, waits for them, and re-layouts: 5.8 us -> 4.35 us
  transfers between devices with their start and end apart: 13 -> 13, of which waited for: 6 -> 6; matrix products, arithmetic and copies ran while one was open for 0% -> 0% of each run, Pallas kernels for 8% -> 7%
where the time goes in v6:
time: 101 us
  starting transfers between devices  41.5 us (41%)
  waiting for transfers between devices  23.2 us (23%)
  blocking collectives  16.1 us (16%)
  Pallas kernels  12.4 us (12%)
  local copies, waits for them, and re-layouts  6.51 us (6%)
    all_to_all x3, starting transfers between devices, exchange(): return lax.all_to_all(value, axis, split_axis=0, concat_axis=0, tiled=True)  21.5 us
    all_gather x1, blocking collectives, per_device(): grad_z = lax.all_gather(grad_z, 'seq')  16.1 us
    ppermute x3, waiting for transfers between devices, with_cross(): return lax.ppermute(value, 'seq', swaps + [(j, i) for i, j in swaps])  11.9 us
    ppermute x3, starting transfers between devices, with_cross(): return lax.ppermute(value, 'seq', swaps + [(j, i) for i, j in swaps])  10.7 us
    ppermute x7, waiting for transfers between devices, swapped(): return lax.ppermute(value, axis, [(i, i ^ step) for i in range(16)])  9.35 us
    ppermute x7, starting transfers between devices, swapped(): return lax.ppermute(value, axis, [(i, i ^ step) for i in range(16)])  9.32 us
    unnamed x18, local copies, waits for them, and re-layouts  4.35 us
    pallas_call x1, Pallas kernels, per_device(): call(second_grads, struct((16, 48, 128), BF16), spots(VMEM, pl.ANY), [plt...  3.42 us
  transfers between devices with their start and end apart: 13, of which 6 were waited for; matrix products, arithmetic and copies ran while one was open for 0% of the time, Pallas kernels for 7%

profile of v6, /device:TPU:32, one launch (start us, length us, event | category | flops | bytes accessed | tf_op | source)
XLA Modules:
  0.0 100.6 jit_solution(4079753913778391511)
XLA Ops:
  0.6 1.1 %reshape.10.pixel_ref = bf16[16,8,1536]{2,1,0:T(8,128)(2,1)S(1)} reshape(bf16[1,16,2,4,1536]{4,3,2,1,0:T(4,128)(2,1)} %param.12) | data formatting | bytes 786432 | tf_op jit(solution)/shard_map/reshape | solution.py:327
  1.7 0.9 reshape.11.tokens_ref
  2.7 0.9 shard_map.86.before_ref
  3.6 1.3 %copy-done.1 = bf16[27,512,128]{2,1,0:T(8,128)(2,1)S(1)} copy-done((bf16[27,512,128]{2,1,0:T(8,128)(2,1)S(1)}, bf16[27,512,128]{2,1,0:T(8,128)(2,1)}, u32[]{:S(2)}) %copy-start.1) | copy-done | bytes 3538968
  4.9 0.8 shard_map.87
  5.7 3.8 %collective-permute-start.1 = (f32[128,128]{1,0:T(8,128)S(1)}, f32[128,128]{1,0:T(8,128)S(1)}, u32[]{:S(2)}, u32[]{:S(2)}) collective-permute-start(f32[128,128]{1,0:T(8,128)S(1)} %get-tuple-element.22), channel_id=1, source_target_pairs={{1,2},{3,4},{5,6},{7,8},{9,10},{11,12},{13,14},{2,1},{4,3},{6,5},{... | collective-permute-start | bytes 196616 | tf_op jit(solution)/shard_map/ppermute | solution.py:320
  9.6 7.4 %all-to-all-start = ((bf16[16,128,128]{2,1,0:T(8,128)(2,1)}), bf16[16,128,128]{2,1,0:T(8,128)(2,1)S(1)}, u32[]{:S(2)}, u32[]{:S(2)}) async-start(bf16[16,128,128]{2,1,0:T(8,128)(2,1)} %shard_map.86.before_ref), calls=%async_computation | async-start | bytes 1048576 | tf_op jit(solution)/shard_map/all_to_all | solution.py:307
  17.1 0.2 collective-permute-start.2
  17.3 2.1 %collective-permute-start.3 = (bf16[128,128]{1,0:T(8,128)(2,1)S(1)}, bf16[128,128]{1,0:T(8,128)(2,1)S(1)}, u32[]{:S(2)}, u32[]{:S(2)}) collective-permute-start(bf16[128,128]{1,0:T(8,128)(2,1)S(1)} %get-tuple-element.23.here_ref), channel_id=1, source_target_pairs={{1,2},{3,4},{5,6},{7,8},{9,10},{11,12},{13,14},{2,1},{4,3},{6,5},{... | collective-permute-start | bytes 98312 | tf_op jit(solution)/shard_map/ppermute | solution.py:320
  19.5 9.9 %collective-permute-done.3.cross_ref = bf16[128,128]{1,0:T(8,128)(2,1)S(1)} collective-permute-done((bf16[128,128]{1,0:T(8,128)(2,1)S(1)}, bf16[128,128]{1,0:T(8,128)(2,1)S(1)}, u32[]{:S(2)}, u32[]{:S(2)}) %collective-permute-start.3) | collective-permute-done | bytes 32800 | tf_op jit(solution)/shard_map/ppermute | solution.py:320
  29.4 1.9 %all-to-all-done.packed_ref = bf16[16,128,128]{2,1,0:T(8,128)(2,1)S(1)} async-done(((bf16[16,128,128]{2,1,0:T(8,128)(2,1)}), bf16[16,128,128]{2,1,0:T(8,128)(2,1)S(1)}, u32[]{:S(2)}, u32[]{:S(2)}) %all-to-all-start) | async-done | bytes 524320 | tf_op jit(solution)/shard_map/all_to_all | solution.py:307
  31.4 2.7 %shard_map.89 = (bf16[16,480,128]{2,1,0:T(8,128)(2,1)S(1)}, bf16[512,384]{1,0:T(8,128)(2,1)S(1)}) custom-call(bf16[128,128]{1,0:T(8,128)(2,1)S(1)} %collective-permute-done.2.pair_ref, bf16[128,128]{1,0:T(8,128)(2,1)S(1)} %get-tuple-element.23.here_ref, bf16[128,128]{1,0:T(8,128)(2,1)S(1)} %collective-permute-done.3.cross_ref, ...), custom_call_target="tpu_custom_call" | custom-call | tf_op jit(solution)/shard_map/pallas_call | solution.py:343
  34.1 1.3 %copy-done.2 = bf16[16,480,128]{2,1,0:T(8,128)(2,1)} copy-done((bf16[16,480,128]{2,1,0:T(8,128)(2,1)}, bf16[16,480,128]{2,1,0:T(8,128)(2,1)S(1)}, u32[]{:S(2)}) %copy-start.2) | copy-done | bytes 1966104
  35.4 0.8 copy-done.3
  36.1 7.1 %all-to-all-start.1 = ((bf16[16,480,128]{2,1,0:T(8,128)(2,1)}), bf16[16,480,128]{2,1,0:T(8,128)(2,1)}, u32[]{:S(2)}, u32[]{:S(2)}) async-start(bf16[16,480,128]{2,1,0:T(8,128)(2,1)} %copy-done.2), calls=%async_computation.1 | async-start | bytes 3932160 | tf_op jit(solution)/shard_map/all_to_all | solution.py:307
  43.2 1.0 copy-done.4
  44.2 2.4 %shard_map.90 = (f32[128,128]{1,0:T(8,128)S(1)}, f32[128,128]{1,0:T(8,128)S(1)}, f32[128,128]{1,0:T(8,128)S(1)}) custom-call(bf16[512,384]{1,0:T(8,128)(2,1)S(1)} %copy-done.4, bf16[27,128,384]{2,1,0:T(8,128)(2,1)S(1)} %copy-done), custom_call_target="tpu_custom_call" | custom-call | bytes 4194304 | tf_op jit(solution)/shard_map/pallas_call | solution.py:352
  46.7 4.7 %collective-permute-start.5 = (f32[128,128]{1,0:T(8,128)S(1)}, f32[128,128]{1,0:T(8,128)S(1)}, u32[]{:S(2)}, u32[]{:S(2)}) collective-permute-start(f32[128,128]{1,0:T(8,128)S(1)} %get-tuple-element.27), channel_id=1, source_target_pairs={{1,2},{3,4},{5,6},{7,8},{9,10},{11,12},{13,14},{2,1},{4,3},{6,5},{... | collective-permute-start | bytes 196616 | tf_op jit(solution)/shard_map/ppermute | solution.py:320
  51.4 1.9 %collective-permute-done.5.cross_ref = f32[128,128]{1,0:T(8,128)S(1)} collective-permute-done((f32[128,128]{1,0:T(8,128)S(1)}, f32[128,128]{1,0:T(8,128)S(1)}, u32[]{:S(2)}, u32[]{:S(2)}) %collective-permute-start.5) | collective-permute-done | bytes 65568 | tf_op jit(solution)/shard_map/ppermute | solution.py:320
  53.4 16.1 %all-gather = bf16[2048,128]{1,0:T(8,128)(2,1)S(1)} all-gather(bf16[128,128]{1,0:T(8,128)(2,1)S(1)} %shard_map.91), channel_id=2, replica_groups=mesh['dp'=16,'seq'=16] {'seq'}, dimensions={0}, use_global_device_ids=true | all-gather | bytes 557056 | tf_op jit(solution)/shard_map/all_gather | solution.py:363
  69.5 1.3 %shard_map.92 = (f32[8,8,896]{2,1,0:T(8,128)S(1)}, f32[8,8,896]{2,1,0:T(8,128)S(1)}) custom-call(bf16[16,128,128]{2,1,0:T(8,128)(2,1)S(1)} %all-to-all-done.packed_ref, bf16[16,128,128]{2,1,0:T(8,128)(2,1)S(1)} %bitcast.4), custom_call_target="tpu_custom_call" | custom-call | tf_op jit(solution)/shard_map/pallas_call | solution.py:366
  70.8 3.5 %collective-permute-start.6 = (f32[8,8,896]{2,1,0:T(8,128)S(1)}, f32[8,8,896]{2,1,0:T(8,128)S(1)}, u32[]{:S(2)}, u32[]{:S(2)}) collective-permute-start(f32[8,8,896]{2,1,0:T(8,128)S(1)} %get-tuple-element.30), channel_id=1, source_target_pairs={{0,32},{16,48},{32,0},{48,16},{64,96},{80,112},{96,64},{112,80},{1... | collective-permute-start | bytes 688136 | tf_op jit(solution)/shard_map/ppermute | solution.py:311
  74.3 3.4 %shard_map.96 = bf16[16,48,128]{2,1,0:T(8,128)(2,1)} custom-call(bf16[16,480,128]{2,1,0:T(8,128)(2,1)} %all-to-all-done.1.blocks_ref, f32[8,8,896]{2,1,0:T(8,128)S(1)} %get-tuple-element.29.kept_ref.before_ref), custom_call_target="tpu_custom_call" | custom-call | bytes 4194304 | tf_op jit(solution)/shard_map/pallas_call | solution.py:379
  77.7 7.0 %all-to-all-start.2 = ((bf16[16,48,128]{2,1,0:T(8,128)(2,1)}), bf16[16,48,128]{2,1,0:T(8,128)(2,1)S(1)}, u32[]{:S(2)}, u32[]{:S(2)}) async-start(bf16[16,48,128]{2,1,0:T(8,128)(2,1)} %shard_map.96), calls=%async_computation.2 | async-start | bytes 393216 | tf_op jit(solution)/shard_map/all_to_all | solution.py:307
  84.8 0.6 collective-permute-start.7
  85.4 4.6 %collective-permute-done.7.came_ref = f32[4,8,896]{2,1,0:T(8,128)S(1)} collective-permute-done((f32[4,8,896]{2,1,0:T(8,128)S(1)}, f32[4,8,896]{2,1,0:T(8,128)S(1)}, u32[]{:S(2)}, u32[]{:S(2)}) %collective-permute-start.7) | collective-permute-done | bytes 114720 | tf_op jit(solution)/shard_map/ppermute | solution.py:311
  90.1 3.1 %collective-permute-start.8 = (f32[2,8,896]{2,1,0:T(8,128)S(1)}, f32[2,8,896]{2,1,0:T(8,128)S(1)}, u32[]{:S(2)}, u32[]{:S(2)}) collective-permute-start(f32[2,8,896]{2,1,0:T(8,128)S(1)} %get-tuple-element.34), channel_id=1, source_target_pairs={{0,128},{16,144},{32,160},{48,176},{64,192},{80,208},{96,224},{112... | collective-permute-start | bytes 172040 | tf_op jit(solution)/shard_map/ppermute | solution.py:311
  93.2 2.6 %collective-permute-done.8.came_ref = f32[2,8,896]{2,1,0:T(8,128)S(1)} collective-permute-done((f32[2,8,896]{2,1,0:T(8,128)S(1)}, f32[2,8,896]{2,1,0:T(8,128)S(1)}, u32[]{:S(2)}, u32[]{:S(2)}) %collective-permute-start.8) | collective-permute-done | bytes 57376 | tf_op jit(solution)/shard_map/ppermute | solution.py:311
  95.9 1.6 %collective-permute-start.9 = (f32[1,8,896]{2,1,0:T(8,128)S(1)}, f32[1,8,896]{2,1,0:T(8,128)S(1)}, u32[]{:S(2)}, u32[]{:S(2)}) collective-permute-start(f32[1,8,896]{2,1,0:T(8,128)S(1)} %get-tuple-element.36), channel_id=1, source_target_pairs={{0,64},{16,80},{32,96},{48,112},{64,0},{80,16},{96,32},{112,48},{1... | collective-permute-start | bytes 86024 | tf_op jit(solution)/shard_map/ppermute | solution.py:311
  97.6 0.1 copy.9
  97.8 2.1 %collective-permute-done.9.came_ref = f32[1,8,896]{2,1,0:T(8,128)S(1)} collective-permute-done((f32[1,8,896]{2,1,0:T(8,128)S(1)}, f32[1,8,896]{2,1,0:T(8,128)S(1)}, u32[]{:S(2)}, u32[]{:S(2)}) %collective-permute-start.9) | collective-permute-done | bytes 28704 | tf_op jit(solution)/shard_map/ppermute | solution.py:311
  99.8 0.7 shard_map.98
  (30 shorter events, 0.5 us)
Async XLA Ops:
  2.7 2.2 %copy-start.1 = (bf16[27,512,128]{2,1,0:T(8,128)(2,1)S(1)}, bf16[27,512,128]{2,1,0:T(8,128)(2,1)}, u32[]{:S(2)}) copy-start(bf16[27,512,128]{2,1,0:T(8,128)(2,1)} %weight_ref.3) | copy-start | bytes 10616836
  4.9 12.2 %copy-start.7 = (f32[128]{0:T(128)S(1)}, f32[128]{0:T(128)}, u32[]{:S(2)}) copy-start(f32[128]{0:T(128)} %param.9) | copy-start | bytes 1540
  5.6 11.4 %collective-permute-start = (f32[128,128]{1,0:T(8,128)S(1)}, f32[128,128]{1,0:T(8,128)S(1)}, u32[]{:S(2)}, u32[]{:S(2)}) collective-permute-start(f32[128,128]{1,0:T(8,128)S(1)} %get-tuple-element.20), channel_id=1, source_target_pairs={{0,1},{1,0},{2,3},{3,2},{4,5},{5,4},{6,7},{7,6},{8,9},{9,8},{10,11... | collective-permute-start | bytes 196616 | tf_op jit(solution)/shard_map/ppermute | solution.py:311
  5.7 11.3 %collective-permute-start.1 = (f32[128,128]{1,0:T(8,128)S(1)}, f32[128,128]{1,0:T(8,128)S(1)}, u32[]{:S(2)}, u32[]{:S(2)}) collective-permute-start(f32[128,128]{1,0:T(8,128)S(1)} %get-tuple-element.22), channel_id=1, source_target_pairs={{1,2},{3,4},{5,6},{7,8},{9,10},{11,12},{13,14},{2,1},{4,3},{6,5},{... | collective-permute-start | bytes 196616 | tf_op jit(solution)/shard_map/ppermute | solution.py:320
  9.6 21.8 %all-to-all-start = ((bf16[16,128,128]{2,1,0:T(8,128)(2,1)}), bf16[16,128,128]{2,1,0:T(8,128)(2,1)S(1)}, u32[]{:S(2)}, u32[]{:S(2)}) async-start(bf16[16,128,128]{2,1,0:T(8,128)(2,1)} %shard_map.86.before_ref), calls=%async_computation | async-start | bytes 1048576 | tf_op jit(solution)/shard_map/all_to_all | solution.py:307
  17.0 2.4 %copy-start.8 = (f32[384]{0:T(512)S(1)}, f32[384]{0:T(512)}, u32[]{:S(2)}) copy-start(f32[384]{0:T(512)} %param.11) | copy-start | bytes 4612
  17.0 14.3 %copy-start = (bf16[27,128,384]{2,1,0:T(8,128)(2,1)S(1)}, bf16[27,128,384]{2,1,0:T(8,128)(2,1)}, u32[]{:S(2)}) copy-start(bf16[27,128,384]{2,1,0:T(8,128)(2,1)} %weight_ref.5) | copy-start | bytes 7962628
  17.0 14.3 %copy-start.6 = (s32[1,115]{1,0:T(1,128)S(1)}, s32[1,115]{1,0:T(1,128)}, u32[]{:S(2)}) copy-start(s32[1,115]{1,0:T(1,128)} %index_ref.1) | copy-start | bytes 1384
  17.1 2.4 %collective-permute-start.2 = (bf16[128,128]{1,0:T(8,128)(2,1)S(1)}, bf16[128,128]{1,0:T(8,128)(2,1)S(1)}, u32[]{:S(2)}, u32[]{:S(2)}) collective-permute-start(bf16[128,128]{1,0:T(8,128)(2,1)S(1)} %get-tuple-element.23.here_ref), channel_id=1, source_target_pairs={{0,1},{1,0},{2,3},{3,2},{4,5},{5,4},{6,7},{7,6},{8,9},{9,8},{10,11... | collective-permute-start | bytes 98312 | tf_op jit(solution)/shard_map/ppermute | solution.py:311
  17.3 12.1 %collective-permute-start.3 = (bf16[128,128]{1,0:T(8,128)(2,1)S(1)}, bf16[128,128]{1,0:T(8,128)(2,1)S(1)}, u32[]{:S(2)}, u32[]{:S(2)}) collective-permute-start(bf16[128,128]{1,0:T(8,128)(2,1)S(1)} %get-tuple-element.23.here_ref), channel_id=1, source_target_pairs={{1,2},{3,4},{5,6},{7,8},{9,10},{11,12},{13,14},{2,1},{4,3},{6,5},{... | collective-permute-start | bytes 98312 | tf_op jit(solution)/shard_map/ppermute | solution.py:320
  34.1 1.3 %copy-start.2 = (bf16[16,480,128]{2,1,0:T(8,128)(2,1)}, bf16[16,480,128]{2,1,0:T(8,128)(2,1)S(1)}, u32[]{:S(2)}) copy-start(bf16[16,480,128]{2,1,0:T(8,128)(2,1)S(1)} %get-tuple-element.37) | copy-start | bytes 5898244
  35.4 0.8 copy-start.3
  36.1 38.2 %all-to-all-start.1 = ((bf16[16,480,128]{2,1,0:T(8,128)(2,1)}), bf16[16,480,128]{2,1,0:T(8,128)(2,1)}, u32[]{:S(2)}, u32[]{:S(2)}) async-start(bf16[16,480,128]{2,1,0:T(8,128)(2,1)} %copy-done.2), calls=%async_computation.1 | async-start | bytes 3932160 | tf_op jit(solution)/shard_map/all_to_all | solution.py:307
  43.2 1.0 copy-start.4
  46.6 4.8 %collective-permute-start.4 = (f32[128,128]{1,0:T(8,128)S(1)}, f32[128,128]{1,0:T(8,128)S(1)}, u32[]{:S(2)}, u32[]{:S(2)}) collective-permute-start(f32[128,128]{1,0:T(8,128)S(1)} %get-tuple-element.25), channel_id=1, source_target_pairs={{0,1},{1,0},{2,3},{3,2},{4,5},{5,4},{6,7},{7,6},{8,9},{9,8},{10,11... | collective-permute-start | bytes 196616 | tf_op jit(solution)/shard_map/ppermute | solution.py:311
  46.7 6.7 %collective-permute-start.5 = (f32[128,128]{1,0:T(8,128)S(1)}, f32[128,128]{1,0:T(8,128)S(1)}, u32[]{:S(2)}, u32[]{:S(2)}) collective-permute-start(f32[128,128]{1,0:T(8,128)S(1)} %get-tuple-element.27), channel_id=1, source_target_pairs={{1,2},{3,4},{5,6},{7,8},{9,10},{11,12},{13,14},{2,1},{4,3},{6,5},{... | collective-permute-start | bytes 196616 | tf_op jit(solution)/shard_map/ppermute | solution.py:320
  70.8 13.9 %collective-permute-start.6 = (f32[8,8,896]{2,1,0:T(8,128)S(1)}, f32[8,8,896]{2,1,0:T(8,128)S(1)}, u32[]{:S(2)}, u32[]{:S(2)}) collective-permute-start(f32[8,8,896]{2,1,0:T(8,128)S(1)} %get-tuple-element.30), channel_id=1, source_target_pairs={{0,32},{16,48},{32,0},{48,16},{64,96},{80,112},{96,64},{112,80},{1... | collective-permute-start | bytes 688136 | tf_op jit(solution)/shard_map/ppermute | solution.py:311
  77.7 19.8 %all-to-all-start.2 = ((bf16[16,48,128]{2,1,0:T(8,128)(2,1)}), bf16[16,48,128]{2,1,0:T(8,128)(2,1)S(1)}, u32[]{:S(2)}, u32[]{:S(2)}) async-start(bf16[16,48,128]{2,1,0:T(8,128)(2,1)} %shard_map.96), calls=%async_computation.2 | async-start | bytes 393216 | tf_op jit(solution)/shard_map/all_to_all | solution.py:307
  84.8 5.3 %collective-permute-start.7 = (f32[4,8,896]{2,1,0:T(8,128)S(1)}, f32[4,8,896]{2,1,0:T(8,128)S(1)}, u32[]{:S(2)}, u32[]{:S(2)}) collective-permute-start(f32[4,8,896]{2,1,0:T(8,128)S(1)} %get-tuple-element.32), channel_id=1, source_target_pairs={{0,16},{16,0},{32,48},{48,32},{64,80},{80,64},{96,112},{112,96},{1... | collective-permute-start | bytes 344072 | tf_op jit(solution)/shard_map/ppermute | solution.py:311
  90.1 5.8 %collective-permute-start.8 = (f32[2,8,896]{2,1,0:T(8,128)S(1)}, f32[2,8,896]{2,1,0:T(8,128)S(1)}, u32[]{:S(2)}, u32[]{:S(2)}) collective-permute-start(f32[2,8,896]{2,1,0:T(8,128)S(1)} %get-tuple-element.34), channel_id=1, source_target_pairs={{0,128},{16,144},{32,160},{48,176},{64,192},{80,208},{96,224},{112... | collective-permute-start | bytes 172040 | tf_op jit(solution)/shard_map/ppermute | solution.py:311
  95.9 4.0 %collective-permute-start.9 = (f32[1,8,896]{2,1,0:T(8,128)S(1)}, f32[1,8,896]{2,1,0:T(8,128)S(1)}, u32[]{:S(2)}, u32[]{:S(2)}) collective-permute-start(f32[1,8,896]{2,1,0:T(8,128)S(1)} %get-tuple-element.36), channel_id=1, source_target_pairs={{0,64},{16,80},{32,96},{48,112},{64,0},{80,16},{96,32},{112,48},{1... | collective-permute-start | bytes 86024 | tf_op jit(solution)/shard_map/ppermute | solution.py:311
  97.8 2.8 %copy-start.5 = (f32[27,8,24]{0,2,1:T(8,128)}, f32[27,8,24]{0,2,1:T(8,128)S(1)}, u32[]{:S(2)}) copy-start(f32[27,8,24]{0,2,1:T(8,128)S(1)} %copy.9) | copy-start | bytes 62212

commit v7 on v6

--- a/solution.py
+++ b/solution.py
@@ -59,11 +59,13 @@
     return [pl.BlockSpec(memory_space=kind) for kind in kinds]
 
 
-def packed_inputs(pixel_ref, tokens_ref, out_ref):
-    turned = tokens_ref[...].T
+def packed_inputs(pixel_ref, tokens_ref, out_ref, field_ref):
+    tokens = tokens_ref[...].astype(F32).reshape(POS, D).astype(BF16)
+    field_ref[...] = tokens
+    turned = tokens.T
     width = D // 16
     for block in range(16):
-        pix = pixel_ref[block].astype(F32)
+        pix = pixel_ref[block].astype(F32).reshape(8, 4 * CO)
         out_ref[block, 0:CHUNK] = jnp.concatenate(
             [pix[:, n * 128 : (n + 1) * 128] for n in range(4 * CO // 128)], axis=0
         ).astype(BF16)
@@ -198,8 +200,16 @@
     out_ref[...] = jax.vjp(gelu_tanh, zsum_ref[...])[1](grad)[0].astype(BF16)
 
 
-def second_grads(blocks_ref, before_ref, out_ref, left, right):
+def second_grads(source_ref, before_ref, out_ref, left, right, blocks_ref, sems):
     del before_ref
+    copies = [
+        pltpu.make_async_copy(
+            source_ref.at[4 * n : 4 * n + 4], blocks_ref.at[4 * n : 4 * n + 4], sems.at[n]
+        )
+        for n in range(4)
+    ]
+    for copy in copies:
+        copy.start()
     wide, thin = CO // 16, C1 // 16
     masks = {}
     for row in (-1, 0, 1):
@@ -207,6 +217,8 @@
             masks[(row, col)] = spot_mask(row, col, (1, POS), 1)
     for clip in range(16):
         lanes = slice(clip * POS, (clip + 1) * POS)
+        if clip % 4 == 0:
+            copies[clip // 4].wait()
         value = blocks_ref[clip, 0:CHUNK].astype(F32)
         parts = []
         for row, i in PAIRS:
@@ -321,10 +333,12 @@
 
 
 def per_device(tokens, conv_first, bias_first, conv_second, bias_second, pixels, mask_index):
-    field = tokens.reshape(POS, D)
-    packed = call(
-        packed_inputs, struct((16, CHUNK + D // 16, POS), BF16), spots(VMEM, VMEM), flops=FLOPS // 10
-    )(pixels.reshape(16, 8, 4 * CO), field)
+    packed, field = call(
+        packed_inputs,
+        (struct((16, CHUNK + D // 16, POS), BF16), struct((POS, D), BF16)),
+        spots(VMEM, VMEM),
+        flops=FLOPS // 10,
+    )(pixels[0], tokens[0, 0])
     plane = struct((POS, C1), F32)
     pair, keep, cross = call(
         first_conv,
@@ -379,8 +393,13 @@
     second = call(
         second_grads,
         struct((16, 48, 128), BF16),
-        spots(VMEM, pl.ANY),
-        [pltpu.VMEM((CO, 16 * POS), BF16), pltpu.VMEM((16 * POS, CO), BF16)],
+        spots(pl.ANY, pl.ANY),
+        [
+            pltpu.VMEM((CO, 16 * POS), BF16),
+            pltpu.VMEM((16 * POS, CO), BF16),
+            pltpu.VMEM((16, CHUNK + 3 * POS, POS), BF16),
+            pltpu.SemaphoreType.DMA((4,)),
+        ],
         size=4 << 20,
     )(blocks, grad_first_half)
     grad_second = call(summed, struct((27, C1 // 16, CO // 16), F32), spots(VMEM))(

time: 101 us -> 101 us (level)
    reshape x2 -> x0, local copies, waits for them, and re-layouts: 2.03 us -> none  [the longest x1 1.09 us: per_device(): pixels.reshape(16, 8, 4 * CO)]
    unnamed x18 -> x22, local copies, waits for them, and re-layouts: 4.35 us -> 6.23 us
where the time goes in v7:
time: 101 us
  starting transfers between devices  41.5 us (41%)
  waiting for transfers between devices  23.1 us (23%)
  blocking collectives  16.1 us (16%)
  Pallas kernels  12.6 us (12%)
  local copies, waits for them, and re-layouts  6.36 us (6%)
    all_to_all x3, starting transfers between devices, exchange(): return lax.all_to_all(value, axis, split_axis=0, concat_axis=0, tiled=True)  21.5 us
    all_gather x1, blocking collectives, per_device(): grad_z = lax.all_gather(grad_z, 'seq')  16.1 us
    ppermute x3, waiting for transfers between devices, with_cross(): return lax.ppermute(value, 'seq', swaps + [(j, i) for i, j in swaps])  11.9 us
    ppermute x3, starting transfers between devices, with_cross(): return lax.ppermute(value, 'seq', swaps + [(j, i) for i, j in swaps])  10.6 us
    ppermute x7, starting transfers between devices, swapped(): return lax.ppermute(value, axis, [(i, i ^ step) for i in range(16)])  9.34 us
    ppermute x7, waiting for transfers between devices, swapped(): return lax.ppermute(value, axis, [(i, i ^ step) for i in range(16)])  9.33 us
    unnamed x22, local copies, waits for them, and re-layouts  6.23 us
    pallas_call x1, Pallas kernels, per_device(): call(second_grads, struct((16, 48, 128), BF16), spots(pl.ANY, pl.ANY), [p...  3.55 us
  transfers between devices with their start and end apart: 13, of which 6 were waited for; matrix products, arithmetic and copies ran while one was open for 0% of the time, Pallas kernels for 7%

profile of v7, /device:TPU:32, one launch (start us, length us, event | category | flops | bytes accessed | tf_op | source)
XLA Modules:
  0.0 100.5 jit_solution(3870307825031389868)
XLA Ops:
  0.6 1.0 copy-done.7
  1.6 0.9 copy-done.8
  2.5 0.9 shard_map.86
  3.4 1.3 %copy-done.1 = bf16[27,512,128]{2,1,0:T(8,128)(2,1)S(1)} copy-done((bf16[27,512,128]{2,1,0:T(8,128)(2,1)S(1)}, bf16[27,512,128]{2,1,0:T(8,128)(2,1)}, u32[]{:S(2)}) %copy-start.1) | copy-done | bytes 3538968
  4.7 0.8 shard_map.87
  5.6 3.8 %collective-permute-start.1 = (f32[128,128]{1,0:T(8,128)S(1)}, f32[128,128]{1,0:T(8,128)S(1)}, u32[]{:S(2)}, u32[]{:S(2)}) collective-permute-start(f32[128,128]{1,0:T(8,128)S(1)} %get-tuple-element.26), channel_id=1, source_target_pairs={{1,2},{3,4},{5,6},{7,8},{9,10},{11,12},{13,14},{2,1},{4,3},{6,5},{... | collective-permute-start | bytes 196616 | tf_op jit(solution)/shard_map/ppermute | solution.py:332
  9.4 7.4 %all-to-all-start = ((bf16[16,128,128]{2,1,0:T(8,128)(2,1)}), bf16[16,128,128]{2,1,0:T(8,128)(2,1)S(1)}, u32[]{:S(2)}, u32[]{:S(2)}) async-start(bf16[16,128,128]{2,1,0:T(8,128)(2,1)} %get-tuple-element.22.before_ref), calls=%async_computation | async-start | bytes 1048576 | tf_op jit(solution)/shard_map/all_to_all | solution.py:319
  17.0 0.2 collective-permute-start.2
  17.2 2.1 %collective-permute-start.3 = (bf16[128,128]{1,0:T(8,128)(2,1)S(1)}, bf16[128,128]{1,0:T(8,128)(2,1)S(1)}, u32[]{:S(2)}, u32[]{:S(2)}) collective-permute-start(bf16[128,128]{1,0:T(8,128)(2,1)S(1)} %get-tuple-element.27.here_ref), channel_id=1, source_target_pairs={{1,2},{3,4},{5,6},{7,8},{9,10},{11,12},{13,14},{2,1},{4,3},{6,5},{... | collective-permute-start | bytes 98312 | tf_op jit(solution)/shard_map/ppermute | solution.py:332
  19.3 9.9 %collective-permute-done.3.cross_ref = bf16[128,128]{1,0:T(8,128)(2,1)S(1)} collective-permute-done((bf16[128,128]{1,0:T(8,128)(2,1)S(1)}, bf16[128,128]{1,0:T(8,128)(2,1)S(1)}, u32[]{:S(2)}, u32[]{:S(2)}) %collective-permute-start.3) | collective-permute-done | bytes 32800 | tf_op jit(solution)/shard_map/ppermute | solution.py:332
  29.3 1.9 %all-to-all-done.packed_ref = bf16[16,128,128]{2,1,0:T(8,128)(2,1)S(1)} async-done(((bf16[16,128,128]{2,1,0:T(8,128)(2,1)}), bf16[16,128,128]{2,1,0:T(8,128)(2,1)S(1)}, u32[]{:S(2)}, u32[]{:S(2)}) %all-to-all-start) | async-done | bytes 524320 | tf_op jit(solution)/shard_map/all_to_all | solution.py:319
  31.2 2.7 %shard_map.89 = (bf16[16,480,128]{2,1,0:T(8,128)(2,1)S(1)}, bf16[512,384]{1,0:T(8,128)(2,1)S(1)}) custom-call(bf16[128,128]{1,0:T(8,128)(2,1)S(1)} %collective-permute-done.2.pair_ref, bf16[128,128]{1,0:T(8,128)(2,1)S(1)} %get-tuple-element.27.here_ref, bf16[128,128]{1,0:T(8,128)(2,1)S(1)} %collective-permute-done.3.cross_ref, ...), custom_call_target="tpu_custom_call" | custom-call | tf_op jit(solution)/shard_map/pallas_call | solution.py:357
  33.9 1.3 %copy-done.2 = bf16[16,480,128]{2,1,0:T(8,128)(2,1)} copy-done((bf16[16,480,128]{2,1,0:T(8,128)(2,1)}, bf16[16,480,128]{2,1,0:T(8,128)(2,1)S(1)}, u32[]{:S(2)}) %copy-start.2) | copy-done | bytes 1966104
  35.2 0.8 copy-done.3
  36.0 7.1 %all-to-all-start.1 = ((bf16[16,480,128]{2,1,0:T(8,128)(2,1)}), bf16[16,480,128]{2,1,0:T(8,128)(2,1)}, u32[]{:S(2)}, u32[]{:S(2)}) async-start(bf16[16,480,128]{2,1,0:T(8,128)(2,1)} %copy-done.2), calls=%async_computation.1 | async-start | bytes 3932160 | tf_op jit(solution)/shard_map/all_to_all | solution.py:319
  43.1 1.0 copy-done.4
  44.0 2.4 %shard_map.90 = (f32[128,128]{1,0:T(8,128)S(1)}, f32[128,128]{1,0:T(8,128)S(1)}, f32[128,128]{1,0:T(8,128)S(1)}) custom-call(bf16[512,384]{1,0:T(8,128)(2,1)S(1)} %copy-done.4, bf16[27,128,384]{2,1,0:T(8,128)(2,1)S(1)} %copy-done), custom_call_target="tpu_custom_call" | custom-call | bytes 4194304 | tf_op jit(solution)/shard_map/pallas_call | solution.py:366
  46.5 4.7 %collective-permute-start.5 = (f32[128,128]{1,0:T(8,128)S(1)}, f32[128,128]{1,0:T(8,128)S(1)}, u32[]{:S(2)}, u32[]{:S(2)}) collective-permute-start(f32[128,128]{1,0:T(8,128)S(1)} %get-tuple-element.31), channel_id=1, source_target_pairs={{1,2},{3,4},{5,6},{7,8},{9,10},{11,12},{13,14},{2,1},{4,3},{6,5},{... | collective-permute-start | bytes 196616 | tf_op jit(solution)/shard_map/ppermute | solution.py:332
  51.2 1.9 %collective-permute-done.5.cross_ref = f32[128,128]{1,0:T(8,128)S(1)} collective-permute-done((f32[128,128]{1,0:T(8,128)S(1)}, f32[128,128]{1,0:T(8,128)S(1)}, u32[]{:S(2)}, u32[]{:S(2)}) %collective-permute-start.5) | collective-permute-done | bytes 65568 | tf_op jit(solution)/shard_map/ppermute | solution.py:332
  53.2 16.1 %all-gather = bf16[2048,128]{1,0:T(8,128)(2,1)S(1)} all-gather(bf16[128,128]{1,0:T(8,128)(2,1)S(1)} %shard_map.91), channel_id=2, replica_groups=mesh['dp'=16,'seq'=16] {'seq'}, dimensions={0}, use_global_device_ids=true | all-gather | bytes 557056 | tf_op jit(solution)/shard_map/all_gather | solution.py:377
  69.4 1.3 %shard_map.92 = (f32[8,8,896]{2,1,0:T(8,128)S(1)}, f32[8,8,896]{2,1,0:T(8,128)S(1)}) custom-call(bf16[16,128,128]{2,1,0:T(8,128)(2,1)S(1)} %all-to-all-done.packed_ref, bf16[16,128,128]{2,1,0:T(8,128)(2,1)S(1)} %bitcast.6), custom_call_target="tpu_custom_call" | custom-call | tf_op jit(solution)/shard_map/pallas_call | solution.py:380
  70.6 3.5 %collective-permute-start.6 = (f32[8,8,896]{2,1,0:T(8,128)S(1)}, f32[8,8,896]{2,1,0:T(8,128)S(1)}, u32[]{:S(2)}, u32[]{:S(2)}) collective-permute-start(f32[8,8,896]{2,1,0:T(8,128)S(1)} %get-tuple-element.34), channel_id=1, source_target_pairs={{0,32},{16,48},{32,0},{48,16},{64,96},{80,112},{96,64},{112,80},{1... | collective-permute-start | bytes 688136 | tf_op jit(solution)/shard_map/ppermute | solution.py:323
  74.1 3.6 %shard_map.96 = bf16[16,48,128]{2,1,0:T(8,128)(2,1)} custom-call(bf16[16,480,128]{2,1,0:T(8,128)(2,1)} %all-to-all-done.1.source_ref, f32[8,8,896]{2,1,0:T(8,128)S(1)} %get-tuple-element.33.kept_ref.before_ref), custom_call_target="tpu_custom_call" | custom-call | bytes 4194304 | tf_op jit(solution)/shard_map/pallas_call | solution.py:393
  77.7 7.0 %all-to-all-start.2 = ((bf16[16,48,128]{2,1,0:T(8,128)(2,1)}), bf16[16,48,128]{2,1,0:T(8,128)(2,1)S(1)}, u32[]{:S(2)}, u32[]{:S(2)}) async-start(bf16[16,48,128]{2,1,0:T(8,128)(2,1)} %shard_map.96), calls=%async_computation.2 | async-start | bytes 393216 | tf_op jit(solution)/shard_map/all_to_all | solution.py:319
  84.7 0.7 collective-permute-start.7
  85.4 4.6 %collective-permute-done.7.came_ref = f32[4,8,896]{2,1,0:T(8,128)S(1)} collective-permute-done((f32[4,8,896]{2,1,0:T(8,128)S(1)}, f32[4,8,896]{2,1,0:T(8,128)S(1)}, u32[]{:S(2)}, u32[]{:S(2)}) %collective-permute-start.7) | collective-permute-done | bytes 114720 | tf_op jit(solution)/shard_map/ppermute | solution.py:323
  90.1 3.1 %collective-permute-start.8 = (f32[2,8,896]{2,1,0:T(8,128)S(1)}, f32[2,8,896]{2,1,0:T(8,128)S(1)}, u32[]{:S(2)}, u32[]{:S(2)}) collective-permute-start(f32[2,8,896]{2,1,0:T(8,128)S(1)} %get-tuple-element.38), channel_id=1, source_target_pairs={{0,128},{16,144},{32,160},{48,176},{64,192},{80,208},{96,224},{112... | collective-permute-start | bytes 172040 | tf_op jit(solution)/shard_map/ppermute | solution.py:323
  93.2 2.6 %collective-permute-done.8.came_ref = f32[2,8,896]{2,1,0:T(8,128)S(1)} collective-permute-done((f32[2,8,896]{2,1,0:T(8,128)S(1)}, f32[2,8,896]{2,1,0:T(8,128)S(1)}, u32[]{:S(2)}, u32[]{:S(2)}) %collective-permute-start.8) | collective-permute-done | bytes 57376 | tf_op jit(solution)/shard_map/ppermute | solution.py:323
  95.8 1.6 %collective-permute-start.9 = (f32[1,8,896]{2,1,0:T(8,128)S(1)}, f32[1,8,896]{2,1,0:T(8,128)S(1)}, u32[]{:S(2)}, u32[]{:S(2)}) collective-permute-start(f32[1,8,896]{2,1,0:T(8,128)S(1)} %get-tuple-element.40), channel_id=1, source_target_pairs={{0,64},{16,80},{32,96},{48,112},{64,0},{80,16},{96,32},{112,48},{1... | collective-permute-start | bytes 86024 | tf_op jit(solution)/shard_map/ppermute | solution.py:323
  97.6 0.1 copy.9
  97.8 2.1 %collective-permute-done.9.came_ref = f32[1,8,896]{2,1,0:T(8,128)S(1)} collective-permute-done((f32[1,8,896]{2,1,0:T(8,128)S(1)}, f32[1,8,896]{2,1,0:T(8,128)S(1)}, u32[]{:S(2)}, u32[]{:S(2)}) %collective-permute-start.9) | collective-permute-done | bytes 28704 | tf_op jit(solution)/shard_map/ppermute | solution.py:323
  99.8 0.7 shard_map.98
  (32 shorter events, 0.5 us)
Async XLA Ops:
  0.6 1.0 copy-start.7
  1.6 0.9 copy-start.8
  2.5 2.2 %copy-start.1 = (bf16[27,512,128]{2,1,0:T(8,128)(2,1)S(1)}, bf16[27,512,128]{2,1,0:T(8,128)(2,1)}, u32[]{:S(2)}) copy-start(bf16[27,512,128]{2,1,0:T(8,128)(2,1)} %weight_ref.3) | copy-start | bytes 10616836
  3.4 13.5 %copy-start.9 = (f32[128]{0:T(128)S(1)}, f32[128]{0:T(128)}, u32[]{:S(2)}) copy-start(f32[128]{0:T(128)} %param.9) | copy-start | bytes 1540
  5.5 11.4 %collective-permute-start = (f32[128,128]{1,0:T(8,128)S(1)}, f32[128,128]{1,0:T(8,128)S(1)}, u32[]{:S(2)}, u32[]{:S(2)}) collective-permute-start(f32[128,128]{1,0:T(8,128)S(1)} %get-tuple-element.24), channel_id=1, source_target_pairs={{0,1},{1,0},{2,3},{3,2},{4,5},{5,4},{6,7},{7,6},{8,9},{9,8},{10,11... | collective-permute-start | bytes 196616 | tf_op jit(solution)/shard_map/ppermute | solution.py:323
  5.6 11.3 %collective-permute-start.1 = (f32[128,128]{1,0:T(8,128)S(1)}, f32[128,128]{1,0:T(8,128)S(1)}, u32[]{:S(2)}, u32[]{:S(2)}) collective-permute-start(f32[128,128]{1,0:T(8,128)S(1)} %get-tuple-element.26), channel_id=1, source_target_pairs={{1,2},{3,4},{5,6},{7,8},{9,10},{11,12},{13,14},{2,1},{4,3},{6,5},{... | collective-permute-start | bytes 196616 | tf_op jit(solution)/shard_map/ppermute | solution.py:332
  9.4 21.8 %all-to-all-start = ((bf16[16,128,128]{2,1,0:T(8,128)(2,1)}), bf16[16,128,128]{2,1,0:T(8,128)(2,1)S(1)}, u32[]{:S(2)}, u32[]{:S(2)}) async-start(bf16[16,128,128]{2,1,0:T(8,128)(2,1)} %get-tuple-element.22.before_ref), calls=%async_computation | async-start | bytes 1048576 | tf_op jit(solution)/shard_map/all_to_all | solution.py:319
  16.9 2.4 %copy-start.10 = (f32[384]{0:T(512)S(1)}, f32[384]{0:T(512)}, u32[]{:S(2)}) copy-start(f32[384]{0:T(512)} %param.11) | copy-start | bytes 4612
  16.9 14.3 %copy-start = (bf16[27,128,384]{2,1,0:T(8,128)(2,1)S(1)}, bf16[27,128,384]{2,1,0:T(8,128)(2,1)}, u32[]{:S(2)}) copy-start(bf16[27,128,384]{2,1,0:T(8,128)(2,1)} %weight_ref.5) | copy-start | bytes 7962628
  16.9 14.3 %copy-start.6 = (s32[1,115]{1,0:T(1,128)S(1)}, s32[1,115]{1,0:T(1,128)}, u32[]{:S(2)}) copy-start(s32[1,115]{1,0:T(1,128)} %index_ref.1) | copy-start | bytes 1384
  17.0 2.4 %collective-permute-start.2 = (bf16[128,128]{1,0:T(8,128)(2,1)S(1)}, bf16[128,128]{1,0:T(8,128)(2,1)S(1)}, u32[]{:S(2)}, u32[]{:S(2)}) collective-permute-start(bf16[128,128]{1,0:T(8,128)(2,1)S(1)} %get-tuple-element.27.here_ref), channel_id=1, source_target_pairs={{0,1},{1,0},{2,3},{3,2},{4,5},{5,4},{6,7},{7,6},{8,9},{9,8},{10,11... | collective-permute-start | bytes 98312 | tf_op jit(solution)/shard_map/ppermute | solution.py:323
  17.2 12.1 %collective-permute-start.3 = (bf16[128,128]{1,0:T(8,128)(2,1)S(1)}, bf16[128,128]{1,0:T(8,128)(2,1)S(1)}, u32[]{:S(2)}, u32[]{:S(2)}) collective-permute-start(bf16[128,128]{1,0:T(8,128)(2,1)S(1)} %get-tuple-element.27.here_ref), channel_id=1, source_target_pairs={{1,2},{3,4},{5,6},{7,8},{9,10},{11,12},{13,14},{2,1},{4,3},{6,5},{... | collective-permute-start | bytes 98312 | tf_op jit(solution)/shard_map/ppermute | solution.py:332
  33.9 1.3 %copy-start.2 = (bf16[16,480,128]{2,1,0:T(8,128)(2,1)}, bf16[16,480,128]{2,1,0:T(8,128)(2,1)S(1)}, u32[]{:S(2)}) copy-start(bf16[16,480,128]{2,1,0:T(8,128)(2,1)S(1)} %get-tuple-element.41) | copy-start | bytes 5898244
  35.2 0.8 copy-start.3
  36.0 38.2 %all-to-all-start.1 = ((bf16[16,480,128]{2,1,0:T(8,128)(2,1)}), bf16[16,480,128]{2,1,0:T(8,128)(2,1)}, u32[]{:S(2)}, u32[]{:S(2)}) async-start(bf16[16,480,128]{2,1,0:T(8,128)(2,1)} %copy-done.2), calls=%async_computation.1 | async-start | bytes 3932160 | tf_op jit(solution)/shard_map/all_to_all | solution.py:319
  43.0 1.0 copy-start.4
  46.4 4.8 %collective-permute-start.4 = (f32[128,128]{1,0:T(8,128)S(1)}, f32[128,128]{1,0:T(8,128)S(1)}, u32[]{:S(2)}, u32[]{:S(2)}) collective-permute-start(f32[128,128]{1,0:T(8,128)S(1)} %get-tuple-element.29), channel_id=1, source_target_pairs={{0,1},{1,0},{2,3},{3,2},{4,5},{5,4},{6,7},{7,6},{8,9},{9,8},{10,11... | collective-permute-start | bytes 196616 | tf_op jit(solution)/shard_map/ppermute | solution.py:323
  46.5 6.6 %collective-permute-start.5 = (f32[128,128]{1,0:T(8,128)S(1)}, f32[128,128]{1,0:T(8,128)S(1)}, u32[]{:S(2)}, u32[]{:S(2)}) collective-permute-start(f32[128,128]{1,0:T(8,128)S(1)} %get-tuple-element.31), channel_id=1, source_target_pairs={{1,2},{3,4},{5,6},{7,8},{9,10},{11,12},{13,14},{2,1},{4,3},{6,5},{... | collective-permute-start | bytes 196616 | tf_op jit(solution)/shard_map/ppermute | solution.py:332
  70.6 14.1 %collective-permute-start.6 = (f32[8,8,896]{2,1,0:T(8,128)S(1)}, f32[8,8,896]{2,1,0:T(8,128)S(1)}, u32[]{:S(2)}, u32[]{:S(2)}) collective-permute-start(f32[8,8,896]{2,1,0:T(8,128)S(1)} %get-tuple-element.34), channel_id=1, source_target_pairs={{0,32},{16,48},{32,0},{48,16},{64,96},{80,112},{96,64},{112,80},{1... | collective-permute-start | bytes 688136 | tf_op jit(solution)/shard_map/ppermute | solution.py:323
  77.7 19.8 %all-to-all-start.2 = ((bf16[16,48,128]{2,1,0:T(8,128)(2,1)}), bf16[16,48,128]{2,1,0:T(8,128)(2,1)S(1)}, u32[]{:S(2)}, u32[]{:S(2)}) async-start(bf16[16,48,128]{2,1,0:T(8,128)(2,1)} %shard_map.96), calls=%async_computation.2 | async-start | bytes 393216 | tf_op jit(solution)/shard_map/all_to_all | solution.py:319
  84.7 5.3 %collective-permute-start.7 = (f32[4,8,896]{2,1,0:T(8,128)S(1)}, f32[4,8,896]{2,1,0:T(8,128)S(1)}, u32[]{:S(2)}, u32[]{:S(2)}) collective-permute-start(f32[4,8,896]{2,1,0:T(8,128)S(1)} %get-tuple-element.36), channel_id=1, source_target_pairs={{0,16},{16,0},{32,48},{48,32},{64,80},{80,64},{96,112},{112,96},{1... | collective-permute-start | bytes 344072 | tf_op jit(solution)/shard_map/ppermute | solution.py:323
  90.1 5.8 %collective-permute-start.8 = (f32[2,8,896]{2,1,0:T(8,128)S(1)}, f32[2,8,896]{2,1,0:T(8,128)S(1)}, u32[]{:S(2)}, u32[]{:S(2)}) collective-permute-start(f32[2,8,896]{2,1,0:T(8,128)S(1)} %get-tuple-element.38), channel_id=1, source_target_pairs={{0,128},{16,144},{32,160},{48,176},{64,192},{80,208},{96,224},{112... | collective-permute-start | bytes 172040 | tf_op jit(solution)/shard_map/ppermute | solution.py:323
  95.8 4.0 %collective-permute-start.9 = (f32[1,8,896]{2,1,0:T(8,128)S(1)}, f32[1,8,896]{2,1,0:T(8,128)S(1)}, u32[]{:S(2)}, u32[]{:S(2)}) collective-permute-start(f32[1,8,896]{2,1,0:T(8,128)S(1)} %get-tuple-element.40), channel_id=1, source_target_pairs={{0,64},{16,80},{32,96},{48,112},{64,0},{80,16},{96,32},{112,48},{1... | collective-permute-start | bytes 86024 | tf_op jit(solution)/shard_map/ppermute | solution.py:323
  97.7 2.8 %copy-start.5 = (f32[27,8,24]{0,2,1:T(8,128)}, f32[27,8,24]{0,2,1:T(8,128)S(1)}, u32[]{:S(2)}) copy-start(f32[27,8,24]{0,2,1:T(8,128)S(1)} %copy.9) | copy-start | bytes 62212

commit v8 on v6

--- a/solution.py
+++ b/solution.py
@@ -59,11 +59,23 @@
     return [pl.BlockSpec(memory_space=kind) for kind in kinds]
 
 
-def packed_inputs(pixel_ref, tokens_ref, out_ref):
-    turned = tokens_ref[...].T
+def packed_inputs(pixel_source, tokens_source, out_ref, field_ref, pixel_ref, tokens_ref, sems):
+    copies = [
+        pltpu.make_async_copy(source, target, sems.at[n])
+        for n, (source, target) in enumerate(
+            ((tokens_source, tokens_ref), (pixel_source, pixel_ref))
+        )
+    ]
+    for copy in copies:
+        copy.start()
+    copies[0].wait()
+    tokens = tokens_ref[...].astype(F32).reshape(POS, D).astype(BF16)
+    field_ref[...] = tokens
+    turned = tokens.T
     width = D // 16
+    copies[1].wait()
     for block in range(16):
-        pix = pixel_ref[block].astype(F32)
+        pix = pixel_ref[block].astype(F32).reshape(8, 4 * CO)
         out_ref[block, 0:CHUNK] = jnp.concatenate(
             [pix[:, n * 128 : (n + 1) * 128] for n in range(4 * CO // 128)], axis=0
         ).astype(BF16)
@@ -183,7 +195,7 @@
     bit = lax.axis_index("dp") // STEPS[level] % 2
     for at, (zero, one) in enumerate(pairs):
         keep_ref[at] = jnp.where(bit == 0, zero, one)
-        send_ref[at] = jnp.where(bit == 0, one, zero)
+        send_ref[at] = jnp.where(bit == 0, one, zero).astype(send_ref.dtype)
 
 
 def hidden_values(pair_ref, keep_ref, cross_ref, bias_ref, zsum_ref, hidden_ref):
@@ -246,7 +258,7 @@
 
 def half_sum(level, kept_ref, came_ref, keep_ref, send_ref):
     pairs = [
-        tuple(kept_ref[at] + came_ref[at] for at in (two, two + 1))
+        tuple(kept_ref[at] + came_ref[at].astype(F32) for at in (two, two + 1))
         for two in range(0, kept_ref.shape[0], 2)
     ]
     halved(pairs, level, keep_ref, send_ref)
@@ -321,10 +333,18 @@
 
 
 def per_device(tokens, conv_first, bias_first, conv_second, bias_second, pixels, mask_index):
-    field = tokens.reshape(POS, D)
-    packed = call(
-        packed_inputs, struct((16, CHUNK + D // 16, POS), BF16), spots(VMEM, VMEM), flops=FLOPS // 10
-    )(pixels.reshape(16, 8, 4 * CO), field)
+    packed, field = call(
+        packed_inputs,
+        (struct((16, CHUNK + D // 16, POS), BF16), struct((POS, D), BF16)),
+        spots(pltpu.HBM, pltpu.HBM),
+        [
+            pltpu.VMEM((16, 2, 4, 4 * CO), BF16),
+            pltpu.VMEM((32, 4, D), BF16),
+            pltpu.SemaphoreType.DMA((2,)),
+        ],
+        flops=FLOPS // 10,
+        limit=56,
+    )(pixels[0], tokens[0, 0])
     plane = struct((POS, C1), F32)
     pair, keep, cross = call(
         first_conv,
@@ -373,8 +393,9 @@
     for level in (1, 2, 3):
         half = struct((8 >> level, C1 // 16, 7 * 128), F32)
         came = swapped(send, STEPS[level - 1], "dp")
+        sent = struct(half.shape, BF16 if level == 1 else F32)
         keep, send = call(
-            partial(half_sum, level), (half, half), spots(VMEM, VMEM)
+            partial(half_sum, level), (half, sent), spots(VMEM, VMEM)
         )(keep, came)
     second = call(
         second_grads,

time: 101 us -> 99.1 us (0.981)
  local copies, waits for them, and re-layouts: 6.51 us -> 4.17 us
  Pallas kernels: 12.4 us -> 13.7 us
  waiting for transfers between devices: 23.2 us -> 22.1 us
    reshape x2 -> x0, local copies, waits for them, and re-layouts: 2.03 us -> none  [the longest x1 1.09 us: per_device(): pixels.reshape(16, 8, 4 * CO)]
    pallas_call x4, Pallas kernels: 0.97 us -> 2.17 us  [the longest x1 2.1 us: per_device(): call(packed_inputs, (struct((16, CHUNK + D // 16, POS), BF16), struct((PO...]
    ppermute x7, waiting for transfers between devices: 9.35 us -> 8.31 us  [swapped(): return lax.ppermute(value, axis, [(i, i ^ step) for i in range(16)])]
    unnamed x18 -> x20, local copies, waits for them, and re-layouts: 4.35 us -> 4.04 us
where the time goes in v8:
time: 99.1 us; the launch traced here: 98.4 us
  starting transfers between devices  41.5 us (42%)
  waiting for transfers between devices  22.1 us (22%)
  blocking collectives  16.1 us (16%)
  Pallas kernels  13.7 us (14%)
  local copies, waits for them, and re-layouts  4.17 us (4%)
    all_to_all x3, starting transfers between devices, exchange(): return lax.all_to_all(value, axis, split_axis=0, concat_axis=0, tiled=True)  21.5 us
    all_gather x1, blocking collectives, per_device(): grad_z = lax.all_gather(grad_z, 'seq')  16.1 us
    ppermute x3, waiting for transfers between devices, with_cross(): return lax.ppermute(value, 'seq', swaps + [(j, i) for i, j in swaps])  11.9 us
    ppermute x3, starting transfers between devices, with_cross(): return lax.ppermute(value, 'seq', swaps + [(j, i) for i, j in swaps])  10.6 us
    ppermute x7, starting transfers between devices, swapped(): return lax.ppermute(value, axis, [(i, i ^ step) for i in range(16)])  9.33 us
    ppermute x7, waiting for transfers between devices, swapped(): return lax.ppermute(value, axis, [(i, i ^ step) for i in range(16)])  8.31 us
    unnamed x20, local copies, waits for them, and re-layouts  4.04 us
    pallas_call x1, Pallas kernels, per_device(): call(second_grads, struct((16, 48, 128), BF16), spots(VMEM, pl.ANY), [plt...  3.43 us
  transfers between devices with their start and end apart: 13, of which 6 were waited for; matrix products, arithmetic and copies ran while one was open for 0% of the time, Pallas kernels for 7%

profile of v8, /device:TPU:32, one launch (start us, length us, event | category | flops | bytes accessed | tf_op | source)
XLA Modules:
  0.0 98.4 jit_solution(16855762760853058274)
XLA Ops:
  0.6 2.1 %shard_map.86 = (bf16[16,128,128]{2,1,0:T(8,128)(2,1)}, bf16[128,512]{1,0:T(8,128)(2,1)}) custom-call(bf16[16,2,4,1536]{3,2,1,0:T(4,128)(2,1)} %bitcast.10, bf16[32,4,512]{2,1,0:T(4,128)(2,1)} %bitcast.11), custom_call_target="tpu_custom_call" | custom-call | flops 4000000000 | tf_op jit(solution)/shard_map/pallas_call | solution.py:336
  2.8 0.9 copy-done.6
  3.7 0.8 shard_map.87
  4.5 0.1 collective-permute-start
  4.6 3.8 %collective-permute-start.1 = (f32[128,128]{1,0:T(8,128)S(1)}, f32[128,128]{1,0:T(8,128)S(1)}, u32[]{:S(2)}, u32[]{:S(2)}) collective-permute-start(f32[128,128]{1,0:T(8,128)S(1)} %get-tuple-element.26), channel_id=1, source_target_pairs={{1,2},{3,4},{5,6},{7,8},{9,10},{11,12},{13,14},{2,1},{4,3},{6,5},{... | collective-permute-start | bytes 196616 | tf_op jit(solution)/shard_map/ppermute | solution.py:332
  8.5 7.4 %all-to-all-start = ((bf16[16,128,128]{2,1,0:T(8,128)(2,1)}), bf16[16,128,128]{2,1,0:T(8,128)(2,1)S(1)}, u32[]{:S(2)}, u32[]{:S(2)}) async-start(bf16[16,128,128]{2,1,0:T(8,128)(2,1)} %get-tuple-element.22.before_ref), calls=%async_computation | async-start | bytes 1048576 | tf_op jit(solution)/shard_map/all_to_all | solution.py:319
  16.0 0.2 collective-permute-start.2
  16.2 2.1 %collective-permute-start.3 = (bf16[128,128]{1,0:T(8,128)(2,1)S(1)}, bf16[128,128]{1,0:T(8,128)(2,1)S(1)}, u32[]{:S(2)}, u32[]{:S(2)}) collective-permute-start(bf16[128,128]{1,0:T(8,128)(2,1)S(1)} %get-tuple-element.27.here_ref), channel_id=1, source_target_pairs={{1,2},{3,4},{5,6},{7,8},{9,10},{11,12},{13,14},{2,1},{4,3},{6,5},{... | collective-permute-start | bytes 98312 | tf_op jit(solution)/shard_map/ppermute | solution.py:332
  18.4 9.9 %collective-permute-done.3.cross_ref = bf16[128,128]{1,0:T(8,128)(2,1)S(1)} collective-permute-done((bf16[128,128]{1,0:T(8,128)(2,1)S(1)}, bf16[128,128]{1,0:T(8,128)(2,1)S(1)}, u32[]{:S(2)}, u32[]{:S(2)}) %collective-permute-start.3) | collective-permute-done | bytes 32800 | tf_op jit(solution)/shard_map/ppermute | solution.py:332
  28.3 1.9 %all-to-all-done.packed_ref = bf16[16,128,128]{2,1,0:T(8,128)(2,1)S(1)} async-done(((bf16[16,128,128]{2,1,0:T(8,128)(2,1)}), bf16[16,128,128]{2,1,0:T(8,128)(2,1)S(1)}, u32[]{:S(2)}, u32[]{:S(2)}) %all-to-all-start) | async-done | bytes 524320 | tf_op jit(solution)/shard_map/all_to_all | solution.py:319
  30.2 2.7 %shard_map.89 = (bf16[16,480,128]{2,1,0:T(8,128)(2,1)S(1)}, bf16[512,384]{1,0:T(8,128)(2,1)S(1)}) custom-call(bf16[128,128]{1,0:T(8,128)(2,1)S(1)} %collective-permute-done.2.pair_ref, bf16[128,128]{1,0:T(8,128)(2,1)S(1)} %get-tuple-element.27.here_ref, bf16[128,128]{1,0:T(8,128)(2,1)S(1)} %collective-permute-done.3.cross_ref, ...), custom_call_target="tpu_custom_call" | custom-call | tf_op jit(solution)/shard_map/pallas_call | solution.py:363
  33.0 1.3 %copy-done.2 = bf16[16,480,128]{2,1,0:T(8,128)(2,1)} copy-done((bf16[16,480,128]{2,1,0:T(8,128)(2,1)}, bf16[16,480,128]{2,1,0:T(8,128)(2,1)S(1)}, u32[]{:S(2)}) %copy-start.2) | copy-done | bytes 1966104
  34.2 0.8 copy-done.3
  35.0 7.1 %all-to-all-start.1 = ((bf16[16,480,128]{2,1,0:T(8,128)(2,1)}), bf16[16,480,128]{2,1,0:T(8,128)(2,1)}, u32[]{:S(2)}, u32[]{:S(2)}) async-start(bf16[16,480,128]{2,1,0:T(8,128)(2,1)} %copy-done.2), calls=%async_computation.1 | async-start | bytes 3932160 | tf_op jit(solution)/shard_map/all_to_all | solution.py:319
  42.1 1.0 %copy-done.4 = bf16[512,384]{1,0:T(8,128)(2,1)S(1)} copy-done((bf16[512,384]{1,0:T(8,128)(2,1)S(1)}, bf16[512,384]{1,0:T(8,128)(2,1)}, u32[]{:S(2)}) %copy-start.4) | copy-done | bytes 393240
  43.1 2.4 %shard_map.90 = (f32[128,128]{1,0:T(8,128)S(1)}, f32[128,128]{1,0:T(8,128)S(1)}, f32[128,128]{1,0:T(8,128)S(1)}) custom-call(bf16[512,384]{1,0:T(8,128)(2,1)S(1)} %copy-done.4, bf16[27,128,384]{2,1,0:T(8,128)(2,1)S(1)} %copy-done), custom_call_target="tpu_custom_call" | custom-call | bytes 4194304 | tf_op jit(solution)/shard_map/pallas_call | solution.py:372
  45.6 4.7 %collective-permute-start.5 = (f32[128,128]{1,0:T(8,128)S(1)}, f32[128,128]{1,0:T(8,128)S(1)}, u32[]{:S(2)}, u32[]{:S(2)}) collective-permute-start(f32[128,128]{1,0:T(8,128)S(1)} %get-tuple-element.31), channel_id=1, source_target_pairs={{1,2},{3,4},{5,6},{7,8},{9,10},{11,12},{13,14},{2,1},{4,3},{6,5},{... | collective-permute-start | bytes 196616 | tf_op jit(solution)/shard_map/ppermute | solution.py:332
  50.3 1.9 %collective-permute-done.5.cross_ref = f32[128,128]{1,0:T(8,128)S(1)} collective-permute-done((f32[128,128]{1,0:T(8,128)S(1)}, f32[128,128]{1,0:T(8,128)S(1)}, u32[]{:S(2)}, u32[]{:S(2)}) %collective-permute-start.5) | collective-permute-done | bytes 65568 | tf_op jit(solution)/shard_map/ppermute | solution.py:332
  52.3 16.1 %all-gather = bf16[2048,128]{1,0:T(8,128)(2,1)S(1)} all-gather(bf16[128,128]{1,0:T(8,128)(2,1)S(1)} %shard_map.91), channel_id=2, replica_groups=mesh['dp'=16,'seq'=16] {'seq'}, dimensions={0}, use_global_device_ids=true | all-gather | bytes 557056 | tf_op jit(solution)/shard_map/all_gather | solution.py:383
  68.4 1.3 %shard_map.92 = (f32[8,8,896]{2,1,0:T(8,128)S(1)}, f32[8,8,896]{2,1,0:T(8,128)S(1)}) custom-call(bf16[16,128,128]{2,1,0:T(8,128)(2,1)S(1)} %all-to-all-done.packed_ref, bf16[16,128,128]{2,1,0:T(8,128)(2,1)S(1)} %bitcast.6), custom_call_target="tpu_custom_call" | custom-call | tf_op jit(solution)/shard_map/pallas_call | solution.py:386
  69.7 3.5 %collective-permute-start.6 = (f32[8,8,896]{2,1,0:T(8,128)S(1)}, f32[8,8,896]{2,1,0:T(8,128)S(1)}, u32[]{:S(2)}, u32[]{:S(2)}) collective-permute-start(f32[8,8,896]{2,1,0:T(8,128)S(1)} %get-tuple-element.34), channel_id=1, source_target_pairs={{0,32},{16,48},{32,0},{48,16},{64,96},{80,112},{96,64},{112,80},{1... | collective-permute-start | bytes 688136 | tf_op jit(solution)/shard_map/ppermute | solution.py:323
  73.1 3.4 %shard_map.96 = bf16[16,48,128]{2,1,0:T(8,128)(2,1)} custom-call(bf16[16,480,128]{2,1,0:T(8,128)(2,1)} %all-to-all-done.1.blocks_ref, f32[8,8,896]{2,1,0:T(8,128)S(1)} %get-tuple-element.33.kept_ref.before_ref), custom_call_target="tpu_custom_call" | custom-call | bytes 4194304 | tf_op jit(solution)/shard_map/pallas_call | solution.py:400
  76.6 7.0 %all-to-all-start.2 = ((bf16[16,48,128]{2,1,0:T(8,128)(2,1)}), bf16[16,48,128]{2,1,0:T(8,128)(2,1)S(1)}, u32[]{:S(2)}, u32[]{:S(2)}) async-start(bf16[16,48,128]{2,1,0:T(8,128)(2,1)} %shard_map.96), calls=%async_computation.2 | async-start | bytes 393216 | tf_op jit(solution)/shard_map/all_to_all | solution.py:319
  83.6 0.7 collective-permute-start.7
  84.3 3.6 %collective-permute-done.7.came_ref = bf16[4,8,896]{2,1,0:T(8,128)(2,1)S(1)} collective-permute-done((bf16[4,8,896]{2,1,0:T(8,128)(2,1)S(1)}, bf16[4,8,896]{2,1,0:T(8,128)(2,1)S(1)}, u32[]{:S(2)}, u32[]{:S(2)}) %collective-permute-start.7) | collective-permute-done | bytes 57376 | tf_op jit(solution)/shard_map/ppermute | solution.py:323
  87.9 3.1 %collective-permute-start.8 = (f32[2,8,896]{2,1,0:T(8,128)S(1)}, f32[2,8,896]{2,1,0:T(8,128)S(1)}, u32[]{:S(2)}, u32[]{:S(2)}) collective-permute-start(f32[2,8,896]{2,1,0:T(8,128)S(1)} %get-tuple-element.38), channel_id=1, source_target_pairs={{0,128},{16,144},{32,160},{48,176},{64,192},{80,208},{96,224},{112... | collective-permute-start | bytes 172040 | tf_op jit(solution)/shard_map/ppermute | solution.py:323
  91.1 2.6 %collective-permute-done.8.came_ref = f32[2,8,896]{2,1,0:T(8,128)S(1)} collective-permute-done((f32[2,8,896]{2,1,0:T(8,128)S(1)}, f32[2,8,896]{2,1,0:T(8,128)S(1)}, u32[]{:S(2)}, u32[]{:S(2)}) %collective-permute-start.8) | collective-permute-done | bytes 57376 | tf_op jit(solution)/shard_map/ppermute | solution.py:323
  93.7 1.6 %collective-permute-start.9 = (f32[1,8,896]{2,1,0:T(8,128)S(1)}, f32[1,8,896]{2,1,0:T(8,128)S(1)}, u32[]{:S(2)}, u32[]{:S(2)}) collective-permute-start(f32[1,8,896]{2,1,0:T(8,128)S(1)} %get-tuple-element.40), channel_id=1, source_target_pairs={{0,64},{16,80},{32,96},{48,112},{64,0},{80,16},{96,32},{112,48},{1... | collective-permute-start | bytes 86024 | tf_op jit(solution)/shard_map/ppermute | solution.py:323
  95.4 0.1 shard_map.97
  95.5 0.1 copy.9
  95.6 2.1 %collective-permute-done.9.came_ref = f32[1,8,896]{2,1,0:T(8,128)S(1)} collective-permute-done((f32[1,8,896]{2,1,0:T(8,128)S(1)}, f32[1,8,896]{2,1,0:T(8,128)S(1)}, u32[]{:S(2)}, u32[]{:S(2)}) %collective-permute-start.9) | collective-permute-done | bytes 28704 | tf_op jit(solution)/shard_map/ppermute | solution.py:323
  97.7 0.7 shard_map.98
  (30 shorter events, 0.4 us)
Async XLA Ops:
  0.6 2.2 %copy-start.1 = (bf16[27,512,128]{2,1,0:T(8,128)(2,1)S(1)}, bf16[27,512,128]{2,1,0:T(8,128)(2,1)}, u32[]{:S(2)}) copy-start(bf16[27,512,128]{2,1,0:T(8,128)(2,1)} %weight_ref.3) | copy-start | bytes 10616836
  2.7 13.1 %copy-start.8 = (f32[128]{0:T(128)S(1)}, f32[128]{0:T(128)}, u32[]{:S(2)}) copy-start(f32[128]{0:T(128)} %param.9) | copy-start | bytes 1540
  2.8 0.9 copy-start.6
  4.5 11.4 %collective-permute-start = (f32[128,128]{1,0:T(8,128)S(1)}, f32[128,128]{1,0:T(8,128)S(1)}, u32[]{:S(2)}, u32[]{:S(2)}) collective-permute-start(f32[128,128]{1,0:T(8,128)S(1)} %get-tuple-element.24), channel_id=1, source_target_pairs={{0,1},{1,0},{2,3},{3,2},{4,5},{5,4},{6,7},{7,6},{8,9},{9,8},{10,11... | collective-permute-start | bytes 196616 | tf_op jit(solution)/shard_map/ppermute | solution.py:323
  4.6 11.3 %collective-permute-start.1 = (f32[128,128]{1,0:T(8,128)S(1)}, f32[128,128]{1,0:T(8,128)S(1)}, u32[]{:S(2)}, u32[]{:S(2)}) collective-permute-start(f32[128,128]{1,0:T(8,128)S(1)} %get-tuple-element.26), channel_id=1, source_target_pairs={{1,2},{3,4},{5,6},{7,8},{9,10},{11,12},{13,14},{2,1},{4,3},{6,5},{... | collective-permute-start | bytes 196616 | tf_op jit(solution)/shard_map/ppermute | solution.py:332
  8.5 21.8 %all-to-all-start = ((bf16[16,128,128]{2,1,0:T(8,128)(2,1)}), bf16[16,128,128]{2,1,0:T(8,128)(2,1)S(1)}, u32[]{:S(2)}, u32[]{:S(2)}) async-start(bf16[16,128,128]{2,1,0:T(8,128)(2,1)} %get-tuple-element.22.before_ref), calls=%async_computation | async-start | bytes 1048576 | tf_op jit(solution)/shard_map/all_to_all | solution.py:319
  15.9 2.4 %copy-start.9 = (f32[384]{0:T(512)S(1)}, f32[384]{0:T(512)}, u32[]{:S(2)}) copy-start(f32[384]{0:T(512)} %param.11) | copy-start | bytes 4612
  15.9 14.3 %copy-start = (bf16[27,128,384]{2,1,0:T(8,128)(2,1)S(1)}, bf16[27,128,384]{2,1,0:T(8,128)(2,1)}, u32[]{:S(2)}) copy-start(bf16[27,128,384]{2,1,0:T(8,128)(2,1)} %weight_ref.5) | copy-start | bytes 7962628
  15.9 14.3 %copy-start.7 = (s32[1,115]{1,0:T(1,128)S(1)}, s32[1,115]{1,0:T(1,128)}, u32[]{:S(2)}) copy-start(s32[1,115]{1,0:T(1,128)} %index_ref.1) | copy-start | bytes 1384
  16.0 2.4 %collective-permute-start.2 = (bf16[128,128]{1,0:T(8,128)(2,1)S(1)}, bf16[128,128]{1,0:T(8,128)(2,1)S(1)}, u32[]{:S(2)}, u32[]{:S(2)}) collective-permute-start(bf16[128,128]{1,0:T(8,128)(2,1)S(1)} %get-tuple-element.27.here_ref), channel_id=1, source_target_pairs={{0,1},{1,0},{2,3},{3,2},{4,5},{5,4},{6,7},{7,6},{8,9},{9,8},{10,11... | collective-permute-start | bytes 98312 | tf_op jit(solution)/shard_map/ppermute | solution.py:323
  16.2 12.1 %collective-permute-start.3 = (bf16[128,128]{1,0:T(8,128)(2,1)S(1)}, bf16[128,128]{1,0:T(8,128)(2,1)S(1)}, u32[]{:S(2)}, u32[]{:S(2)}) collective-permute-start(bf16[128,128]{1,0:T(8,128)(2,1)S(1)} %get-tuple-element.27.here_ref), channel_id=1, source_target_pairs={{1,2},{3,4},{5,6},{7,8},{9,10},{11,12},{13,14},{2,1},{4,3},{6,5},{... | collective-permute-start | bytes 98312 | tf_op jit(solution)/shard_map/ppermute | solution.py:332
  32.9 1.3 %copy-start.2 = (bf16[16,480,128]{2,1,0:T(8,128)(2,1)}, bf16[16,480,128]{2,1,0:T(8,128)(2,1)S(1)}, u32[]{:S(2)}) copy-start(bf16[16,480,128]{2,1,0:T(8,128)(2,1)S(1)} %get-tuple-element.41) | copy-start | bytes 5898244
  34.2 0.8 copy-start.3
  35.0 38.2 %all-to-all-start.1 = ((bf16[16,480,128]{2,1,0:T(8,128)(2,1)}), bf16[16,480,128]{2,1,0:T(8,128)(2,1)}, u32[]{:S(2)}, u32[]{:S(2)}) async-start(bf16[16,480,128]{2,1,0:T(8,128)(2,1)} %copy-done.2), calls=%async_computation.1 | async-start | bytes 3932160 | tf_op jit(solution)/shard_map/all_to_all | solution.py:319
  42.1 1.0 %copy-start.4 = (bf16[512,384]{1,0:T(8,128)(2,1)S(1)}, bf16[512,384]{1,0:T(8,128)(2,1)}, u32[]{:S(2)}) copy-start(bf16[512,384]{1,0:T(8,128)(2,1)} %copy-done.3) | copy-start | bytes 1179652
  45.5 4.8 %collective-permute-start.4 = (f32[128,128]{1,0:T(8,128)S(1)}, f32[128,128]{1,0:T(8,128)S(1)}, u32[]{:S(2)}, u32[]{:S(2)}) collective-permute-start(f32[128,128]{1,0:T(8,128)S(1)} %get-tuple-element.29), channel_id=1, source_target_pairs={{0,1},{1,0},{2,3},{3,2},{4,5},{5,4},{6,7},{7,6},{8,9},{9,8},{10,11... | collective-permute-start | bytes 196616 | tf_op jit(solution)/shard_map/ppermute | solution.py:323
  45.6 6.7 %collective-permute-start.5 = (f32[128,128]{1,0:T(8,128)S(1)}, f32[128,128]{1,0:T(8,128)S(1)}, u32[]{:S(2)}, u32[]{:S(2)}) collective-permute-start(f32[128,128]{1,0:T(8,128)S(1)} %get-tuple-element.31), channel_id=1, source_target_pairs={{1,2},{3,4},{5,6},{7,8},{9,10},{11,12},{13,14},{2,1},{4,3},{6,5},{... | collective-permute-start | bytes 196616 | tf_op jit(solution)/shard_map/ppermute | solution.py:332
  69.7 13.9 %collective-permute-start.6 = (f32[8,8,896]{2,1,0:T(8,128)S(1)}, f32[8,8,896]{2,1,0:T(8,128)S(1)}, u32[]{:S(2)}, u32[]{:S(2)}) collective-permute-start(f32[8,8,896]{2,1,0:T(8,128)S(1)} %get-tuple-element.34), channel_id=1, source_target_pairs={{0,32},{16,48},{32,0},{48,16},{64,96},{80,112},{96,64},{112,80},{1... | collective-permute-start | bytes 688136 | tf_op jit(solution)/shard_map/ppermute | solution.py:323
  76.6 18.8 %all-to-all-start.2 = ((bf16[16,48,128]{2,1,0:T(8,128)(2,1)}), bf16[16,48,128]{2,1,0:T(8,128)(2,1)S(1)}, u32[]{:S(2)}, u32[]{:S(2)}) async-start(bf16[16,48,128]{2,1,0:T(8,128)(2,1)} %shard_map.96), calls=%async_computation.2 | async-start | bytes 393216 | tf_op jit(solution)/shard_map/all_to_all | solution.py:319
  83.6 4.3 %collective-permute-start.7 = (bf16[4,8,896]{2,1,0:T(8,128)(2,1)S(1)}, bf16[4,8,896]{2,1,0:T(8,128)(2,1)S(1)}, u32[]{:S(2)}, u32[]{:S(2)}) collective-permute-start(bf16[4,8,896]{2,1,0:T(8,128)(2,1)S(1)} %get-tuple-element.36), channel_id=1, source_target_pairs={{0,16},{16,0},{32,48},{48,32},{64,80},{80,64},{96,112},{112,96},{1... | collective-permute-start | bytes 172040 | tf_op jit(solution)/shard_map/ppermute | solution.py:323
  87.9 5.8 %collective-permute-start.8 = (f32[2,8,896]{2,1,0:T(8,128)S(1)}, f32[2,8,896]{2,1,0:T(8,128)S(1)}, u32[]{:S(2)}, u32[]{:S(2)}) collective-permute-start(f32[2,8,896]{2,1,0:T(8,128)S(1)} %get-tuple-element.38), channel_id=1, source_target_pairs={{0,128},{16,144},{32,160},{48,176},{64,192},{80,208},{96,224},{112... | collective-permute-start | bytes 172040 | tf_op jit(solution)/shard_map/ppermute | solution.py:323
  93.7 4.0 %collective-permute-start.9 = (f32[1,8,896]{2,1,0:T(8,128)S(1)}, f32[1,8,896]{2,1,0:T(8,128)S(1)}, u32[]{:S(2)}, u32[]{:S(2)}) collective-permute-start(f32[1,8,896]{2,1,0:T(8,128)S(1)} %get-tuple-element.40), channel_id=1, source_target_pairs={{0,64},{16,80},{32,96},{48,112},{64,0},{80,16},{96,32},{112,48},{1... | collective-permute-start | bytes 86024 | tf_op jit(solution)/shard_map/ppermute | solution.py:323
  95.6 2.8 %copy-start.5 = (f32[27,8,24]{0,2,1:T(8,128)}, f32[27,8,24]{0,2,1:T(8,128)S(1)}, u32[]{:S(2)}) copy-start(f32[27,8,24]{0,2,1:T(8,128)S(1)} %copy.9) | copy-start | bytes 62212

commit v9 on v8

--- a/solution.py
+++ b/solution.py
@@ -59,18 +59,25 @@
     return [pl.BlockSpec(memory_space=kind) for kind in kinds]
 
 
-def packed_inputs(pixel_source, tokens_source, out_ref, field_ref, pixel_ref, tokens_ref, sems):
+def packed_and_convolved(pixel_source, tokens_source, weight_source,
+                         out_ref, pair_ref, keep_ref, cross_ref,
+                         pixel_ref, tokens_ref, weight_ref, padded, sems):
     copies = [
         pltpu.make_async_copy(source, target, sems.at[n])
         for n, (source, target) in enumerate(
-            ((tokens_source, tokens_ref), (pixel_source, pixel_ref))
+            (
+                (tokens_source, tokens_ref),
+                (pixel_source, pixel_ref),
+                (weight_source, weight_ref),
+            )
         )
     ]
     for copy in copies:
         copy.start()
     copies[0].wait()
-    tokens = tokens_ref[...].astype(F32).reshape(POS, D).astype(BF16)
-    field_ref[...] = tokens
+    tokens = tokens_ref[...].astype(F32).reshape(POS, D)
+    padded[PAD : PAD + POS] = tokens
+    tokens = tokens.astype(BF16)
     turned = tokens.T
     width = D // 16
     copies[1].wait()
@@ -80,13 +87,9 @@
             [pix[:, n * 128 : (n + 1) * 128] for n in range(4 * CO // 128)], axis=0
         ).astype(BF16)
         out_ref[block, CHUNK:] = turned[block * width : (block + 1) * width]
-
-
-def first_conv(tokens_ref, weight_ref, before_ref, pair_ref, keep_ref, cross_ref, padded):
-    del before_ref
     padded[0:PAD] = jnp.zeros((PAD, D), F32)
     padded[PAD + POS :] = jnp.zeros((PAD, D), F32)
-    padded[PAD : PAD + POS] = tokens_ref[...].astype(F32)
+    copies[2].wait()
     total = jnp.zeros((POS, 3 * C1), F32)
     for row, col in TAPS9:
         step = PAD + COLS * (row - 1) + col - 1
@@ -333,25 +336,20 @@
 
 
 def per_device(tokens, conv_first, bias_first, conv_second, bias_second, pixels, mask_index):
-    packed, field = call(
-        packed_inputs,
-        (struct((16, CHUNK + D // 16, POS), BF16), struct((POS, D), BF16)),
-        spots(pltpu.HBM, pltpu.HBM),
+    plane = struct((POS, C1), F32)
+    packed, pair, keep, cross = call(
+        packed_and_convolved,
+        (struct((16, CHUNK + D // 16, POS), BF16), plane, plane, plane),
+        spots(pltpu.HBM, pltpu.HBM, pltpu.HBM),
         [
             pltpu.VMEM((16, 2, 4, 4 * CO), BF16),
             pltpu.VMEM((32, 4, D), BF16),
-            pltpu.SemaphoreType.DMA((2,)),
+            pltpu.VMEM((27, D, C1), BF16),
+            pltpu.VMEM((POS + 2 * PAD, D), F32),
+            pltpu.SemaphoreType.DMA((3,)),
         ],
-        flops=FLOPS // 10,
-        limit=56,
-    )(pixels[0], tokens[0, 0])
-    plane = struct((POS, C1), F32)
-    pair, keep, cross = call(
-        first_conv,
-        (plane, plane, plane),
-        spots(VMEM, VMEM, pl.ANY),
-        [pltpu.VMEM((POS + 2 * PAD, D), F32)],
-    )(field, conv_first, packed)
+        limit=60,
+    )(pixels[0], tokens[0, 0], conv_first)
     packed = exchange(packed, "seq")
     zsum, hidden = call(
         hidden_values,

time: 99.1 us -> 98.9 us (level)
    pallas_call x2 -> x1, Pallas kernels: 2.87 us -> 3.67 us  [per_device(): call(packed_and_convolved, (struct((16, CHUNK + D // 16, POS), BF16), pla...]
    unnamed x20 -> x18, local copies, waits for them, and re-layouts: 4.04 us -> 3.89 us
where the time goes in v9:
time: 98.9 us; the launch traced here: 98.3 us
  starting transfers between devices  41.5 us (42%)
  waiting for transfers between devices  21.3 us (22%)
  blocking collectives  16.1 us (16%)
  Pallas kernels  14.5 us (15%)
  local copies, waits for them, and re-layouts  4.02 us (4%)
    all_to_all x3, starting transfers between devices, exchange(): return lax.all_to_all(value, axis, split_axis=0, concat_axis=0, tiled=True)  21.5 us
    all_gather x1, blocking collectives, per_device(): grad_z = lax.all_gather(grad_z, 'seq')  16.1 us
    ppermute x3, waiting for transfers between devices, with_cross(): return lax.ppermute(value, 'seq', swaps + [(j, i) for i, j in swaps])  11 us
    ppermute x3, starting transfers between devices, with_cross(): return lax.ppermute(value, 'seq', swaps + [(j, i) for i, j in swaps])  10.7 us
    ppermute x7, starting transfers between devices, swapped(): return lax.ppermute(value, axis, [(i, i ^ step) for i in range(16)])  9.33 us
    ppermute x7, waiting for transfers between devices, swapped(): return lax.ppermute(value, axis, [(i, i ^ step) for i in range(16)])  8.31 us
    unnamed x18, local copies, waits for them, and re-layouts  3.89 us
    pallas_call x1, Pallas kernels, per_device(): call(packed_and_convolved, (struct((16, CHUNK + D // 16, POS), BF16), pla...  3.67 us
  transfers between devices with their start and end apart: 13, of which 6 were waited for; matrix products, arithmetic and copies ran while one was open for 0% of the time, Pallas kernels for 7%

profile of v9, /device:TPU:32, one launch (start us, length us, event | category | flops | bytes accessed | tf_op | source)
XLA Modules:
  0.0 98.3 jit_solution(16986852333891841557)
XLA Ops:
  0.6 3.7 %shard_map.86 = (bf16[16,128,128]{2,1,0:T(8,128)(2,1)}, f32[128,128]{1,0:T(8,128)}, f32[128,128]{1,0:T(8,128)}, f32[128,128]{1,0:T(8,128)}) custom-call(bf16[16,2,4,1536]{3,2,1,0:T(4,128)(2,1)} %bitcast.9, bf16[32,4,512]{2,1,0:T(4,128)(2,1)} %bitcast.10, bf16[27,512,128]{2,1,0:T(8,128)(2,1)} %weight_source.1), custom_call_target="tpu_custom_call" | custom-call | tf_op jit(solution)/shard_map/pallas_call | solution.py:340
  4.3 0.1 collective-permute-start
  4.4 3.8 %collective-permute-start.1 = (f32[128,128]{1,0:T(8,128)}, f32[128,128]{1,0:T(8,128)S(1)}, u32[]{:S(2)}, u32[]{:S(2)}) collective-permute-start(f32[128,128]{1,0:T(8,128)} %get-tuple-element.24), channel_id=1, source_target_pairs={{1,2},{3,4},{5,6},{7,8},{9,10},{11,12},{13,14},{2,1},{4,3},{6,5},{... | collective-permute-start | bytes 196616 | tf_op jit(solution)/shard_map/ppermute | solution.py:335
  8.3 7.4 %all-to-all-start = ((bf16[16,128,128]{2,1,0:T(8,128)(2,1)}), bf16[16,128,128]{2,1,0:T(8,128)(2,1)S(1)}, u32[]{:S(2)}, u32[]{:S(2)}) async-start(bf16[16,128,128]{2,1,0:T(8,128)(2,1)} %get-tuple-element.21), calls=%async_computation | async-start | bytes 1048576 | tf_op jit(solution)/shard_map/all_to_all | solution.py:322
  15.7 0.8 copy-done.6
  16.6 0.2 collective-permute-start.2
  16.8 2.1 %collective-permute-start.3 = (bf16[128,128]{1,0:T(8,128)(2,1)S(1)}, bf16[128,128]{1,0:T(8,128)(2,1)S(1)}, u32[]{:S(2)}, u32[]{:S(2)}) collective-permute-start(bf16[128,128]{1,0:T(8,128)(2,1)S(1)} %get-tuple-element.25.here_ref), channel_id=1, source_target_pairs={{1,2},{3,4},{5,6},{7,8},{9,10},{11,12},{13,14},{2,1},{4,3},{6,5},{... | collective-permute-start | bytes 98312 | tf_op jit(solution)/shard_map/ppermute | solution.py:335
  19.0 9.1 %collective-permute-done.3.cross_ref = bf16[128,128]{1,0:T(8,128)(2,1)S(1)} collective-permute-done((bf16[128,128]{1,0:T(8,128)(2,1)S(1)}, bf16[128,128]{1,0:T(8,128)(2,1)S(1)}, u32[]{:S(2)}, u32[]{:S(2)}) %collective-permute-start.3) | collective-permute-done | bytes 32800 | tf_op jit(solution)/shard_map/ppermute | solution.py:335
  28.1 1.9 %all-to-all-done.packed_ref = bf16[16,128,128]{2,1,0:T(8,128)(2,1)S(1)} async-done(((bf16[16,128,128]{2,1,0:T(8,128)(2,1)}), bf16[16,128,128]{2,1,0:T(8,128)(2,1)S(1)}, u32[]{:S(2)}, u32[]{:S(2)}) %all-to-all-start) | async-done | bytes 524320 | tf_op jit(solution)/shard_map/all_to_all | solution.py:322
  30.0 2.7 %shard_map.88 = (bf16[16,480,128]{2,1,0:T(8,128)(2,1)S(1)}, bf16[512,384]{1,0:T(8,128)(2,1)S(1)}) custom-call(bf16[128,128]{1,0:T(8,128)(2,1)S(1)} %collective-permute-done.2.pair_ref, bf16[128,128]{1,0:T(8,128)(2,1)S(1)} %get-tuple-element.25.here_ref, bf16[128,128]{1,0:T(8,128)(2,1)S(1)} %collective-permute-done.3.cross_ref, ...), custom_call_target="tpu_custom_call" | custom-call | tf_op jit(solution)/shard_map/pallas_call | solution.py:361
  32.8 1.3 %copy-done.1 = bf16[16,480,128]{2,1,0:T(8,128)(2,1)} copy-done((bf16[16,480,128]{2,1,0:T(8,128)(2,1)}, bf16[16,480,128]{2,1,0:T(8,128)(2,1)S(1)}, u32[]{:S(2)}) %copy-start.1) | copy-done | bytes 1966104
  34.1 0.8 copy-done.2
  34.8 7.1 %all-to-all-start.1 = ((bf16[16,480,128]{2,1,0:T(8,128)(2,1)}), bf16[16,480,128]{2,1,0:T(8,128)(2,1)}, u32[]{:S(2)}, u32[]{:S(2)}) async-start(bf16[16,480,128]{2,1,0:T(8,128)(2,1)} %copy-done.1), calls=%async_computation.1 | async-start | bytes 3932160 | tf_op jit(solution)/shard_map/all_to_all | solution.py:322
  41.9 1.0 %copy-done.3 = bf16[512,384]{1,0:T(8,128)(2,1)S(1)} copy-done((bf16[512,384]{1,0:T(8,128)(2,1)S(1)}, bf16[512,384]{1,0:T(8,128)(2,1)}, u32[]{:S(2)}) %copy-start.3) | copy-done | bytes 393240
  42.9 2.4 %shard_map.89 = (f32[128,128]{1,0:T(8,128)S(1)}, f32[128,128]{1,0:T(8,128)S(1)}, f32[128,128]{1,0:T(8,128)S(1)}) custom-call(bf16[512,384]{1,0:T(8,128)(2,1)S(1)} %copy-done.3, bf16[27,128,384]{2,1,0:T(8,128)(2,1)S(1)} %copy-done), custom_call_target="tpu_custom_call" | custom-call | bytes 4194304 | tf_op jit(solution)/shard_map/pallas_call | solution.py:370
  45.3 0.1 collective-permute-start.4
  45.4 4.7 %collective-permute-start.5 = (f32[128,128]{1,0:T(8,128)S(1)}, f32[128,128]{1,0:T(8,128)S(1)}, u32[]{:S(2)}, u32[]{:S(2)}) collective-permute-start(f32[128,128]{1,0:T(8,128)S(1)} %get-tuple-element.29), channel_id=1, source_target_pairs={{1,2},{3,4},{5,6},{7,8},{9,10},{11,12},{13,14},{2,1},{4,3},{6,5},{... | collective-permute-start | bytes 196616 | tf_op jit(solution)/shard_map/ppermute | solution.py:335
  50.2 1.9 %collective-permute-done.5.cross_ref = f32[128,128]{1,0:T(8,128)S(1)} collective-permute-done((f32[128,128]{1,0:T(8,128)S(1)}, f32[128,128]{1,0:T(8,128)S(1)}, u32[]{:S(2)}, u32[]{:S(2)}) %collective-permute-start.5) | collective-permute-done | bytes 65568 | tf_op jit(solution)/shard_map/ppermute | solution.py:335
  52.1 16.1 %all-gather = bf16[2048,128]{1,0:T(8,128)(2,1)S(1)} all-gather(bf16[128,128]{1,0:T(8,128)(2,1)S(1)} %shard_map.90), channel_id=2, replica_groups=mesh['dp'=16,'seq'=16] {'seq'}, dimensions={0}, use_global_device_ids=true | all-gather | bytes 557056 | tf_op jit(solution)/shard_map/all_gather | solution.py:381
  68.3 1.3 %shard_map.91 = (f32[8,8,896]{2,1,0:T(8,128)S(1)}, f32[8,8,896]{2,1,0:T(8,128)S(1)}) custom-call(bf16[16,128,128]{2,1,0:T(8,128)(2,1)S(1)} %all-to-all-done.packed_ref, bf16[16,128,128]{2,1,0:T(8,128)(2,1)S(1)} %bitcast.6), custom_call_target="tpu_custom_call" | custom-call | tf_op jit(solution)/shard_map/pallas_call | solution.py:384
  69.5 3.5 %collective-permute-start.6 = (f32[8,8,896]{2,1,0:T(8,128)S(1)}, f32[8,8,896]{2,1,0:T(8,128)S(1)}, u32[]{:S(2)}, u32[]{:S(2)}) collective-permute-start(f32[8,8,896]{2,1,0:T(8,128)S(1)} %get-tuple-element.32), channel_id=1, source_target_pairs={{0,32},{16,48},{32,0},{48,16},{64,96},{80,112},{96,64},{112,80},{1... | collective-permute-start | bytes 688136 | tf_op jit(solution)/shard_map/ppermute | solution.py:326
  73.0 3.4 %shard_map.95 = bf16[16,48,128]{2,1,0:T(8,128)(2,1)} custom-call(bf16[16,480,128]{2,1,0:T(8,128)(2,1)} %all-to-all-done.1.blocks_ref, f32[8,8,896]{2,1,0:T(8,128)S(1)} %get-tuple-element.31.kept_ref.before_ref), custom_call_target="tpu_custom_call" | custom-call | bytes 4194304 | tf_op jit(solution)/shard_map/pallas_call | solution.py:398
  76.4 7.0 %all-to-all-start.2 = ((bf16[16,48,128]{2,1,0:T(8,128)(2,1)}), bf16[16,48,128]{2,1,0:T(8,128)(2,1)S(1)}, u32[]{:S(2)}, u32[]{:S(2)}) async-start(bf16[16,48,128]{2,1,0:T(8,128)(2,1)} %shard_map.95), calls=%async_computation.2 | async-start | bytes 393216 | tf_op jit(solution)/shard_map/all_to_all | solution.py:322
  83.5 0.7 collective-permute-start.7
  84.1 3.6 %collective-permute-done.7.came_ref = bf16[4,8,896]{2,1,0:T(8,128)(2,1)S(1)} collective-permute-done((bf16[4,8,896]{2,1,0:T(8,128)(2,1)S(1)}, bf16[4,8,896]{2,1,0:T(8,128)(2,1)S(1)}, u32[]{:S(2)}, u32[]{:S(2)}) %collective-permute-start.7) | collective-permute-done | bytes 57376 | tf_op jit(solution)/shard_map/ppermute | solution.py:326
  87.8 3.1 %collective-permute-start.8 = (f32[2,8,896]{2,1,0:T(8,128)S(1)}, f32[2,8,896]{2,1,0:T(8,128)S(1)}, u32[]{:S(2)}, u32[]{:S(2)}) collective-permute-start(f32[2,8,896]{2,1,0:T(8,128)S(1)} %get-tuple-element.36), channel_id=1, source_target_pairs={{0,128},{16,144},{32,160},{48,176},{64,192},{80,208},{96,224},{112... | collective-permute-start | bytes 172040 | tf_op jit(solution)/shard_map/ppermute | solution.py:326
  90.9 2.6 %collective-permute-done.8.came_ref = f32[2,8,896]{2,1,0:T(8,128)S(1)} collective-permute-done((f32[2,8,896]{2,1,0:T(8,128)S(1)}, f32[2,8,896]{2,1,0:T(8,128)S(1)}, u32[]{:S(2)}, u32[]{:S(2)}) %collective-permute-start.8) | collective-permute-done | bytes 57376 | tf_op jit(solution)/shard_map/ppermute | solution.py:326
  93.6 1.6 %collective-permute-start.9 = (f32[1,8,896]{2,1,0:T(8,128)S(1)}, f32[1,8,896]{2,1,0:T(8,128)S(1)}, u32[]{:S(2)}, u32[]{:S(2)}) collective-permute-start(f32[1,8,896]{2,1,0:T(8,128)S(1)} %get-tuple-element.38), channel_id=1, source_target_pairs={{0,64},{16,80},{32,96},{48,112},{64,0},{80,16},{96,32},{112,48},{1... | collective-permute-start | bytes 86024 | tf_op jit(solution)/shard_map/ppermute | solution.py:326
  95.2 0.1 shard_map.96
  95.3 0.1 copy.9
  95.5 2.1 %collective-permute-done.9.came_ref = f32[1,8,896]{2,1,0:T(8,128)S(1)} collective-permute-done((f32[1,8,896]{2,1,0:T(8,128)S(1)}, f32[1,8,896]{2,1,0:T(8,128)S(1)}, u32[]{:S(2)}, u32[]{:S(2)}) %collective-permute-start.9) | collective-permute-done | bytes 28704 | tf_op jit(solution)/shard_map/ppermute | solution.py:326
  97.5 0.7 shard_map.97
  (27 shorter events, 0.2 us)
Async XLA Ops:
  0.6 15.1 %copy-start.7 = (f32[128]{0:T(128)S(1)}, f32[128]{0:T(128)}, u32[]{:S(2)}) copy-start(f32[128]{0:T(128)} %param.9) | copy-start | bytes 1540
  4.3 11.4 %collective-permute-start = (f32[128,128]{1,0:T(8,128)}, f32[128,128]{1,0:T(8,128)S(1)}, u32[]{:S(2)}, u32[]{:S(2)}) collective-permute-start(f32[128,128]{1,0:T(8,128)} %get-tuple-element.22), channel_id=1, source_target_pairs={{0,1},{1,0},{2,3},{3,2},{4,5},{5,4},{6,7},{7,6},{8,9},{9,8},{10,11... | collective-permute-start | bytes 196616 | tf_op jit(solution)/shard_map/ppermute | solution.py:326
  4.4 11.3 %collective-permute-start.1 = (f32[128,128]{1,0:T(8,128)}, f32[128,128]{1,0:T(8,128)S(1)}, u32[]{:S(2)}, u32[]{:S(2)}) collective-permute-start(f32[128,128]{1,0:T(8,128)} %get-tuple-element.24), channel_id=1, source_target_pairs={{1,2},{3,4},{5,6},{7,8},{9,10},{11,12},{13,14},{2,1},{4,3},{6,5},{... | collective-permute-start | bytes 196616 | tf_op jit(solution)/shard_map/ppermute | solution.py:335
  8.3 21.8 %all-to-all-start = ((bf16[16,128,128]{2,1,0:T(8,128)(2,1)}), bf16[16,128,128]{2,1,0:T(8,128)(2,1)S(1)}, u32[]{:S(2)}, u32[]{:S(2)}) async-start(bf16[16,128,128]{2,1,0:T(8,128)(2,1)} %get-tuple-element.21), calls=%async_computation | async-start | bytes 1048576 | tf_op jit(solution)/shard_map/all_to_all | solution.py:322
  15.7 0.8 copy-start.6
  16.5 2.4 %copy-start.8 = (f32[384]{0:T(512)S(1)}, f32[384]{0:T(512)}, u32[]{:S(2)}) copy-start(f32[384]{0:T(512)} %param.11) | copy-start | bytes 4612
  16.5 13.5 %copy-start = (bf16[27,128,384]{2,1,0:T(8,128)(2,1)S(1)}, bf16[27,128,384]{2,1,0:T(8,128)(2,1)}, u32[]{:S(2)}) copy-start(bf16[27,128,384]{2,1,0:T(8,128)(2,1)} %weight_ref.3) | copy-start | bytes 7962628
  16.5 13.5 %copy-start.5 = (s32[1,115]{1,0:T(1,128)S(1)}, s32[1,115]{1,0:T(1,128)}, u32[]{:S(2)}) copy-start(s32[1,115]{1,0:T(1,128)} %index_ref.1) | copy-start | bytes 1384
  16.6 2.4 %collective-permute-start.2 = (bf16[128,128]{1,0:T(8,128)(2,1)S(1)}, bf16[128,128]{1,0:T(8,128)(2,1)S(1)}, u32[]{:S(2)}, u32[]{:S(2)}) collective-permute-start(bf16[128,128]{1,0:T(8,128)(2,1)S(1)} %get-tuple-element.25.here_ref), channel_id=1, source_target_pairs={{0,1},{1,0},{2,3},{3,2},{4,5},{5,4},{6,7},{7,6},{8,9},{9,8},{10,11... | collective-permute-start | bytes 98312 | tf_op jit(solution)/shard_map/ppermute | solution.py:326
  16.8 11.3 %collective-permute-start.3 = (bf16[128,128]{1,0:T(8,128)(2,1)S(1)}, bf16[128,128]{1,0:T(8,128)(2,1)S(1)}, u32[]{:S(2)}, u32[]{:S(2)}) collective-permute-start(bf16[128,128]{1,0:T(8,128)(2,1)S(1)} %get-tuple-element.25.here_ref), channel_id=1, source_target_pairs={{1,2},{3,4},{5,6},{7,8},{9,10},{11,12},{13,14},{2,1},{4,3},{6,5},{... | collective-permute-start | bytes 98312 | tf_op jit(solution)/shard_map/ppermute | solution.py:335
  32.8 1.3 %copy-start.1 = (bf16[16,480,128]{2,1,0:T(8,128)(2,1)}, bf16[16,480,128]{2,1,0:T(8,128)(2,1)S(1)}, u32[]{:S(2)}) copy-start(bf16[16,480,128]{2,1,0:T(8,128)(2,1)S(1)} %get-tuple-element.39) | copy-start | bytes 5898244
  34.1 0.8 copy-start.2
  34.8 38.2 %all-to-all-start.1 = ((bf16[16,480,128]{2,1,0:T(8,128)(2,1)}), bf16[16,480,128]{2,1,0:T(8,128)(2,1)}, u32[]{:S(2)}, u32[]{:S(2)}) async-start(bf16[16,480,128]{2,1,0:T(8,128)(2,1)} %copy-done.1), calls=%async_computation.1 | async-start | bytes 3932160 | tf_op jit(solution)/shard_map/all_to_all | solution.py:322
  41.9 1.0 %copy-start.3 = (bf16[512,384]{1,0:T(8,128)(2,1)S(1)}, bf16[512,384]{1,0:T(8,128)(2,1)}, u32[]{:S(2)}) copy-start(bf16[512,384]{1,0:T(8,128)(2,1)} %copy-done.2) | copy-start | bytes 1179652
  45.3 4.8 %collective-permute-start.4 = (f32[128,128]{1,0:T(8,128)S(1)}, f32[128,128]{1,0:T(8,128)S(1)}, u32[]{:S(2)}, u32[]{:S(2)}) collective-permute-start(f32[128,128]{1,0:T(8,128)S(1)} %get-tuple-element.27), channel_id=1, source_target_pairs={{0,1},{1,0},{2,3},{3,2},{4,5},{5,4},{6,7},{7,6},{8,9},{9,8},{10,11... | collective-permute-start | bytes 196616 | tf_op jit(solution)/shard_map/ppermute | solution.py:326
  45.4 6.7 %collective-permute-start.5 = (f32[128,128]{1,0:T(8,128)S(1)}, f32[128,128]{1,0:T(8,128)S(1)}, u32[]{:S(2)}, u32[]{:S(2)}) collective-permute-start(f32[128,128]{1,0:T(8,128)S(1)} %get-tuple-element.29), channel_id=1, source_target_pairs={{1,2},{3,4},{5,6},{7,8},{9,10},{11,12},{13,14},{2,1},{4,3},{6,5},{... | collective-permute-start | bytes 196616 | tf_op jit(solution)/shard_map/ppermute | solution.py:335
  69.5 13.9 %collective-permute-start.6 = (f32[8,8,896]{2,1,0:T(8,128)S(1)}, f32[8,8,896]{2,1,0:T(8,128)S(1)}, u32[]{:S(2)}, u32[]{:S(2)}) collective-permute-start(f32[8,8,896]{2,1,0:T(8,128)S(1)} %get-tuple-element.32), channel_id=1, source_target_pairs={{0,32},{16,48},{32,0},{48,16},{64,96},{80,112},{96,64},{112,80},{1... | collective-permute-start | bytes 688136 | tf_op jit(solution)/shard_map/ppermute | solution.py:326
  76.4 18.8 %all-to-all-start.2 = ((bf16[16,48,128]{2,1,0:T(8,128)(2,1)}), bf16[16,48,128]{2,1,0:T(8,128)(2,1)S(1)}, u32[]{:S(2)}, u32[]{:S(2)}) async-start(bf16[16,48,128]{2,1,0:T(8,128)(2,1)} %shard_map.95), calls=%async_computation.2 | async-start | bytes 393216 | tf_op jit(solution)/shard_map/all_to_all | solution.py:322
  83.5 4.3 %collective-permute-start.7 = (bf16[4,8,896]{2,1,0:T(8,128)(2,1)S(1)}, bf16[4,8,896]{2,1,0:T(8,128)(2,1)S(1)}, u32[]{:S(2)}, u32[]{:S(2)}) collective-permute-start(bf16[4,8,896]{2,1,0:T(8,128)(2,1)S(1)} %get-tuple-element.34), channel_id=1, source_target_pairs={{0,16},{16,0},{32,48},{48,32},{64,80},{80,64},{96,112},{112,96},{1... | collective-permute-start | bytes 172040 | tf_op jit(solution)/shard_map/ppermute | solution.py:326
  87.8 5.8 %collective-permute-start.8 = (f32[2,8,896]{2,1,0:T(8,128)S(1)}, f32[2,8,896]{2,1,0:T(8,128)S(1)}, u32[]{:S(2)}, u32[]{:S(2)}) collective-permute-start(f32[2,8,896]{2,1,0:T(8,128)S(1)} %get-tuple-element.36), channel_id=1, source_target_pairs={{0,128},{16,144},{32,160},{48,176},{64,192},{80,208},{96,224},{112... | collective-permute-start | bytes 172040 | tf_op jit(solution)/shard_map/ppermute | solution.py:326
  93.6 4.0 %collective-permute-start.9 = (f32[1,8,896]{2,1,0:T(8,128)S(1)}, f32[1,8,896]{2,1,0:T(8,128)S(1)}, u32[]{:S(2)}, u32[]{:S(2)}) collective-permute-start(f32[1,8,896]{2,1,0:T(8,128)S(1)} %get-tuple-element.38), channel_id=1, source_target_pairs={{0,64},{16,80},{32,96},{48,112},{64,0},{80,16},{96,32},{112,48},{1... | collective-permute-start | bytes 86024 | tf_op jit(solution)/shard_map/ppermute | solution.py:326
  95.5 2.8 %copy-start.4 = (f32[27,8,24]{0,2,1:T(8,128)}, f32[27,8,24]{0,2,1:T(8,128)S(1)}, u32[]{:S(2)}) copy-start(f32[27,8,24]{0,2,1:T(8,128)S(1)} %copy.9) | copy-start | bytes 62212

commit v10 on v9

--- a/solution.py
+++ b/solution.py
@@ -374,6 +374,7 @@
         [pltpu.VMEM((9, POS + 2 * PAD, 3 * C1), F32)],
         size=4 << 20,
     )(cot, conv_second)
+    blocks, keep = lax.optimization_barrier((blocks, keep))
     blocks = exchange(blocks, "dp")
     grad_z = call(hidden_grads, struct((POS, C1), BF16), spots(*[VMEM] * 4))(
         with_pair(pair), keep, with_cross(cross), zsum
@@ -391,7 +392,7 @@
     for level in (1, 2, 3):
         half = struct((8 >> level, C1 // 16, 7 * 128), F32)
         came = swapped(send, STEPS[level - 1], "dp")
-        sent = struct(half.shape, BF16 if level == 1 else F32)
+        sent = struct(half.shape, BF16 if level in (1, 2) else F32)
         keep, send = call(
             partial(half_sum, level), (half, sent), spots(VMEM, VMEM)
         )(keep, came)

time: 98.9 us -> 105 us (1.062)
  waiting for transfers between devices: 21.3 us -> 36.5 us
  starting transfers between devices: 41.5 us -> 35.9 us
  local copies, waits for them, and re-layouts: 4.02 us -> 2.26 us
  Pallas kernels: 14.5 us -> 12.9 us
    ppermute x7, waiting for transfers between devices: 8.31 us -> 18.4 us  [swapped(): return lax.ppermute(value, axis, [(i, i ^ step) for i in range(16)])]
    all_to_all x3, waiting for transfers between devices: 1.96 us -> 6.99 us  [exchange(): return lax.all_to_all(value, axis, split_axis=0, concat_axis=0, tiled=True)]
    ppermute x7, starting transfers between devices: 9.33 us -> 4.6 us  [swapped(): return lax.ppermute(value, axis, [(i, i ^ step) for i in range(16)])]
    unnamed x18 -> x14, local copies, waits for them, and re-layouts: 3.89 us -> 2.13 us
    pallas_call x1, Pallas kernels: 3.42 us -> 1.89 us  [per_device(): call(second_grads, struct((16, 48, 128), BF16), spots(VMEM, pl.ANY), [plt...]
  transfers between devices with their start and end apart: 13 -> 13, of which waited for: 6 -> 8; matrix products, arithmetic and copies ran while one was open for 0% -> 0% of each run, Pallas kernels for 7% -> 1%
where the time goes in v10:
time: 105 us
  waiting for transfers between devices  36.5 us (35%)
  starting transfers between devices  35.9 us (34%)
  blocking collectives  16.2 us (15%)
  Pallas kernels  12.9 us (12%)
  local copies, waits for them, and re-layouts  2.26 us (2%)
    all_to_all x3, starting transfers between devices, exchange(): return lax.all_to_all(value, axis, split_axis=0, concat_axis=0, tiled=True)  20.7 us
    ppermute x7, waiting for transfers between devices, swapped(): return lax.ppermute(value, axis, [(i, i ^ step) for i in range(16)])  18.4 us
    all_gather x1, blocking collectives, per_device(): grad_z = lax.all_gather(grad_z, 'seq')  16.2 us
    ppermute x3, waiting for transfers between devices, with_cross(): return lax.ppermute(value, 'seq', swaps + [(j, i) for i, j in swaps])  11 us
    ppermute x3, starting transfers between devices, with_cross(): return lax.ppermute(value, 'seq', swaps + [(j, i) for i, j in swaps])  10.7 us
    all_to_all x3, waiting for transfers between devices, exchange(): return lax.all_to_all(value, axis, split_axis=0, concat_axis=0, tiled=True)  6.99 us
    ppermute x7, starting transfers between devices, swapped(): return lax.ppermute(value, axis, [(i, i ^ step) for i in range(16)])  4.6 us
    pallas_call x1, Pallas kernels, per_device(): call(packed_and_convolved, (struct((16, CHUNK + D // 16, POS), BF16), pla...  3.67 us
  transfers between devices with their start and end apart: 13, of which 8 were waited for; matrix products, arithmetic and copies ran while one was open for 0% of the time, Pallas kernels for 1%

profile of v10, /device:TPU:32, one launch (start us, length us, event | category | flops | bytes accessed | tf_op | source)
XLA Modules:
  0.0 104.5 jit_solution(543648062921972411)
XLA Ops:
  0.6 3.7 %shard_map.86 = (bf16[16,128,128]{2,1,0:T(8,128)(2,1)}, f32[128,128]{1,0:T(8,128)}, f32[128,128]{1,0:T(8,128)}, f32[128,128]{1,0:T(8,128)}) custom-call(bf16[16,2,4,1536]{3,2,1,0:T(4,128)(2,1)} %bitcast.9, bf16[32,4,512]{2,1,0:T(4,128)(2,1)} %bitcast.10, bf16[27,512,128]{2,1,0:T(8,128)(2,1)} %weight_source.1), custom_call_target="tpu_custom_call" | custom-call | tf_op jit(solution)/shard_map/pallas_call | solution.py:340
  4.3 0.1 collective-permute-start
  4.4 3.8 %collective-permute-start.1 = (f32[128,128]{1,0:T(8,128)}, f32[128,128]{1,0:T(8,128)S(1)}, u32[]{:S(2)}, u32[]{:S(2)}) collective-permute-start(f32[128,128]{1,0:T(8,128)} %get-tuple-element.26), channel_id=1, source_target_pairs={{1,2},{3,4},{5,6},{7,8},{9,10},{11,12},{13,14},{2,1},{4,3},{6,5},{... | collective-permute-start | bytes 196616 | tf_op jit(solution)/shard_map/ppermute | solution.py:335
  8.3 7.4 %all-to-all-start = ((bf16[16,128,128]{2,1,0:T(8,128)(2,1)}), bf16[16,128,128]{2,1,0:T(8,128)(2,1)S(1)}, u32[]{:S(2)}, u32[]{:S(2)}) async-start(bf16[16,128,128]{2,1,0:T(8,128)(2,1)} %get-tuple-element.23), calls=%async_computation | async-start | bytes 1048576 | tf_op jit(solution)/shard_map/all_to_all | solution.py:322
  15.7 0.8 copy-done.4
  16.6 0.2 collective-permute-start.2
  16.8 2.1 %collective-permute-start.3 = (bf16[128,128]{1,0:T(8,128)(2,1)S(1)}, bf16[128,128]{1,0:T(8,128)(2,1)S(1)}, u32[]{:S(2)}, u32[]{:S(2)}) collective-permute-start(bf16[128,128]{1,0:T(8,128)(2,1)S(1)} %get-tuple-element.27.here_ref), channel_id=1, source_target_pairs={{1,2},{3,4},{5,6},{7,8},{9,10},{11,12},{13,14},{2,1},{4,3},{6,5},{... | collective-permute-start | bytes 98312 | tf_op jit(solution)/shard_map/ppermute | solution.py:335
  19.0 9.1 %collective-permute-done.3.cross_ref = bf16[128,128]{1,0:T(8,128)(2,1)S(1)} collective-permute-done((bf16[128,128]{1,0:T(8,128)(2,1)S(1)}, bf16[128,128]{1,0:T(8,128)(2,1)S(1)}, u32[]{:S(2)}, u32[]{:S(2)}) %collective-permute-start.3) | collective-permute-done | bytes 32800 | tf_op jit(solution)/shard_map/ppermute | solution.py:335
  28.1 1.9 %all-to-all-done.packed_ref = bf16[16,128,128]{2,1,0:T(8,128)(2,1)S(1)} async-done(((bf16[16,128,128]{2,1,0:T(8,128)(2,1)}), bf16[16,128,128]{2,1,0:T(8,128)(2,1)S(1)}, u32[]{:S(2)}, u32[]{:S(2)}) %all-to-all-start) | async-done | bytes 524320 | tf_op jit(solution)/shard_map/all_to_all | solution.py:322
  30.0 2.7 %shard_map.88 = (bf16[16,480,128]{2,1,0:T(8,128)(2,1)S(1)}, bf16[512,384]{1,0:T(8,128)(2,1)S(1)}) custom-call(bf16[128,128]{1,0:T(8,128)(2,1)S(1)} %collective-permute-done.2.pair_ref, bf16[128,128]{1,0:T(8,128)(2,1)S(1)} %get-tuple-element.27.here_ref, bf16[128,128]{1,0:T(8,128)(2,1)S(1)} %collective-permute-done.3.cross_ref, ...), custom_call_target="tpu_custom_call" | custom-call | tf_op jit(solution)/shard_map/pallas_call | solution.py:361
  32.7 1.3 %copy-done.1 = bf16[16,480,128]{2,1,0:T(8,128)(2,1)} copy-done((bf16[16,480,128]{2,1,0:T(8,128)(2,1)}, bf16[16,480,128]{2,1,0:T(8,128)(2,1)S(1)}, u32[]{:S(2)}) %copy-start.1) | copy-done | bytes 1966104
  34.0 2.4 %shard_map.89 = (f32[128,128]{1,0:T(8,128)S(1)}, f32[128,128]{1,0:T(8,128)S(1)}, f32[128,128]{1,0:T(8,128)S(1)}) custom-call(bf16[512,384]{1,0:T(8,128)(2,1)S(1)} %get-tuple-element.28.cots, bf16[27,128,384]{2,1,0:T(8,128)(2,1)S(1)} %copy-done), custom_call_target="tpu_custom_call" | custom-call | bytes 4194304 | tf_op jit(solution)/shard_map/pallas_call | solution.py:370
  36.4 7.0 %all-to-all-start.1 = ((bf16[16,480,128]{2,1,0:T(8,128)(2,1)}), bf16[16,480,128]{2,1,0:T(8,128)(2,1)S(1)}, u32[]{:S(2)}, u32[]{:S(2)}) async-start(bf16[16,480,128]{2,1,0:T(8,128)(2,1)} %copy-done.1), calls=%async_computation.1 | async-start | bytes 3932160 | tf_op jit(solution)/shard_map/all_to_all | solution.py:322
  43.5 0.1 collective-permute-start.4
  43.6 4.7 %collective-permute-start.5 = (f32[128,128]{1,0:T(8,128)S(1)}, f32[128,128]{1,0:T(8,128)S(1)}, u32[]{:S(2)}, u32[]{:S(2)}) collective-permute-start(f32[128,128]{1,0:T(8,128)S(1)} %get-tuple-element.33), channel_id=1, source_target_pairs={{1,2},{3,4},{5,6},{7,8},{9,10},{11,12},{13,14},{2,1},{4,3},{6,5},{... | collective-permute-start | bytes 196616 | tf_op jit(solution)/shard_map/ppermute | solution.py:335
  48.3 1.9 %collective-permute-done.5.cross_ref = f32[128,128]{1,0:T(8,128)S(1)} collective-permute-done((f32[128,128]{1,0:T(8,128)S(1)}, f32[128,128]{1,0:T(8,128)S(1)}, u32[]{:S(2)}, u32[]{:S(2)}) %collective-permute-start.5) | collective-permute-done | bytes 65568 | tf_op jit(solution)/shard_map/ppermute | solution.py:335
  50.3 16.2 %all-gather = bf16[2048,128]{1,0:T(8,128)(2,1)S(1)} all-gather(bf16[128,128]{1,0:T(8,128)(2,1)S(1)} %shard_map.90), channel_id=2, replica_groups=mesh['dp'=16,'seq'=16] {'seq'}, dimensions={0}, use_global_device_ids=true | all-gather | bytes 557056 | tf_op jit(solution)/shard_map/all_gather | solution.py:382
  66.4 1.3 %shard_map.91 = (f32[8,8,896]{2,1,0:T(8,128)S(1)}, f32[8,8,896]{2,1,0:T(8,128)S(1)}) custom-call(bf16[16,128,128]{2,1,0:T(8,128)(2,1)S(1)} %all-to-all-done.packed_ref, bf16[16,128,128]{2,1,0:T(8,128)(2,1)S(1)} %bitcast.6), custom_call_target="tpu_custom_call" | custom-call | tf_op jit(solution)/shard_map/pallas_call | solution.py:385
  67.7 5.0 %all-to-all-done.1.blocks_ref = bf16[16,480,128]{2,1,0:T(8,128)(2,1)S(1)} async-done(((bf16[16,480,128]{2,1,0:T(8,128)(2,1)}), bf16[16,480,128]{2,1,0:T(8,128)(2,1)S(1)}, u32[]{:S(2)}, u32[]{:S(2)}) %all-to-all-start.1) | async-done | bytes 1966112 | tf_op jit(solution)/shard_map/all_to_all | solution.py:322
  72.7 1.9 %shard_map.95 = bf16[16,48,128]{2,1,0:T(8,128)(2,1)} custom-call(bf16[16,480,128]{2,1,0:T(8,128)(2,1)S(1)} %all-to-all-done.1.blocks_ref, f32[8,8,896]{2,1,0:T(8,128)S(1)} %get-tuple-element.35.kept_ref.before_ref), custom_call_target="tpu_custom_call" | custom-call | bytes 4194304 | tf_op jit(solution)/shard_map/pallas_call | solution.py:399
  74.6 6.2 %all-to-all-start.2 = ((bf16[16,48,128]{2,1,0:T(8,128)(2,1)}), bf16[16,48,128]{2,1,0:T(8,128)(2,1)S(1)}, u32[]{:S(2)}, u32[]{:S(2)}) async-start(bf16[16,48,128]{2,1,0:T(8,128)(2,1)} %shard_map.95), calls=%async_computation.2 | async-start | bytes 393216 | tf_op jit(solution)/shard_map/all_to_all | solution.py:322
  80.9 2.0 %collective-permute-start.6 = (f32[8,8,896]{2,1,0:T(8,128)S(1)}, f32[8,8,896]{2,1,0:T(8,128)S(1)}, u32[]{:S(2)}, u32[]{:S(2)}) collective-permute-start(f32[8,8,896]{2,1,0:T(8,128)S(1)} %get-tuple-element.36), channel_id=1, source_target_pairs={{0,32},{16,48},{32,0},{48,16},{64,96},{80,112},{96,64},{112,80},{1... | collective-permute-start | bytes 688136 | tf_op jit(solution)/shard_map/ppermute | solution.py:326
  82.8 7.2 %collective-permute-done.6.came_ref = f32[8,8,896]{2,1,0:T(8,128)S(1)} collective-permute-done((f32[8,8,896]{2,1,0:T(8,128)S(1)}, f32[8,8,896]{2,1,0:T(8,128)S(1)}, u32[]{:S(2)}, u32[]{:S(2)}) %collective-permute-start.6) | collective-permute-done | bytes 229408 | tf_op jit(solution)/shard_map/ppermute | solution.py:326
  90.1 0.7 collective-permute-start.7
  90.8 3.6 %collective-permute-done.7.came_ref = bf16[4,8,896]{2,1,0:T(8,128)(2,1)S(1)} collective-permute-done((bf16[4,8,896]{2,1,0:T(8,128)(2,1)S(1)}, bf16[4,8,896]{2,1,0:T(8,128)(2,1)S(1)}, u32[]{:S(2)}, u32[]{:S(2)}) %collective-permute-start.7) | collective-permute-done | bytes 57376 | tf_op jit(solution)/shard_map/ppermute | solution.py:326
  94.4 1.4 %collective-permute-start.8 = (bf16[2,8,896]{2,1,0:T(8,128)(2,1)S(1)}, bf16[2,8,896]{2,1,0:T(8,128)(2,1)S(1)}, u32[]{:S(2)}, u32[]{:S(2)}) collective-permute-start(bf16[2,8,896]{2,1,0:T(8,128)(2,1)S(1)} %get-tuple-element.40), channel_id=1, source_target_pairs={{0,128},{16,144},{32,160},{48,176},{64,192},{80,208},{96,224},{112... | collective-permute-start | bytes 86024 | tf_op jit(solution)/shard_map/ppermute | solution.py:326
  95.7 4.1 %collective-permute-done.8.came_ref = bf16[2,8,896]{2,1,0:T(8,128)(2,1)S(1)} collective-permute-done((bf16[2,8,896]{2,1,0:T(8,128)(2,1)S(1)}, bf16[2,8,896]{2,1,0:T(8,128)(2,1)S(1)}, u32[]{:S(2)}, u32[]{:S(2)}) %collective-permute-start.8) | collective-permute-done | bytes 28704 | tf_op jit(solution)/shard_map/ppermute | solution.py:326
  99.8 0.2 collective-permute-start.9
  100.0 0.1 shard_map.96
  100.1 0.1 copy.9
  100.2 3.5 %collective-permute-done.9.came_ref = f32[1,8,896]{2,1,0:T(8,128)S(1)} collective-permute-done((f32[1,8,896]{2,1,0:T(8,128)S(1)}, f32[1,8,896]{2,1,0:T(8,128)S(1)}, u32[]{:S(2)}, u32[]{:S(2)}) %collective-permute-start.9) | collective-permute-done | bytes 28704 | tf_op jit(solution)/shard_map/ppermute | solution.py:326
  103.8 0.7 shard_map.97
  (23 shorter events, 0.2 us)
Async XLA Ops:
  0.6 15.1 %copy-start.5 = (f32[128]{0:T(128)S(1)}, f32[128]{0:T(128)}, u32[]{:S(2)}) copy-start(f32[128]{0:T(128)} %param.9) | copy-start | bytes 1540
  4.3 11.4 %collective-permute-start = (f32[128,128]{1,0:T(8,128)}, f32[128,128]{1,0:T(8,128)S(1)}, u32[]{:S(2)}, u32[]{:S(2)}) collective-permute-start(f32[128,128]{1,0:T(8,128)} %get-tuple-element.24), channel_id=1, source_target_pairs={{0,1},{1,0},{2,3},{3,2},{4,5},{5,4},{6,7},{7,6},{8,9},{9,8},{10,11... | collective-permute-start | bytes 196616 | tf_op jit(solution)/shard_map/ppermute | solution.py:326
  4.4 11.3 %collective-permute-start.1 = (f32[128,128]{1,0:T(8,128)}, f32[128,128]{1,0:T(8,128)S(1)}, u32[]{:S(2)}, u32[]{:S(2)}) collective-permute-start(f32[128,128]{1,0:T(8,128)} %get-tuple-element.26), channel_id=1, source_target_pairs={{1,2},{3,4},{5,6},{7,8},{9,10},{11,12},{13,14},{2,1},{4,3},{6,5},{... | collective-permute-start | bytes 196616 | tf_op jit(solution)/shard_map/ppermute | solution.py:335
  8.3 21.8 %all-to-all-start = ((bf16[16,128,128]{2,1,0:T(8,128)(2,1)}), bf16[16,128,128]{2,1,0:T(8,128)(2,1)S(1)}, u32[]{:S(2)}, u32[]{:S(2)}) async-start(bf16[16,128,128]{2,1,0:T(8,128)(2,1)} %get-tuple-element.23), calls=%async_computation | async-start | bytes 1048576 | tf_op jit(solution)/shard_map/all_to_all | solution.py:322
  15.7 0.8 copy-start.4
  16.5 2.4 %copy-start.6 = (f32[384]{0:T(512)S(1)}, f32[384]{0:T(512)}, u32[]{:S(2)}) copy-start(f32[384]{0:T(512)} %param.11) | copy-start | bytes 4612
  16.5 13.5 %copy-start = (bf16[27,128,384]{2,1,0:T(8,128)(2,1)S(1)}, bf16[27,128,384]{2,1,0:T(8,128)(2,1)}, u32[]{:S(2)}) copy-start(bf16[27,128,384]{2,1,0:T(8,128)(2,1)} %weight_ref.3) | copy-start | bytes 7962628
  16.5 13.5 %copy-start.3 = (s32[1,115]{1,0:T(1,128)S(1)}, s32[1,115]{1,0:T(1,128)}, u32[]{:S(2)}) copy-start(s32[1,115]{1,0:T(1,128)} %index_ref.1) | copy-start | bytes 1384
  16.6 2.4 %collective-permute-start.2 = (bf16[128,128]{1,0:T(8,128)(2,1)S(1)}, bf16[128,128]{1,0:T(8,128)(2,1)S(1)}, u32[]{:S(2)}, u32[]{:S(2)}) collective-permute-start(bf16[128,128]{1,0:T(8,128)(2,1)S(1)} %get-tuple-element.27.here_ref), channel_id=1, source_target_pairs={{0,1},{1,0},{2,3},{3,2},{4,5},{5,4},{6,7},{7,6},{8,9},{9,8},{10,11... | collective-permute-start | bytes 98312 | tf_op jit(solution)/shard_map/ppermute | solution.py:326
  16.8 11.3 %collective-permute-start.3 = (bf16[128,128]{1,0:T(8,128)(2,1)S(1)}, bf16[128,128]{1,0:T(8,128)(2,1)S(1)}, u32[]{:S(2)}, u32[]{:S(2)}) collective-permute-start(bf16[128,128]{1,0:T(8,128)(2,1)S(1)} %get-tuple-element.27.here_ref), channel_id=1, source_target_pairs={{1,2},{3,4},{5,6},{7,8},{9,10},{11,12},{13,14},{2,1},{4,3},{6,5},{... | collective-permute-start | bytes 98312 | tf_op jit(solution)/shard_map/ppermute | solution.py:335
  32.7 1.3 %copy-start.1 = (bf16[16,480,128]{2,1,0:T(8,128)(2,1)}, bf16[16,480,128]{2,1,0:T(8,128)(2,1)S(1)}, u32[]{:S(2)}) copy-start(bf16[16,480,128]{2,1,0:T(8,128)(2,1)S(1)} %get-tuple-element.43) | copy-start | bytes 5898244
  36.4 36.3 %all-to-all-start.1 = ((bf16[16,480,128]{2,1,0:T(8,128)(2,1)}), bf16[16,480,128]{2,1,0:T(8,128)(2,1)S(1)}, u32[]{:S(2)}, u32[]{:S(2)}) async-start(bf16[16,480,128]{2,1,0:T(8,128)(2,1)} %copy-done.1), calls=%async_computation.1 | async-start | bytes 3932160 | tf_op jit(solution)/shard_map/all_to_all | solution.py:322
  43.5 4.8 %collective-permute-start.4 = (f32[128,128]{1,0:T(8,128)S(1)}, f32[128,128]{1,0:T(8,128)S(1)}, u32[]{:S(2)}, u32[]{:S(2)}) collective-permute-start(f32[128,128]{1,0:T(8,128)S(1)} %get-tuple-element.29), channel_id=1, source_target_pairs={{0,1},{1,0},{2,3},{3,2},{4,5},{5,4},{6,7},{7,6},{8,9},{9,8},{10,11... | collective-permute-start | bytes 196616 | tf_op jit(solution)/shard_map/ppermute | solution.py:326
  43.6 6.7 %collective-permute-start.5 = (f32[128,128]{1,0:T(8,128)S(1)}, f32[128,128]{1,0:T(8,128)S(1)}, u32[]{:S(2)}, u32[]{:S(2)}) collective-permute-start(f32[128,128]{1,0:T(8,128)S(1)} %get-tuple-element.33), channel_id=1, source_target_pairs={{1,2},{3,4},{5,6},{7,8},{9,10},{11,12},{13,14},{2,1},{4,3},{6,5},{... | collective-permute-start | bytes 196616 | tf_op jit(solution)/shard_map/ppermute | solution.py:335
  74.6 25.4 %all-to-all-start.2 = ((bf16[16,48,128]{2,1,0:T(8,128)(2,1)}), bf16[16,48,128]{2,1,0:T(8,128)(2,1)S(1)}, u32[]{:S(2)}, u32[]{:S(2)}) async-start(bf16[16,48,128]{2,1,0:T(8,128)(2,1)} %shard_map.95), calls=%async_computation.2 | async-start | bytes 393216 | tf_op jit(solution)/shard_map/all_to_all | solution.py:322
  80.9 9.2 %collective-permute-start.6 = (f32[8,8,896]{2,1,0:T(8,128)S(1)}, f32[8,8,896]{2,1,0:T(8,128)S(1)}, u32[]{:S(2)}, u32[]{:S(2)}) collective-permute-start(f32[8,8,896]{2,1,0:T(8,128)S(1)} %get-tuple-element.36), channel_id=1, source_target_pairs={{0,32},{16,48},{32,0},{48,16},{64,96},{80,112},{96,64},{112,80},{1... | collective-permute-start | bytes 688136 | tf_op jit(solution)/shard_map/ppermute | solution.py:326
  90.1 4.3 %collective-permute-start.7 = (bf16[4,8,896]{2,1,0:T(8,128)(2,1)S(1)}, bf16[4,8,896]{2,1,0:T(8,128)(2,1)S(1)}, u32[]{:S(2)}, u32[]{:S(2)}) collective-permute-start(bf16[4,8,896]{2,1,0:T(8,128)(2,1)S(1)} %get-tuple-element.38), channel_id=1, source_target_pairs={{0,16},{16,0},{32,48},{48,32},{64,80},{80,64},{96,112},{112,96},{1... | collective-permute-start | bytes 172040 | tf_op jit(solution)/shard_map/ppermute | solution.py:326
  94.4 5.5 %collective-permute-start.8 = (bf16[2,8,896]{2,1,0:T(8,128)(2,1)S(1)}, bf16[2,8,896]{2,1,0:T(8,128)(2,1)S(1)}, u32[]{:S(2)}, u32[]{:S(2)}) collective-permute-start(bf16[2,8,896]{2,1,0:T(8,128)(2,1)S(1)} %get-tuple-element.40), channel_id=1, source_target_pairs={{0,128},{16,144},{32,160},{48,176},{64,192},{80,208},{96,224},{112... | collective-permute-start | bytes 86024 | tf_op jit(solution)/shard_map/ppermute | solution.py:326
  99.8 4.0 %collective-permute-start.9 = (f32[1,8,896]{2,1,0:T(8,128)S(1)}, f32[1,8,896]{2,1,0:T(8,128)S(1)}, u32[]{:S(2)}, u32[]{:S(2)}) collective-permute-start(f32[1,8,896]{2,1,0:T(8,128)S(1)} %get-tuple-element.42), channel_id=1, source_target_pairs={{0,64},{16,80},{32,96},{48,112},{64,0},{80,16},{96,32},{112,48},{1... | collective-permute-start | bytes 86024 | tf_op jit(solution)/shard_map/ppermute | solution.py:326
  100.2 4.3 %copy-start.2 = (f32[27,8,24]{0,2,1:T(8,128)}, f32[27,8,24]{0,2,1:T(8,128)S(1)}, u32[]{:S(2)}) copy-start(f32[27,8,24]{0,2,1:T(8,128)S(1)} %copy.9) | copy-start | bytes 62212
